TPU v7x, 32 devices: a whole 2x2x4 slice. The times are simulated.
32 devices in a mesh: dp: 16 (over z, y, core), tensor: 2 (over x).
Axes of the slice: x: 2, y: 2, z: 4, core: 2. Of those that a mesh axis runs over, the one named last changes fastest.
Arguments:
- tokens: bfloat16 [32768, 768], P(('dp', 'tensor')), may hold values from -6 to 6
- out_grad: bfloat16 [32768, 768], P(('dp', 'tensor')), may hold values from -6 to 6
- seq_lengths: int32 [48], replicated, may hold values from 1 to 1024, 32768 in all
- deal_order: int32 [48], replicated, may hold values from 0 to 47, each once
- input_weight: float32 [2, 3, 768, 768], P(None, None, 'dp', 'tensor'), may hold values from -0.21875 to 0.21875
- output_weight: float32 [2, 768, 768], P(None, 'tensor', 'dp'), may hold values from -0.21875 to 0.21875
- up_projection_weight: float32 [2, 768, 3072], P(None, 'dp', 'tensor'), may hold values from -0.21875 to 0.21875
- down_projection_weight: float32 [2, 3072, 768], P(None, 'tensor', 'dp'), may hold values from -0.109375 to 0.109375
- input_bias: float32 [2, 3, 768], replicated, may hold values from -2 to 2
- short_taps: float32 [2, 3, 3, 768], replicated, may hold values from -3 to 3
- filter_first: float32 [2, 33, 64], replicated, may hold values from -1 to 1
- filter_inner: float32 [2, 2, 64, 64], replicated, may hold values from -0.75 to 0.75
- filter_biases: float32 [2, 3, 64], replicated, may hold values from -3 to 3
- filter_rates: float32 [2, 3, 64], replicated, may hold values from 0.1 to 1.9
- filter_out: float32 [2, 64, 768], replicated, may hold values from -0.09375 to 0.09375
- conv_bias: float32 [2, 768], replicated, may hold values from -4 to 4
- norm_gains: float32 [2, 2, 768], replicated, may hold values from 0.5 to 1.5
- norm_biases: float32 [2, 2, 768], replicated, may hold values from -2 to 2
- output_biases: float32 [2, 2, 768], replicated, may hold values from -2 to 2
- up_projection_bias: float32 [2, 3072], replicated, may hold values from -2 to 2
Outputs:
- out_first: bfloat16 [32768, 768], P(('dp', 'tensor'))
- out_second: bfloat16 [32768, 768], P(('dp', 'tensor'))
- in_grad: bfloat16 [32768, 768], P(('dp', 'tensor'))
- in_weight_grad: float32 [2, 3, 768, 768], P(None, None, 'dp', 'tensor')
- out_weight_grad: float32 [2, 768, 768], P(None, 'tensor', 'dp')
- up_weight_grad: float32 [2, 768, 3072], P(None, 'dp', 'tensor')
- down_weight_grad: float32 [2, 3072, 768], P(None, 'tensor', 'dp')
- in_bias_grad: float32 [2, 3, 768], replicated
- short_taps_grad: float32 [2, 3, 3, 768], replicated
- filter_first_grad: float32 [2, 33, 64], replicated
- filter_inner_grad: float32 [2, 2, 64, 64], replicated
- filter_biases_grad: float32 [2, 3, 64], replicated
- filter_rates_grad: float32 [2, 3, 64], replicated
- filter_out_grad: float32 [2, 64, 768], replicated
- conv_bias_grad: float32 [2, 768], replicated
- norm_gains_grad: float32 [2, 2, 768], replicated
- norm_biases_grad: float32 [2, 2, 768], replicated
- out_biases_grad: float32 [2, 2, 768], replicated
- up_bias_grad: float32 [2, 3072], replicated
Inputs may be any that keep to these rules, and one draw needn't show every extreme that they name: `seq_lengths`: lengths of the sequences in slot order; slot k belongs to index k // 3 of dp; they sum to 32768 and the largest is 1024. Slot k holds the sequence of input rank deal_order[k]; every rank once.
All inputs are finite; a program needn't handle non-finite values.
Results may differ from a plain program's by a relative error of at most 0.024.
Values may be sent and summed in bfloat16 or wider, within the bound.
No kernel may reach another device: no remote copies, remote signals or barrier semaphores. Data moves between devices by JAX's collectives and lax.ppermute only.
A program may use at most 576 MiB of HBM per device.

v0:
```python
import math

import jax
import jax.numpy as jnp
from jax import lax
from jax.sharding import PartitionSpec as P

D = 768
FF = 3072
EMB = 33
LAYERS = 2
LMAX = 1024


highest_accuracy = lax.Precision.HIGHEST
epsilon = 1e-05
shift_value = 0.05


def layer_norm(values, gain, bias):
    middle_state = jnp.mean(values, -1, keepdims=True)
    centered = values - middle_state
    spread = jnp.mean(centered * centered, -1, keepdims=True)
    return centered * lax.rsqrt(spread + epsilon) * gain + bias


def positions_table(length):
    bands = (EMB - 1) // 2
    ramp = jnp.linspace(0.0, 1.0, length, dtype=jnp.float32)[:, None]
    places = jnp.arange(length, dtype=jnp.float32)[:, None] * (2.0 * math.pi / length)
    levels = jnp.linspace(0.0001, bands - 1, bands, dtype=jnp.float32)[None, :]
    return jnp.concatenate([ramp, jnp.cos(levels * places), -jnp.sin(levels * places)], axis=1)


def decay_table(length, channel_ids):
    ramp = jnp.linspace(0.0, 1.0, length, dtype=jnp.float32)[:, None]
    fastest = math.log(0.01) / 0.3
    slowest = math.log(0.01) / 1.5
    speeds = slowest + (fastest - slowest) * channel_ids.astype(jnp.float32) / (D - 1)
    return jnp.exp(-ramp * jnp.abs(speeds)[None, :]) + shift_value


def filter_hidden(positions, first_w, inner_w, bias_w, rate_w):
    inner = jnp.sin(
        rate_w[0] * (jnp.dot(positions, first_w, precision=highest_accuracy) + bias_w[0])
    )
    inner = jnp.sin(
        rate_w[1] * (jnp.dot(inner, inner_w[0], precision=highest_accuracy) + bias_w[1])
    )
    return jnp.sin(rate_w[2] * (jnp.dot(inner, inner_w[1], precision=highest_accuracy) + bias_w[2]))


def short_conv(signal, taps):
    once = jnp.pad(signal, ((0, 0), (1, 0), (0, 0)))[:, :-1]
    twice = jnp.pad(signal, ((0, 0), (2, 0), (0, 0)))[:, :-2]
    return taps[0] * signal + taps[1] * once + taps[2] * twice


def exact_gelu(values):
    return jax.nn.gelu(values, approximate=False)


def slot_starts(seq_lengths, deal_order):
    count = seq_lengths.shape[0]
    match = deal_order[:, None] == jnp.arange(count, dtype=jnp.int32)[None, :]
    by_input = jnp.sum(jnp.where(match, seq_lengths[:, None], 0), axis=0)
    starts = jnp.cumsum(by_input) - by_input
    return jnp.sum(jnp.where(match, starts[None, :], 0), axis=1)


def fourier_tables(length):
    size = 2 * length
    count = (length + 128) // 128 * 128
    places = lax.broadcasted_iota(jnp.int32, (length, count), 0)
    waves = lax.broadcasted_iota(jnp.int32, (length, count), 1)
    angle = (places * waves % size).astype(jnp.float32) * (2.0 * math.pi / size)
    used = (waves <= length).astype(jnp.float32)
    factor = jnp.where((waves == 0) | (waves == length), 1.0, 2.0) * used / size
    cosine = jnp.cos(angle) * used
    sine = jnp.sin(angle) * used
    return (cosine, sine, jnp.cos(angle) * factor, jnp.sin(angle) * factor)


def forward_spectrum(signal, cosine, sine):
    real = jnp.einsum("slc,lk->sck", signal, cosine, precision=highest_accuracy)
    imaginary = jnp.einsum("slc,lk->sck", signal, sine, precision=highest_accuracy)
    return (real, imaginary)


def inverse_spectrum(real, imaginary, back_cosine, back_sine):
    return jnp.einsum("sck,lk->slc", real, back_cosine, precision=highest_accuracy) + jnp.einsum(
        "sck,lk->slc", imaginary, back_sine, precision=highest_accuracy
    )


def widen(local, full_size, offset, axis):
    shape = list(local.shape)
    shape[axis] = full_size
    return lax.dynamic_update_slice_in_dim(jnp.zeros(shape, jnp.float32), local, offset, axis)


def spread(values):
    return lax.all_gather(values, "tensor", axis=0, tiled=True)


def collect(left, right):
    return lax.psum_scatter(
        jnp.dot(left, right, preferred_element_type=jnp.float32).astype(jnp.bfloat16),
        "tensor",
        scatter_dimension=0,
        tiled=True,
    ).astype(jnp.float32)


def share_grads(stacked):
    return (
        lax.psum_scatter(
            stacked[0].astype(jnp.bfloat16), "dp", scatter_dimension=2, tiled=True
        ).astype(jnp.float32),
        lax.psum_scatter(
            stacked[1].astype(jnp.bfloat16), "dp", scatter_dimension=2, tiled=True
        ).astype(jnp.float32),
        lax.psum_scatter(
            stacked[2].astype(jnp.bfloat16), "dp", scatter_dimension=1, tiled=True
        ).astype(jnp.float32),
        lax.psum_scatter(
            stacked[3].astype(jnp.bfloat16), "dp", scatter_dimension=2, tiled=True
        ).astype(jnp.float32),
    )


def shards(
    tokens,
    out_grad,
    seq_lengths,
    deal_order,
    input_weight,
    output_weight,
    up_projection_weight,
    down_projection_weight,
    input_bias,
    short_taps,
    filter_first,
    filter_inner,
    filter_biases,
    filter_rates,
    filter_out,
    conv_bias,
    norm_gains,
    norm_biases,
    output_biases,
    up_projection_bias,
):
    tensor_count = lax.axis_size("tensor")
    tensor_rank = lax.axis_index("tensor")
    group_rank = lax.axis_index("dp")
    token_local = tokens.shape[0] * tensor_count
    width = tokens.shape[1] // tensor_count
    slot_total = seq_lengths.shape[0]
    slot_local = slot_total // lax.axis_size("dp")
    group_rows = slot_local * LMAX
    hidden_local = up_projection_weight.shape[2]
    channel_start = tensor_rank * width
    hidden_start = tensor_rank * hidden_local
    token_cols, grad_cols = (
        lax.all_to_all(tokens, "tensor", split_axis=1, concat_axis=0, tiled=True),
        lax.all_to_all(out_grad, "tensor", split_axis=1, concat_axis=0, tiled=True),
    )
    starts = slot_starts(seq_lengths, deal_order)
    mine_starts = lax.dynamic_slice_in_dim(starts, group_rank * slot_local, slot_local)
    mine_lengths = lax.dynamic_slice_in_dim(seq_lengths, group_rank * slot_local, slot_local)
    offsets = jnp.arange(LMAX, dtype=jnp.int32)
    live = (offsets[None, :] < mine_lengths[:, None]).reshape(-1)
    source = (mine_starts[:, None] + offsets[None, :]).reshape(-1)
    blank = jnp.zeros((group_rows, width), jnp.bfloat16)
    held = (blank, blank)
    pieces = (
        lax.all_gather(token_cols, "dp", axis=0, tiled=True),
        lax.all_gather(grad_cols, "dp", axis=0, tiled=True),
    )
    count = pieces[0].shape[0]
    offset = source
    inside = live & (offset >= 0) & (offset < count)
    picked = jnp.clip(offset, 0, count - 1)
    slot_tokens = jnp.where(inside[:, None], jnp.take(pieces[0], picked, axis=0), held[0])
    slot_grads = jnp.where(inside[:, None], jnp.take(pieces[1], picked, axis=0), held[1])
    row_tokens, row_grads = (
        lax.all_to_all(slot_tokens, "tensor", split_axis=0, concat_axis=1, tiled=True),
        lax.all_to_all(slot_grads, "tensor", split_axis=0, concat_axis=1, tiled=True),
    )
    cosine, sine, back_cosine, back_sine = fourier_tables(LMAX)
    positions = positions_table(LMAX)
    modulation = decay_table(LMAX, channel_start + jnp.arange(width, dtype=jnp.int32))
    hidden_state = row_tokens.astype(jnp.float32)
    kept = []
    layer_outputs = []
    for residual_layer in range(LAYERS):
        in_part, out_part, up_part, down_part = (
            lax.all_gather(
                input_weight[residual_layer].astype(jnp.bfloat16), "dp", axis=1, tiled=True
            ),
            lax.all_gather(
                output_weight[residual_layer].astype(jnp.bfloat16), "dp", axis=1, tiled=True
            ),
            lax.all_gather(
                up_projection_weight[residual_layer].astype(jnp.bfloat16), "dp", axis=0, tiled=True
            ),
            lax.all_gather(
                down_projection_weight[residual_layer].astype(jnp.bfloat16),
                "dp",
                axis=1,
                tiled=True,
            ),
        )
        in_joined = jnp.transpose(in_part, (1, 0, 2)).reshape(D, 3 * width)
        in_all, out_all, up_all, down_all = (in_joined, out_part, up_part, down_part)
        bias_local = lax.dynamic_slice_in_dim(
            input_bias[residual_layer], channel_start, width, 1
        ).reshape(3 * width)
        taps_local = lax.dynamic_slice_in_dim(
            short_taps[residual_layer], channel_start, width, 2
        ).reshape(3, 3 * width)
        conv_local = lax.dynamic_slice_in_dim(conv_bias[residual_layer], channel_start, width, 0)
        out_filter = lax.dynamic_slice_in_dim(filter_out[residual_layer], channel_start, width, 1)
        first_normed, first_back = jax.vjp(
            layer_norm, hidden_state, norm_gains[residual_layer, 0], norm_biases[residual_layer, 0]
        )
        first_all = spread(first_normed.astype(jnp.bfloat16))
        projected_rows = (
            jnp.dot(first_all, in_joined, preferred_element_type=jnp.float32) + bias_local
        ).reshape(slot_local, LMAX, 3 * width)
        mixed, conv_back = jax.vjp(short_conv, projected_rows, taps_local)
        gate_out = mixed[:, :, :width]
        gate_in = mixed[:, :, width : 2 * width]
        values = mixed[:, :, 2 * width :]
        signal = gate_in * values
        inner, filter_back = jax.vjp(
            lambda first_w, inner_w, bias_w, rate_w: filter_hidden(
                positions, first_w, inner_w, bias_w, rate_w
            ),
            filter_first[residual_layer],
            filter_inner[residual_layer],
            filter_biases[residual_layer],
            filter_rates[residual_layer],
        )
        kernel = jnp.dot(inner, out_filter, precision=highest_accuracy) * modulation
        signal_real, signal_imaginary = forward_spectrum(signal, cosine, sine)
        kernel_real, kernel_imaginary = forward_spectrum(kernel[None], cosine, sine)
        conv_full = inverse_spectrum(
            signal_real * kernel_real - signal_imaginary * kernel_imaginary,
            signal_real * kernel_imaginary + signal_imaginary * kernel_real,
            back_cosine,
            back_sine,
        )
        carried = conv_full + conv_local * signal
        mixer_block = (gate_out * carried).astype(jnp.bfloat16).reshape(group_rows, width)
        out_branch = collect(mixer_block, out_part)
        middle_state = hidden_state + out_branch + output_biases[residual_layer, 0]
        second_normed, second_back = jax.vjp(
            layer_norm, middle_state, norm_gains[residual_layer, 1], norm_biases[residual_layer, 1]
        )
        second_low = second_normed.astype(jnp.bfloat16)
        up_input = spread(second_low)
        prior_input = jnp.dot(
            up_input, up_all, preferred_element_type=jnp.float32
        ) + lax.dynamic_slice_in_dim(
            up_projection_bias[residual_layer], hidden_start, hidden_local, 0
        )
        gelu_applied, gelu_back = jax.vjp(exact_gelu, prior_input)
        gelu_applied = gelu_applied.astype(jnp.bfloat16)
        branch = collect(gelu_applied, down_all)
        hidden_state = middle_state + branch + output_biases[residual_layer, 1]
        layer_outputs.append(hidden_state.astype(jnp.bfloat16))
        kept.append(
            {
                "first_back": first_back,
                "first_all": first_all,
                "in_joined": in_joined,
                "in_all": in_all,
                "conv_back": conv_back,
                "gate_out": gate_out,
                "gate_in": gate_in,
                "values": values,
                "signal": signal,
                "filter_back": filter_back,
                "inner": inner,
                "out_filter": out_filter,
                "conv_local": conv_local,
                "signal_real": signal_real,
                "signal_imaginary": signal_imaginary,
                "kernel_real": kernel_real,
                "kernel_imaginary": kernel_imaginary,
                "carried": carried,
                "mixer": mixer_block,
                "out_part": out_part,
                "second_back": second_back,
                "up_input": up_input,
                "up_all": up_all,
                "down_all": down_all,
                "activated": gelu_applied,
                "gelu_back": gelu_back,
            }
        )
    grad_state = row_grads.astype(jnp.float32)
    shared = [None] * LAYERS
    small = [None] * LAYERS
    for residual_layer in reversed(range(LAYERS)):
        kept_now = kept[residual_layer]
        down_bias_grad = jnp.sum(grad_state, axis=0)
        grad_low = grad_state.astype(jnp.bfloat16)
        grad_rows = spread(grad_low)
        down_grad = jnp.einsum(
            "rf,rd->fd", kept_now["activated"], grad_rows, preferred_element_type=jnp.float32
        )
        activated_grad = jnp.einsum(
            "rd,fd->rf", grad_rows, kept_now["down_all"], preferred_element_type=jnp.float32
        )
        before_grad = kept_now["gelu_back"](activated_grad)[0]
        up_bias_grad = jnp.sum(before_grad, axis=0)
        before_low = before_grad.astype(jnp.bfloat16)
        up_grad = jnp.einsum(
            "rd,rf->df", kept_now["up_input"], before_low, preferred_element_type=jnp.float32
        )
        second_grad = collect(before_low, jnp.transpose(kept_now["up_all"]))
        up_bias_grad = widen(up_bias_grad, FF, hidden_start, 0)
        middle_norm_grad, second_gain_grad, second_bias_grad = kept_now["second_back"](second_grad)
        middle_grad = grad_state + middle_norm_grad
        mixer_bias_grad = jnp.sum(middle_grad, axis=0)
        mixer_rows = spread(middle_grad.astype(jnp.bfloat16))
        out_weight_part = jnp.einsum(
            "rc,rd->cd", kept_now["mixer"], mixer_rows, preferred_element_type=jnp.float32
        )
        mixer_grad = jnp.einsum(
            "rd,cd->rc", mixer_rows, kept_now["out_part"], preferred_element_type=jnp.float32
        ).reshape(slot_local, LMAX, width)
        gate_out_grad = mixer_grad * kept_now["carried"]
        carried_grad = mixer_grad * kept_now["gate_out"]
        conv_bias_grad = jnp.sum(carried_grad * kept_now["signal"], axis=(0, 1))
        grad_real, grad_imaginary = forward_spectrum(carried_grad, cosine, sine)
        kernel_real = kept_now["kernel_real"]
        kernel_imaginary = kept_now["kernel_imaginary"]
        signal_real = kept_now["signal_real"]
        signal_imaginary = kept_now["signal_imaginary"]
        signal_grad = (
            inverse_spectrum(
                kernel_real * grad_real + kernel_imaginary * grad_imaginary,
                kernel_real * grad_imaginary - kernel_imaginary * grad_real,
                back_cosine,
                back_sine,
            )
            + kept_now["conv_local"] * carried_grad
        )
        kernel_grad = inverse_spectrum(
            jnp.sum(
                signal_real * grad_real + signal_imaginary * grad_imaginary, axis=0, keepdims=True
            ),
            jnp.sum(
                signal_real * grad_imaginary - signal_imaginary * grad_real, axis=0, keepdims=True
            ),
            back_cosine,
            back_sine,
        )[0]
        gate_in_grad = signal_grad * kept_now["values"]
        values_grad = signal_grad * kept_now["gate_in"]
        mixed_grad = jnp.concatenate([gate_out_grad, gate_in_grad, values_grad], axis=2)
        projected_grad, taps_grad = kept_now["conv_back"](mixed_grad)
        projected_grad = projected_grad.reshape(group_rows, 3 * width)
        in_bias_grad = jnp.sum(projected_grad, axis=0)
        projected_low = projected_grad.astype(jnp.bfloat16)
        in_joined_grad = jnp.einsum(
            "rd,rc->dc", kept_now["first_all"], projected_low, preferred_element_type=jnp.float32
        )
        in_weight_part = jnp.transpose(in_joined_grad.reshape(D, 3, width), (1, 0, 2))
        first_grad = collect(projected_low, jnp.transpose(kept_now["in_joined"]))
        state_norm_grad, first_gain_grad, first_bias_grad = kept_now["first_back"](first_grad)
        grad_state = middle_grad + state_norm_grad
        scaled = kernel_grad * modulation
        filter_out_grad = jnp.dot(
            jnp.transpose(kept_now["inner"]), scaled, precision=highest_accuracy
        )
        inner_grad = jnp.dot(
            scaled, jnp.transpose(kept_now["out_filter"]), precision=highest_accuracy
        )
        first_filter_grad, inner_filter_grad, bias_filter_grad, rate_filter_grad = kept_now[
            "filter_back"
        ](inner_grad)
        small[residual_layer] = (
            widen(in_bias_grad.reshape(3, width), D, channel_start, 1),
            widen(taps_grad.reshape(3, 3, width), D, channel_start, 2),
            first_filter_grad,
            inner_filter_grad,
            bias_filter_grad,
            rate_filter_grad,
            widen(filter_out_grad, D, channel_start, 1),
            widen(conv_bias_grad, D, channel_start, 0),
            jnp.stack([first_gain_grad, second_gain_grad]),
            jnp.stack([first_bias_grad, second_bias_grad]),
            jnp.stack([mixer_bias_grad, down_bias_grad]),
            up_bias_grad,
        )
        grads_now = (in_weight_part, out_weight_part, up_grad, down_grad)
        shared[residual_layer] = share_grads([part[None] for part in grads_now])
    shared_all = [
        jnp.concatenate([shared[residual_layer][index] for residual_layer in range(LAYERS)])
        for index in range(4)
    ]
    stacked = [
        jnp.stack([small[residual_layer][index] for residual_layer in range(LAYERS)])
        for index in range(12)
    ]
    summed = lax.psum(
        (
            stacked[0],
            stacked[1],
            stacked[2],
            stacked[3],
            stacked[4],
            stacked[5],
            stacked[6],
            stacked[7],
            stacked[8],
            stacked[9],
            stacked[10],
            stacked[11],
        ),
        ("dp", "tensor"),
    )
    columns_first, columns_second, columns_grad = (
        lax.all_to_all(layer_outputs[0], "tensor", split_axis=1, concat_axis=0, tiled=True),
        lax.all_to_all(layer_outputs[1], "tensor", split_axis=1, concat_axis=0, tiled=True),
        lax.all_to_all(
            grad_state.astype(jnp.bfloat16), "tensor", split_axis=1, concat_axis=0, tiled=True
        ),
    )
    token_ids = group_rank * token_local + jnp.arange(token_local, dtype=jnp.int32)
    inside_all = (token_ids[:, None] >= starts[None, :]) & (
        token_ids[:, None] < starts[None, :] + seq_lengths[None, :]
    )
    slot_base = jnp.arange(slot_total, dtype=jnp.int32)[None, :] * LMAX - starts[None, :]
    row_of = jnp.sum(jnp.where(inside_all, slot_base + token_ids[:, None], 0), axis=1)
    blank_out = jnp.zeros((token_local, width), jnp.bfloat16)
    held = (blank_out, blank_out, blank_out)
    pieces = (
        lax.all_gather(columns_first, "dp", axis=0, tiled=True),
        lax.all_gather(columns_second, "dp", axis=0, tiled=True),
        lax.all_gather(columns_grad, "dp", axis=0, tiled=True),
    )
    count = pieces[0].shape[0]
    offset = row_of
    inside = (offset >= 0) & (offset < count)
    picked = jnp.clip(offset, 0, count - 1)
    cols_first = jnp.where(inside[:, None], jnp.take(pieces[0], picked, axis=0), held[0])
    cols_second = jnp.where(inside[:, None], jnp.take(pieces[1], picked, axis=0), held[1])
    cols_grad = jnp.where(inside[:, None], jnp.take(pieces[2], picked, axis=0), held[2])
    out_first, out_second, in_grad = (
        lax.all_to_all(cols_first, "tensor", split_axis=0, concat_axis=1, tiled=True),
        lax.all_to_all(cols_second, "tensor", split_axis=0, concat_axis=1, tiled=True),
        lax.all_to_all(cols_grad, "tensor", split_axis=0, concat_axis=1, tiled=True),
    )
    return (
        out_first,
        out_second,
        in_grad,
        shared_all[0],
        shared_all[1],
        shared_all[2],
        shared_all[3],
        summed[0],
        summed[1],
        summed[2],
        summed[3],
        summed[4],
        summed[5],
        summed[6],
        summed[7],
        summed[8],
        summed[9],
        summed[10],
        summed[11],
    )


def solution(mesh):
    in_specs = (
        P(("dp", "tensor"), None),
        P(("dp", "tensor"), None),
        P(),
        P(),
        P(None, None, "dp", "tensor"),
        P(None, "tensor", "dp"),
        P(None, "dp", "tensor"),
        P(None, "tensor", "dp"),
        P(),
        P(),
        P(),
        P(),
        P(),
        P(),
        P(),
        P(),
        P(),
        P(),
        P(),
        P(),
    )
    out_specs = (
        P(("dp", "tensor"), None),
        P(("dp", "tensor"), None),
        P(("dp", "tensor"), None),
        P(None, None, "dp", "tensor"),
        P(None, "tensor", "dp"),
        P(None, "dp", "tensor"),
        P(None, "tensor", "dp"),
        P(),
        P(),
        P(),
        P(),
        P(),
        P(),
        P(),
        P(),
        P(),
        P(),
        P(),
        P(),
    )
    return jax.shard_map(shards, mesh=mesh, in_specs=in_specs, out_specs=out_specs, check_vma=False)
```

profile of v0, /device:TPU:0, one launch (start us, length us, event | category | flops | bytes accessed | tf_op | source)
XLA Modules:
  0.0 4004.6 jit_solution(17134728002932122693)
XLA Ops:
  8.9 24.1 all_to_all.184
  33.3 22.2 all_to_all.185
  57.7 104.6 %all-gather.28.cloned.1.call-done = bf16[32768,384]{1,0:T(8,128)(2,1)} async-done(((bf16[2048,384]{1,0:T(8,128)(2,1)}), bf16[32768,384]{1,0:T(8,128)(2,1)}) %all-gather.28.cloned.1.call-update) | async-done | bytes 25165840 | tf_op jit(solution)/shard_map/all_gather | solution.py:178
  184.3 108.2 %all-gather.42.cloned.1.call-done = bf16[32768,384]{1,0:T(8,128)(2,1)} async-done(((bf16[2048,384]{1,0:T(8,128)(2,1)}), bf16[32768,384]{1,0:T(8,128)(2,1)}) %all-gather.42.cloned.1.call-update) | async-done | bytes 25165840 | tf_op jit(solution)/shard_map/all_gather | solution.py:179
  292.5 24.1 gather_fusion.3
  329.9 24.7 all-to-all-done.1
  369.3 23.7 all-gather.1
  393.1 26.3 fusion.127
  419.4 26.4 fusion.135
  475.9 42.4 %fusion.85 = f32[3,384,1152]{2,1,0:T(8,128)} fusion(f32[1152]{0:T(1024)S(1)} %fusion.328, f32[3,1024,384]{2,1,0:T(8,128)S(1)} %fusion.556), kind=kOutput, calls=%fused_computation.174 | convolution fusion | flops 16325148672 | bytes 10031616 | tf_op jit(solution)/shard_map/slc,lk->sck/dot_general | solution.py:86
  518.2 41.7 %fusion.93 = f32[3,384,1152]{2,1,0:T(8,128)} fusion(f32[1152]{0:T(1024)S(1)} %fusion.328, f32[3,1024,384]{2,1,0:T(8,128)S(1)} %fusion.560), kind=kOutput, calls=%fused_computation.182 | convolution fusion | flops 16325148672 | bytes 10031616 | tf_op jit(solution)/shard_map/slc,lk->sck/dot_general | solution.py:85
  568.1 57.0 %fusion.50 = f32[1024,3,384]{2,0,1:T(8,128)S(1)} fusion(f32[3,384,1152]{2,1,0:T(8,128)} %fusion.85, f32[3,384,1152]{2,1,0:T(8,128)} %fusion.93, f32[384,1152]{1,0:T(8,128)} %fusion.127, f32[384,1152]{1,0:T(8,128)} %fusion.135, f32[1152]{0:T(1024)S(1)} %fusion.331), kind=kOutput, calls=%fused_computation.127 | convolution fusion | flops 16329129984 | bytes 18878976 | tf_op jit(solution)/shard_map/sck,lk->slc/dot_general | solution.py:91
  625.1 40.2 %multiply_convert_fusion.3 = (bf16[3,1024,384]{2,1,0:T(8,128)(2,1)S(1)}, f32[3,1024,384]{2,1,0:T(8,128)}) fusion(f32[3,1024,1152]{2,1,0:T(8,128)S(1)} %multiply_add_fusion.3, f32[384]{0:T(512)S(1)} %get-tuple-element.271, f32[1024,3,384]{2,0,1:T(8,128)S(1)} %fusion.50, f32[1152]{0:T(1024)S(1)} %fusion.331, f32[3,384,1152]{2,1,0:T(8,128)S(1)} %copy-done.33), kind=kOutput, calls=%fused_computation.212 | convolution fusion | flops 16332226560 | bytes 31266816 | tf_op jit(solution)/shard_map/sck,lk->slc/dot_general | solution.py:91
  673.5 53.8 %reduce-scatter.13.cloned.1.call-done = bf16[1536,768]{1,0:T(8,128)(2,1)} async-done(((bf16[3072,768]{1,0:T(8,128)(2,1)}), bf16[1536,768]{1,0:T(8,128)(2,1)}) %reduce-scatter.13.cloned.1.call-update) | async-done | bytes 2359312 | tf_op jit(solution)/shard_map/reduce_scatter | solution.py:107
  737.0 35.5 all-gather.56.cloned.1.call-done
  772.5 63.1 %all-gather.32.cloned.1.call-done = bf16[3072,768]{1,0:T(8,128)(2,1)} async-done(((bf16[1536,768]{1,0:T(8,128)(2,1)}), bf16[3072,768]{1,0:T(8,128)(2,1)}) %all-gather.32.cloned.1.call-update) | async-done | bytes 4718608 | tf_op jit(solution)/shard_map/all_gather | solution.py:103
  835.6 49.9 %multiply_convert_fusion.1 = (bf16[3072,1536]{1,0:T(8,128)(2,1)}, f32[3072,1536]{1,0:T(8,128)}, f32[3072,1536]{1,0:T(8,128)}) fusion(f32[1536]{0:T(1024)S(1)} %dynamic-slice_reduce_fusion.1, bf16[3072,768]{1,0:T(8,128)(2,1)} %all-gather.32.cloned.1.call-done, bf16[1,768,1536]{2,1,0:T(8,128)(2,1)} %all-gather.56.cloned.1.call-done), kind=kOutput, calls=%fused_computation.24 | convolution fusion | flops 7559184384 | bytes 54269952 | tf_op jit(solution)/shard_map/dot_general | solution.py:264
  898.6 59.3 %reduce-scatter.15.cloned.1.call-done = bf16[1536,768]{1,0:T(8,128)(2,1)} async-done(((bf16[3072,768]{1,0:T(8,128)(2,1)}), bf16[1536,768]{1,0:T(8,128)(2,1)}) %reduce-scatter.15.cloned.1.call-update) | async-done | bytes 2359312 | tf_op jit(solution)/shard_map/reduce_scatter | solution.py:107
  973.4 25.0 all-gather.5
  998.5 26.3 fusion.125
  1024.8 26.6 fusion.133
  1092.6 42.4 %fusion.83 = f32[3,384,1152]{2,1,0:T(8,128)} fusion(f32[1152]{0:T(1024)S(1)} %copy-done.119, f32[3,1024,384]{2,1,0:T(8,128)S(1)} %fusion.554), kind=kOutput, calls=%fused_computation.172 | convolution fusion | flops 16325148672 | bytes 10031616 | tf_op jit(solution)/shard_map/slc,lk->sck/dot_general | solution.py:86
  1135.0 41.7 %fusion.91 = f32[3,384,1152]{2,1,0:T(8,128)} fusion(f32[1152]{0:T(1024)S(1)} %copy-done.119, f32[3,1024,384]{2,1,0:T(8,128)S(1)} %fusion.558), kind=kOutput, calls=%fused_computation.180 | convolution fusion | flops 16325148672 | bytes 10031616 | tf_op jit(solution)/shard_map/slc,lk->sck/dot_general | solution.py:85
  1184.9 57.3 %fusion.42 = f32[1024,3,384]{2,0,1:T(8,128)S(1)} fusion(f32[3,384,1152]{2,1,0:T(8,128)} %fusion.83, f32[3,384,1152]{2,1,0:T(8,128)} %fusion.91, f32[384,1152]{1,0:T(8,128)} %fusion.125, f32[384,1152]{1,0:T(8,128)} %fusion.133, f32[1152]{0:T(1024)S(1)} %copy-done.204), kind=kOutput, calls=%fused_computation.119 | convolution fusion | flops 16329129984 | bytes 18878976 | tf_op jit(solution)/shard_map/sck,lk->slc/dot_general | solution.py:91
  1242.3 40.5 %multiply_convert_fusion.2 = (bf16[3,1024,384]{2,1,0:T(8,128)(2,1)S(1)}, f32[3,1024,384]{2,1,0:T(8,128)}) fusion(f32[3,1024,1152]{2,1,0:T(8,128)S(1)} %multiply_add_fusion.2, f32[384]{0:T(512)S(1)} %copy-done.226, f32[1024,3,384]{2,0,1:T(8,128)S(1)} %fusion.42, f32[1152]{0:T(1024)S(1)} %copy-done.204, f32[3,384,1152]{2,1,0:T(8,128)S(1)} %copy-done.32), kind=kOutput, calls=%fused_computation.205 | convolution fusion | flops 16332226560 | bytes 31266816 | tf_op jit(solution)/shard_map/sck,lk->slc/dot_general | solution.py:91
  1289.4 59.3 %reduce-scatter.17.cloned.1.call-done = bf16[1536,768]{1,0:T(8,128)(2,1)} async-done(((bf16[3072,768]{1,0:T(8,128)(2,1)}), bf16[1536,768]{1,0:T(8,128)(2,1)}) %reduce-scatter.17.cloned.1.call-update) | async-done | bytes 2359312 | tf_op jit(solution)/shard_map/reduce_scatter | solution.py:107
  1361.4 27.8 all-to-all-done.7
  1394.1 62.9 %all-gather.38.cloned.1.call-done = bf16[3072,768]{1,0:T(8,128)(2,1)} async-done(((bf16[1536,768]{1,0:T(8,128)(2,1)}), bf16[3072,768]{1,0:T(8,128)(2,1)}) %all-gather.38.cloned.1.call-update) | async-done | bytes 4718608 | tf_op jit(solution)/shard_map/all_gather | solution.py:103
  1457.1 49.9 %multiply_convert_fusion = (bf16[3072,1536]{1,0:T(8,128)(2,1)}, f32[3072,1536]{1,0:T(8,128)}, f32[3072,1536]{1,0:T(8,128)}) fusion(f32[1536]{0:T(1024)S(1)} %dynamic-slice_reduce_fusion, bf16[3072,768]{1,0:T(8,128)(2,1)} %all-gather.38.cloned.1.call-done, bf16[1,768,1536]{2,1,0:T(8,128)(2,1)} %all-gather.62.cloned.1.call-done), kind=kOutput, calls=%fused_computation.11 | convolution fusion | flops 7559184384 | bytes 54269952 | tf_op jit(solution)/shard_map/dot_general | solution.py:264
  1506.9 57.7 %all-gather.44.cloned.1.call-done = bf16[3072,768]{1,0:T(8,128)(2,1)} async-done(((bf16[1536,768]{1,0:T(8,128)(2,1)}), bf16[3072,768]{1,0:T(8,128)(2,1)}) %all-gather.44.cloned.1.call-update) | async-done | bytes 4718608 | tf_op jit(solution)/shard_map/all_gather | solution.py:103
  1564.6 22.2 fusion.483
  1614.6 45.4 %reduce-scatter.21.cloned.1.call-done = bf16[1536,768]{1,0:T(8,128)(2,1)} async-done(((bf16[3072,768]{1,0:T(8,128)(2,1)}), bf16[1536,768]{1,0:T(8,128)(2,1)}) %reduce-scatter.21.cloned.1.call-update) | async-done | bytes 2359312 | tf_op jit(solution)/shard_map/reduce_scatter | solution.py:107
  1664.7 57.5 %reduce-scatter.19.cloned.1.call-done = bf16[1536,768]{1,0:T(8,128)(2,1)} async-done(((bf16[3072,768]{1,0:T(8,128)(2,1)}), bf16[1536,768]{1,0:T(8,128)(2,1)}) %reduce-scatter.19.cloned.1.call-update) | async-done | bytes 2359312 | tf_op jit(solution)/shard_map/reduce_scatter | solution.py:107
  1750.0 44.4 %all-gather.46.cloned.1.call-done = bf16[3072,768]{1,0:T(8,128)(2,1)} async-done(((bf16[1536,768]{1,0:T(8,128)(2,1)}), bf16[3072,768]{1,0:T(8,128)(2,1)}) %all-gather.46.cloned.1.call-update) | async-done | bytes 4718608 | tf_op jit(solution)/shard_map/all_gather | solution.py:103
  1813.0 45.7 %fusion.89 = f32[3,384,1152]{2,1,0:T(8,128)} fusion(f32[3,1024,384]{2,1,0:T(8,128)} %get-tuple-element.174, f32[1152]{0:T(1024)S(1)} %copy-done.120), kind=kOutput, calls=%fused_computation.178 | convolution fusion | flops 16325148672 | bytes 10031616 | tf_op jit(solution)/shard_map/slc,lk->sck/dot_general | solution.py:85
  1858.9 28.1 add_reduce_fusion
  1895.1 44.7 %fusion.34 = f32[1024,3,384]{2,0,1:T(8,128)} fusion(f32[3,384,1152]{2,1,0:T(8,128)} %fusion.89, f32[3,384,1152]{2,1,0:T(8,128)} %get-tuple-element.256, f32[384,1152]{1,0:T(8,128)S(1)} %copy-done.28, f32[384,1152]{1,0:T(8,128)S(1)} %copy-done.29, f32[1152]{0:T(1024)S(1)} %copy-done.205), kind=kOutput, calls=%fused_computation.111 | convolution fusion | flops 16329129984 | bytes 18878976 | tf_op jit(solution)/shard_map/sck,lk->slc/dot_general | solution.py:91
  1939.9 43.4 %slice_multiply_fusion = (f32[3,1024,384]{2,1,0:T(8,128)S(1)}, f32[3,1024,384]{2,1,0:T(8,128)}) fusion(f32[3,1024,1152]{2,1,0:T(8,128)} %copy-done.4, f32[3,1024,384]{2,1,0:T(8,128)S(1)} %bitcast.481, f32[384]{0:T(512)S(1)} %copy-done.227, f32[1024,3,384]{2,0,1:T(8,128)} %fusion.34, f32[1152]{0:T(1024)S(1)} %copy-done.205, f32[3,384,1152]{2,1,0:T(8,128)S(1)} %copy-done.30), kind=kOutput, calls=%fused_computation.217 | convolution fusion | flops 16331046912 | bytes 33626112 | tf_op jit(solution)/shard_map/sck,lk->slc/dot_general | solution.py:91
  1983.3 22.3 multiply_reduce_fusion.1
  2030.5 60.1 %reduce-scatter.23.cloned.1.call-done = bf16[1536,768]{1,0:T(8,128)(2,1)} async-done(((bf16[3072,768]{1,0:T(8,128)(2,1)}), bf16[1536,768]{1,0:T(8,128)(2,1)}) %reduce-scatter.23.cloned.1.call-update) | async-done | bytes 2359312 | tf_op jit(solution)/shard_map/reduce_scatter | solution.py:107
  2113.5 62.8 %all-gather.48.cloned.1.call-done = bf16[3072,768]{1,0:T(8,128)(2,1)} async-done(((bf16[1536,768]{1,0:T(8,128)(2,1)}), bf16[3072,768]{1,0:T(8,128)(2,1)}) %all-gather.48.cloned.1.call-update) | async-done | bytes 4718608 | tf_op jit(solution)/shard_map/all_gather | solution.py:103
  2176.3 22.2 fusion.484
  2211.5 60.1 %reduce-scatter.25.cloned.1.call-done = bf16[1536,768]{1,0:T(8,128)(2,1)} async-done(((bf16[3072,768]{1,0:T(8,128)(2,1)}), bf16[1536,768]{1,0:T(8,128)(2,1)}) %reduce-scatter.25.cloned.1.call-update) | async-done | bytes 2359312 | tf_op jit(solution)/shard_map/reduce_scatter | solution.py:107
  2309.3 44.3 %all-gather.50.cloned.1.call-done = bf16[3072,768]{1,0:T(8,128)(2,1)} async-done(((bf16[1536,768]{1,0:T(8,128)(2,1)}), bf16[3072,768]{1,0:T(8,128)(2,1)}) %all-gather.50.cloned.1.call-update) | async-done | bytes 4718608 | tf_op jit(solution)/shard_map/all_gather | solution.py:103
  2368.4 44.2 %fusion.87 = f32[3,384,1152]{2,1,0:T(8,128)S(1)} fusion(f32[3,1024,384]{2,1,0:T(8,128)} %get-tuple-element.172, f32[1152]{0:T(1024)S(1)} %copy-done.120), kind=kOutput, calls=%fused_computation.176 | convolution fusion | flops 16325148672 | bytes 10031616 | tf_op jit(solution)/shard_map/slc,lk->sck/dot_general | solution.py:85
  2412.7 28.8 add_reduce_fusion.1
  2447.6 43.7 %fusion.26 = f32[1024,3,384]{2,0,1:T(8,128)} fusion(f32[3,384,1152]{2,1,0:T(8,128)S(1)} %fusion.87, f32[3,384,1152]{2,1,0:T(8,128)} %get-tuple-element.257, f32[384,1152]{1,0:T(8,128)S(1)} %copy-done.27, f32[384,1152]{1,0:T(8,128)} %fusion.135, f32[1152]{0:T(1024)S(1)} %copy-done.206), kind=kOutput, calls=%fused_computation.103 | convolution fusion | flops 16329129984 | bytes 18878976 | tf_op jit(solution)/shard_map/sck,lk->slc/dot_general | solution.py:91
  2491.4 43.4 %slice_multiply_fusion.4 = (f32[3,1024,384]{2,1,0:T(8,128)S(1)}, f32[3,1024,384]{2,1,0:T(8,128)}) fusion(f32[3,1024,1152]{2,1,0:T(8,128)} %copy-done.3, f32[3,1024,384]{2,1,0:T(8,128)S(1)} %bitcast.479, f32[384]{0:T(512)S(1)} %copy-done.225, f32[1024,3,384]{2,0,1:T(8,128)} %fusion.26, f32[1152]{0:T(1024)S(1)} %copy-done.206, f32[3,384,1152]{2,1,0:T(8,128)S(1)} %copy-done.31), kind=kOutput, calls=%fused_computation.221 | convolution fusion | flops 16331046912 | bytes 33626112 | tf_op jit(solution)/shard_map/sck,lk->slc/dot_general | solution.py:91
  2606.1 57.6 %all_to_all.186 = bf16[1536,2,384]{2,0,1:T(8,128)(2,1)} all-to-all(bf16[1536,2,384]{2,0,1:T(8,128)(2,1)S(1)} %bitcast.489), channel_id=1, replica_groups=mesh['dp'=16,'tensor'=2] {'tensor'}, dimensions={1} | all-to-all | bytes 4718592 | tf_op jit(solution)/shard_map/all_to_all | solution.py:430
  2664.0 30.6 all_to_all.187
  2710.8 29.4 all_to_all.188
  2791.4 26.2 fusion.119
  2817.8 25.9 add_multiply_fusion
  2929.8 26.4 fusion.117
  2956.4 25.8 add_multiply_fusion.1
  2994.4 23.6 gather_fusion.2
  3018.1 158.0 %all-gather.34.cloned.1.call-done = bf16[49152,384]{1,0:T(8,128)(2,1)} async-done(((bf16[3072,384]{1,0:T(8,128)(2,1)}), bf16[49152,384]{1,0:T(8,128)(2,1)}) %all-gather.34.cloned.1.call-update) | async-done | bytes 37748752 | tf_op jit(solution)/shard_map/all_gather | solution.py:444
  3176.0 32.8 gather_fusion.1
  3208.8 156.6 %all-gather.52.cloned.1.call-done = bf16[49152,384]{1,0:T(8,128)(2,1)} async-done(((bf16[3072,384]{1,0:T(8,128)(2,1)}), bf16[49152,384]{1,0:T(8,128)(2,1)}) %all-gather.52.cloned.1.call-update) | async-done | bytes 37748752 | tf_op jit(solution)/shard_map/all_gather | solution.py:446
  3365.5 32.8 gather_fusion.4
  3432.7 59.6 %reduce-scatter.29.cloned.1.call-done = bf16[1,3,48,384]{3,2,1,0:T(8,128)(2,1)} async-done(((bf16[1,3,768,384]{3,2,1,0:T(8,128)(2,1)}), bf16[1,3,48,384]{3,2,1,0:T(8,128)(2,1)}) %reduce-scatter.29.cloned.1.call-update) | async-done | bytes 110608 | tf_op jit(solution)/shard_map/reduce_scatter | solution.py:117
  3494.1 223.2 %all-reduce.45.cloned.1.call-done = (bf16[1,384,768]{1,0,2:T(2,128)(2,1)}, bf16[1,384,768]{1,0,2:T(2,128)(2,1)}, bf16[1,1536,768]{1,0,2:T(2,128)(2,1)}, bf16[1,1536,768]{1,0,2:T(2,128)(2,1)}) async-done(((bf16[1,384,768]{1,0,2:T(2,128)(2,1)}, bf16[1,384,768]{1,0,2:T(2,128)(2,1)}, bf16[1,1536,768]{1,0,2:T(2,128)(2,1)}, bf16[1,1536,768]{1,0,2:T(2,128)(2,1)}), (bf16[1,384,768]{1,0,2:T(2,128)(2,1)}, ...) | async-done | bytes 5898256
  3728.1 125.6 %all-reduce.41.cloned.1.call-done = (f32[2,3,768]{2,0,1:T(2,128)}, f32[2,3,3,768]{3,0,2,1:T(2,128)}, f32[2,33,64]{2,1,0:T(8,128)}, f32[2,3,64]{2,1,0:T(4,128)}, ...) async-done(((f32[2,3,768]{2,0,1:T(2,128)}, ...) | async-done | bytes 161296 | tf_op jit(solution)/shard_map/psum | solution.py:411
  3862.9 126.8 %all-reduce.43.cloned.1.call-done = (f32[2,2,64,64]{3,2,1,0:T(8,128)}, f32[2,64,768]{2,1,0:T(8,128)}) async-done(((f32[2,2,64,64]{3,2,1,0:T(8,128)}, f32[2,64,768]{2,1,0:T(8,128)}), (f32[2,2,64,64]{3,2,1,0:T(8,128)}, f32[2,64,768]{2,1,0:T(8,128)})) %all-reduce.43.cloned.1.call-update) | async-done | bytes 458768 | tf_op jit(solution)/shard_map/psum | solution.py:411
  (893 shorter events, 716.5 us)
Async XLA Ops:
  7.2 155.1 %all-gather.28.cloned.1.call-start = ((), (), s32[]{:S(2)}) async-start(), calls=%async_computation.22 | async-start | bytes 26738688 | tf_op jit(solution)/shard_map/all_gather | solution.py:178
  33.0 259.5 %all-gather.42.cloned.1.call-start = ((), (), s32[]{:S(2)}) async-start(), calls=%async_computation.33 | async-start | bytes 26738688 | tf_op jit(solution)/shard_map/all_gather | solution.py:179
  55.5 390.3 %all-gather.54.cloned.1.call-start = ((), (), s32[]{:S(2)}) async-start(), calls=%async_computation.47 | async-start | bytes 1880064 | tf_op jit(solution)/shard_map/all_gather | solution.py:199
  322.3 32.3 all-to-all-start.1
  326.2 122.2 %all-gather.30.cloned.1.call-start = ((), (), s32[]{:S(2)}) async-start(), calls=%async_computation.23 | async-start | bytes 7077888 | tf_op jit(solution)/shard_map/all_gather | solution.py:103
  327.9 132.3 %copy-start.129 = (f32[1152]{0:T(1024)}, f32[1152]{0:T(1024)S(1)}, u32[]{:S(2)}) copy-start(f32[1152]{0:T(1024)S(1)} %mul.1039) | copy-start | bytes 13828
  327.9 132.2 %copy-start.110 = (f32[1152]{0:T(1024)}, f32[1152]{0:T(1024)S(1)}, u32[]{:S(2)}) copy-start(f32[1152]{0:T(1024)S(1)} %mul.1048) | copy-start | bytes 13828
  328.0 132.2 %copy-start.112 = (f32[1152]{0:T(1024)}, f32[1152]{0:T(1024)S(1)}, u32[]{:S(2)}) copy-start(f32[1152]{0:T(1024)S(1)} %mul.1051) | copy-start | bytes 13828
  328.6 296.4 %copy-start.224 = (f32[384]{0:T(512)}, f32[384]{0:T(512)S(1)}, u32[]{:S(2)}) copy-start(f32[384]{0:T(512)S(1)} %get-tuple-element.271) | copy-start | bytes 4612
  329.3 403.6 %copy-start.102 = (f32[768]{0:T(1024)}, f32[768]{0:T(1024)S(1)}, u32[]{:S(2)}) copy-start(f32[768]{0:T(1024)S(1)} %get-tuple-element.144) | copy-start | bytes 9220
  359.6 367.7 %reduce-scatter.13.cloned.1.call-start = ((), (), s32[]{:S(2)}) async-start(), calls=%async_computation.24 | async-start | bytes 7077888 | tf_op jit(solution)/shard_map/reduce_scatter | solution.py:107
  359.8 158.4 %copy-start.118 = (f32[1152]{0:T(1024)}, f32[1152]{0:T(1024)S(1)}, u32[]{:S(2)}) copy-start(f32[1152]{0:T(1024)S(1)} %fusion.328) | copy-start | bytes 13828
  359.8 265.3 %copy-start.203 = (f32[1152]{0:T(1024)}, f32[1152]{0:T(1024)S(1)}, u32[]{:S(2)}) copy-start(f32[1152]{0:T(1024)S(1)} %fusion.331) | copy-start | bytes 13828
  474.9 150.2 %copy-start.3 = (f32[3,1024,1152]{2,1,0:T(8,128)}, f32[3,1024,1152]{2,1,0:T(8,128)S(1)}, u32[]{:S(2)}) copy-start(f32[3,1024,1152]{2,1,0:T(8,128)S(1)} %multiply_add_fusion.3) | copy-start | bytes 42467332
  671.0 101.5 %all-gather.56.cloned.1.call-start = ((), (), s32[]{:S(2)}) async-start(), calls=%async_computation.48 | async-start | bytes 2506752 | tf_op jit(solution)/shard_map/all_gather | solution.py:205
  672.9 162.7 %all-gather.32.cloned.1.call-start = ((), (), s32[]{:S(2)}) async-start(), calls=%async_computation.25 | async-start | bytes 7077888 | tf_op jit(solution)/shard_map/all_gather | solution.py:103
  735.4 150.1 %all-gather.58.cloned.1.call-start = ((), (), s32[]{:S(2)}) async-start(), calls=%async_computation.49 | async-start | bytes 2506752 | tf_op jit(solution)/shard_map/all_gather | solution.py:208
  736.3 221.7 %reduce-scatter.15.cloned.1.call-start = ((), (), s32[]{:S(2)}) async-start(), calls=%async_computation.26 | async-start | bytes 7077888 | tf_op jit(solution)/shard_map/reduce_scatter | solution.py:107
  737.0 148.5 %copy-start.209 = (f32[1536]{0:T(1024)}, f32[1536]{0:T(1024)S(1)}, u32[]{:S(2)}) copy-start(f32[1536]{0:T(1024)S(1)} %dynamic-slice_reduce_fusion.1) | copy-start | bytes 18436
  897.8 153.6 %all-gather.60.cloned.1.call-start = ((), (), s32[]{:S(2)}) async-start(), calls=%async_computation.50 | async-start | bytes 1880064 | tf_op jit(solution)/shard_map/all_gather | solution.py:199
  898.4 167.2 %all-gather.36.cloned.1.call-start = ((), (), s32[]{:S(2)}) async-start(), calls=%async_computation.28 | async-start | bytes 7077888 | tf_op jit(solution)/shard_map/all_gather | solution.py:103
  966.2 382.5 %reduce-scatter.17.cloned.1.call-start = ((), (), s32[]{:S(2)}) async-start(), calls=%async_computation.29 | async-start | bytes 7077888 | tf_op jit(solution)/shard_map/reduce_scatter | solution.py:107
  966.4 110.5 %copy-start.131 = (f32[1152]{0:T(1024)}, f32[1152]{0:T(1024)S(1)}, u32[]{:S(2)}) copy-start(f32[1152]{0:T(1024)S(1)} %mul.1103) | copy-start | bytes 13828
  966.4 110.4 %copy-start.114 = (f32[1152]{0:T(1024)}, f32[1152]{0:T(1024)S(1)}, u32[]{:S(2)}) copy-start(f32[1152]{0:T(1024)S(1)} %mul.1112) | copy-start | bytes 13828
  966.4 110.4 %copy-start.116 = (f32[1152]{0:T(1024)}, f32[1152]{0:T(1024)S(1)}, u32[]{:S(2)}) copy-start(f32[1152]{0:T(1024)S(1)} %mul.1115) | copy-start | bytes 13828
  1091.7 150.6 %copy-start.4 = (f32[3,1024,1152]{2,1,0:T(8,128)}, f32[3,1024,1152]{2,1,0:T(8,128)S(1)}, u32[]{:S(2)}) copy-start(f32[3,1024,1152]{2,1,0:T(8,128)S(1)} %multiply_add_fusion.2) | copy-start | bytes 42467332
  1288.6 105.6 %all-gather.62.cloned.1.call-start = ((), (), s32[]{:S(2)}) async-start(), calls=%async_computation.51 | async-start | bytes 2506752 | tf_op jit(solution)/shard_map/all_gather | solution.py:205
  1289.3 167.7 %all-gather.38.cloned.1.call-start = ((), (), s32[]{:S(2)}) async-start(), calls=%async_computation.30 | async-start | bytes 7077888 | tf_op jit(solution)/shard_map/all_gather | solution.py:103
  1356.9 150.0 %all-gather.64.cloned.1.call-start = ((), (), s32[]{:S(2)}) async-start(), calls=%async_computation.52 | async-start | bytes 2506752 | tf_op jit(solution)/shard_map/all_gather | solution.py:208
  1357.5 31.8 all-to-all-start.7
  1361.3 203.3 %all-gather.44.cloned.1.call-start = ((), (), s32[]{:S(2)}) async-start(), calls=%async_computation.34 | async-start | bytes 7077888 | tf_op jit(solution)/shard_map/all_gather | solution.py:103
  1389.3 117.7 %copy-start.18 = (bf16[2,1536,384]{2,1,0:T(8,128)(2,1)}, bf16[2,1536,384]{2,1,0:T(8,128)(2,1)S(1)}, u32[]{:S(2)}) copy-start(bf16[2,1536,384]{2,1,0:T(8,128)(2,1)S(1)} %all-to-all-done.7) | copy-start | bytes 7077892
  1391.1 268.8 %reduce-scatter.21.cloned.1.call-start = ((), (), s32[]{:S(2)}) async-start(), calls=%async_computation.35 | async-start | bytes 7077888 | tf_op jit(solution)/shard_map/reduce_scatter | solution.py:107
  1599.8 122.3 %reduce-scatter.19.cloned.1.call-start = ((), (), s32[]{:S(2)}) async-start(), calls=%async_computation.31 | async-start | bytes 7077888 | tf_op jit(solution)/shard_map/reduce_scatter | solution.py:107
  1614.5 179.8 %all-gather.46.cloned.1.call-start = ((), (), s32[]{:S(2)}) async-start(), calls=%async_computation.36 | async-start | bytes 7077888 | tf_op jit(solution)/shard_map/all_gather | solution.py:103
  1731.5 359.1 %reduce-scatter.23.cloned.1.call-start = ((), (), s32[]{:S(2)}) async-start(), calls=%async_computation.37 | async-start | bytes 7077888 | tf_op jit(solution)/shard_map/reduce_scatter | solution.py:107
  1813.0 192.6 %copy-start.6 = (f32[3,1024,384]{2,1,0:T(8,128)}, f32[3,1024,384]{2,1,0:T(8,128)S(1)}, u32[]{:S(2)}) copy-start(f32[3,1024,384]{2,1,0:T(8,128)S(1)} %get-tuple-element.203) | copy-start | bytes 14155780
  2030.5 145.8 %all-gather.48.cloned.1.call-start = ((), (), s32[]{:S(2)}) async-start(), calls=%async_computation.38 | async-start | bytes 7077888 | tf_op jit(solution)/shard_map/all_gather | solution.py:103
  2113.5 158.1 %reduce-scatter.25.cloned.1.call-start = ((), (), s32[]{:S(2)}) async-start(), calls=%async_computation.39 | async-start | bytes 7077888 | tf_op jit(solution)/shard_map/reduce_scatter | solution.py:107
  2211.4 142.2 %all-gather.50.cloned.1.call-start = ((), (), s32[]{:S(2)}) async-start(), calls=%async_computation.40 | async-start | bytes 7077888 | tf_op jit(solution)/shard_map/all_gather | solution.py:103
  2290.8 404.3 %reduce-scatter.27.cloned.1.call-start = ((), (), s32[]{:S(2)}) async-start(), calls=%async_computation.41 | async-start | bytes 7077888 | tf_op jit(solution)/shard_map/reduce_scatter | solution.py:107
  2368.4 188.0 %copy-start.7 = (f32[3,1024,384]{2,1,0:T(8,128)}, f32[3,1024,384]{2,1,0:T(8,128)S(1)}, u32[]{:S(2)}) copy-start(f32[3,1024,384]{2,1,0:T(8,128)S(1)} %get-tuple-element.201) | copy-start | bytes 14155780
  2579.9 307.4 %reduce-scatter.35.cloned.1.call-start = ((), (), s32[]{:S(2)}) async-start(), calls=%async_computation.46 | async-start | bytes 2506752 | tf_op jit(solution)/shard_map/reduce_scatter | solution.py:123
  2592.7 294.6 %reduce-scatter.33.cloned.1.call-start = ((), (), s32[]{:S(2)}) async-start(), calls=%async_computation.45 | async-start | bytes 2506752 | tf_op jit(solution)/shard_map/reduce_scatter | solution.py:123
  2605.8 388.6 %all-gather.40.cloned.1.call-start = ((), (), s32[]{:S(2)}) async-start(), calls=%async_computation.32 | async-start | bytes 40108032 | tf_op jit(solution)/shard_map/all_gather | solution.py:445
  2663.7 512.3 %all-gather.34.cloned.1.call-start = ((), (), s32[]{:S(2)}) async-start(), calls=%async_computation.27 | async-start | bytes 40108032 | tf_op jit(solution)/shard_map/all_gather | solution.py:444
  2694.6 670.8 %all-gather.52.cloned.1.call-start = ((), (), s32[]{:S(2)}) async-start(), calls=%async_computation.42 | async-start | bytes 40108032 | tf_op jit(solution)/shard_map/all_gather | solution.py:446
  2740.2 692.5 %reduce-scatter.31.cloned.1.call-start = ((), (), s32[]{:S(2)}) async-start(), calls=%async_computation.44 | async-start | bytes 1880064 | tf_op jit(solution)/shard_map/reduce_scatter | solution.py:117
  2863.7 628.7 %reduce-scatter.29.cloned.1.call-start = ((), (), s32[]{:S(2)}) async-start(), calls=%async_computation.43 | async-start | bytes 1880064 | tf_op jit(solution)/shard_map/reduce_scatter | solution.py:117
  2929.7 787.6 %all-reduce.45.cloned.1.call-start = ((), (), s32[]{:S(2)}) async-start(), calls=%async_computation.55 | async-start | bytes 23592960
  3208.8 189.4 %copy-start.215 = (pred[2048]{0:T(1024)(128)(4,1)S(1)}, pred[2048]{0:T(1024)(128)(4,1)}, u32[]{:S(2)}) copy-start(pred[2048]{0:T(1024)(128)(4,1)} %get-tuple-element.223) | copy-start | bytes 6148
  3208.8 189.4 %copy-start.216 = (pred[2048]{0:T(1024)(128)(4,1)S(1)}, pred[2048]{0:T(1024)(128)(4,1)}, u32[]{:S(2)}) copy-start(pred[2048]{0:T(1024)(128)(4,1)} %get-tuple-element.224) | copy-start | bytes 6148
  3402.4 23.9 all-to-all-start.3
  3426.3 292.4 %all-to-all-start.5 = ((bf16[2,1024,384]{2,1,0:T(8,128)(2,1)}), bf16[2,1024,384]{2,1,0:T(8,128)(2,1)S(1)}, u32[]{:S(2)}, u32[]{:S(2)}) async-start(bf16[2,1024,384]{2,1,0:T(8,128)(2,1)} %bitcast.510), calls=%async_computation.9 | async-start | bytes 3145728 | tf_op jit(solution)/shard_map/all_to_all | solution.py:457
  3430.0 423.7 %all-reduce.41.cloned.1.call-start = ((), (), s32[]{:S(2)}) async-start(), calls=%async_computation.53 | async-start | bytes 380928 | tf_op jit(solution)/shard_map/psum | solution.py:411
  3432.0 557.7 %all-reduce.43.cloned.1.call-start = ((), (), s32[]{:S(2)}) async-start(), calls=%async_computation.54 | async-start | bytes 1048576 | tf_op jit(solution)/shard_map/psum | solution.py:411
  3718.6 141.6 %all-to-all-start.9 = ((bf16[2,1024,384]{2,1,0:T(8,128)(2,1)}), bf16[2,1024,384]{2,1,0:T(8,128)(2,1)}, u32[]{:S(2)}, u32[]{:S(2)}) async-start(bf16[2,1024,384]{2,1,0:T(8,128)(2,1)} %bitcast.509), calls=%async_computation.17 | async-start | bytes 3145728 | tf_op jit(solution)/shard_map/all_to_all | solution.py:458
  3857.6 132.1 %copy-start.157 = (f32[2,3,768]{2,0,1:T(2,128)S(1)}, f32[2,3,768]{2,0,1:T(2,128)}, u32[]{:S(2)}) copy-start(f32[2,3,768]{2,0,1:T(2,128)} %get-tuple-element.294) | copy-start | bytes 55300
  3857.6 132.7 %copy-start.136 = (f32[2,3,3,768]{3,0,2,1:T(2,128)S(1)}, f32[2,3,3,768]{3,0,2,1:T(2,128)}, u32[]{:S(2)}) copy-start(f32[2,3,3,768]{3,0,2,1:T(2,128)} %get-tuple-element.295) | copy-start | bytes 165892
  3857.6 136.7 %copy-start.218 = (f32[2,768]{1,0:T(2,128)S(1)}, f32[2,768]{1,0:T(2,128)}, u32[]{:S(2)}) copy-start(f32[2,768]{1,0:T(2,128)} %get-tuple-element.301) | copy-start | bytes 18436
  3857.6 137.3 %copy-start.198 = (f32[2,2,768]{2,1,0:T(2,128)S(1)}, f32[2,2,768]{2,1,0:T(2,128)}, u32[]{:S(2)}) copy-start(f32[2,2,768]{2,1,0:T(2,128)} %get-tuple-element.302) | copy-start | bytes 36868
  3857.6 137.9 %copy-start.197 = (f32[2,2,768]{2,1,0:T(2,128)S(1)}, f32[2,2,768]{2,1,0:T(2,128)}, u32[]{:S(2)}) copy-start(f32[2,2,768]{2,1,0:T(2,128)} %get-tuple-element.303) | copy-start | bytes 36868
  3857.6 138.5 %copy-start.196 = (f32[2,2,768]{2,1,0:T(2,128)S(1)}, f32[2,2,768]{2,1,0:T(2,128)}, u32[]{:S(2)}) copy-start(f32[2,2,768]{2,1,0:T(2,128)} %get-tuple-element.304) | copy-start | bytes 36868
  3857.6 139.1 %copy-start.152 = (f32[2,3072]{1,0:T(2,128)S(1)}, f32[2,3072]{1,0:T(2,128)}, u32[]{:S(2)}) copy-start(f32[2,3072]{1,0:T(2,128)} %get-tuple-element.305) | copy-start | bytes 73732
  (234 other events, 5098.3 us)
Sparse Core Ops, SparseCore 0:
  33.1 129.1 all-gather.27
  163.9 128.5 all-gather.41
  295.4 40.3 all-gather.53
  359.7 61.6 all-gather.29
  671.2 56.1 reduce-scatter.12
  730.3 42.2 all-gather.55
  774.1 61.4 all-gather.31
  838.7 42.2 all-gather.57
  898.0 59.9 reduce-scatter.14
  960.7 40.7 all-gather.59
  1003.1 62.5 all-gather.35
  1288.7 59.9 reduce-scatter.16
  1351.8 42.2 all-gather.61
  1395.6 61.4 all-gather.37
  1459.4 42.2 all-gather.63
  1503.2 61.4 all-gather.43
  1599.9 59.9 reduce-scatter.20
  1662.1 59.9 reduce-scatter.18
  1731.6 62.6 all-gather.45
  2030.6 59.9 reduce-scatter.22
  2113.6 62.6 all-gather.47
  2211.5 59.9 reduce-scatter.24
  2290.9 62.6 all-gather.49
  2580.0 85.2 reduce-scatter.26
  2669.1 62.9 reduce-scatter.34
  2736.2 61.9 reduce-scatter.32
  2799.7 186.8 all-gather.39
  2988.2 187.7 all-gather.33
  3177.6 187.8 all-gather.51
  3369.1 60.2 reduce-scatter.30
  3433.2 59.1 reduce-scatter.28
  3496.5 220.8 all-reduce.44
  3725.3 128.2 all-reduce.40
  3860.6 129.0 all-reduce.42
where the time goes:
time: 4020 us; the launch traced here: 4000 us
  waiting for transfers between devices  1910 us (48%)
  matrix products  1250 us (31%)
  other arithmetic  332 us (8%)
  local copies, waits for them, and re-layouts  258 us (6%)
  blocking collectives  213 us (5%)
    reduce_scatter x8, waiting for transfers between devices, collect(): lax.psum_scatter(jnp.dot(left, right, preferred_element_type=jnp.float32)...  395 us
    all_gather x8, waiting for transfers between devices, spread(): return lax.all_gather(values, 'tensor', axis=0, tiled=True)  347 us
    dot_general x6, matrix products, inverse_spectrum(): jnp.einsum('sck,lk->slc', imaginary, back_sine, precision=highest_accuracy)  255 us
    psum x2, waiting for transfers between devices, shards(): lax.psum((stacked[0], stacked[1], stacked[2], stacked[3], stacked[4], sta...  252 us
    dot_general x6, matrix products, forward_spectrum(): real = jnp.einsum('slc,lk->sck', signal, cosine, precision=highest_accuracy)  226 us
    unnamed x35, waiting for transfers between devices  226 us
    dot_general x6, matrix products, inverse_spectrum(): jnp.einsum('sck,lk->slc', real, back_cosine, precision=highest_accuracy)  219 us
    dot_general x6, matrix products, forward_spectrum(): jnp.einsum('slc,lk->sck', signal, sine, precision=highest_accuracy)  194 us
  transfers between devices with their start and end apart: 39, of which 27 were waited for; matrix products, arithmetic and copies ran while one was open for 19% of the time, Pallas kernels for 0%

commit v1 on v0

v1 whole, which is shorter than its diff:
```python
import functools
import math

import jax
import jax.numpy as jnp
import numpy as np
from jax import lax
from jax.experimental import pallas as pl
from jax.experimental.pallas import tpu as pltpu
from jax.sharding import PartitionSpec as P

D = 768
FF = 3072
EMB = 33
LAYERS = 2
LMAX = 1024
BLK = 128
TAPS = LMAX // BLK
LANES = 384

highest = lax.Precision.HIGHEST
f32 = jnp.float32
bf16 = jnp.bfloat16
epsilon = 1e-05
shift_value = 0.05


def wave_tables():
    waves = (np.arange(BLK) + 0.5)[:, None] * (2.0 * math.pi / (2 * BLK))

    def spectrum(places):
        angle = waves * places[None, :]
        return np.concatenate([np.cos(angle), -np.sin(angle)], axis=0)

    causal = spectrum(np.arange(2 * BLK) - BLK)
    ahead = spectrum(np.arange(2 * BLK))
    single = spectrum(np.arange(BLK))
    back = spectrum(np.arange(BLK)).T / BLK
    return causal, ahead, single, back


def layer_norm_parts(values):
    centered = values - jnp.mean(values, -1, keepdims=True)
    rate = lax.rsqrt(jnp.mean(centered * centered, -1, keepdims=True) + epsilon)
    return centered * rate, rate


def layer_norm_back(grad, scaled, rate, gain):
    g = grad * gain
    return rate * (
        g - jnp.mean(g, -1, keepdims=True) - scaled * jnp.mean(g * scaled, -1, keepdims=True)
    )


def positions_table(length):
    bands = (EMB - 1) // 2
    ramp = jnp.linspace(0.0, 1.0, length, dtype=f32)[:, None]
    places = jnp.arange(length, dtype=f32)[:, None] * (2.0 * math.pi / length)
    levels = jnp.linspace(0.0001, bands - 1, bands, dtype=f32)[None, :]
    return jnp.concatenate([ramp, jnp.cos(levels * places), -jnp.sin(levels * places)], axis=1)


def decay_table(length):
    ramp = jnp.linspace(0.0, 1.0, length, dtype=f32)[:, None]
    fastest = math.log(0.01) / 0.3
    slowest = math.log(0.01) / 1.5
    speeds = slowest + (fastest - slowest) * jnp.arange(D, dtype=jnp.int32).astype(f32) / (D - 1)
    return jnp.exp(-ramp * jnp.abs(speeds)[None, :]) + shift_value


def filter_hidden(positions, first_w, inner_w, bias_w, rate_w):
    inner = jnp.sin(rate_w[0] * (jnp.dot(positions, first_w, precision=highest) + bias_w[0]))
    inner = jnp.sin(rate_w[1] * (jnp.dot(inner, inner_w[0], precision=highest) + bias_w[1]))
    return jnp.sin(rate_w[2] * (jnp.dot(inner, inner_w[1], precision=highest) + bias_w[2]))


def rows_mask(first, count, begin, end):
    rows = first + lax.broadcasted_iota(jnp.int32, (count, 1), 0)
    return (rows >= begin) & (rows < end)


def masked_spectrum(table, block, mask):
    kept = jnp.where(mask, block.astype(f32), 0.0).astype(bf16)
    return jnp.dot(table, kept, preferred_element_type=f32)


def multiply_add(carry, left_re, left_im, right_re, right_im, conj):
    re, im = carry
    if conj:
        return (
            re + (left_re * right_re + left_im * right_im),
            im + (left_re * right_im - left_im * right_re),
        )
    return (
        re + (left_re * right_re - left_im * right_im),
        im + (left_re * right_im + left_im * right_re),
    )


def conv_forward_body(own_block, table, window, kernel, causal, back, out, spectra, total):
    blocks = spectra.shape[0]
    lanes = out.shape[1]
    origin = table[2]

    def segment(n, _):
        begin = table[3 + n] - origin
        end = table[4 + n] - origin
        head = lax.div(begin, BLK)
        tail = jnp.minimum(lax.div(end - 1, BLK), blocks - 1)

        def transform(j, _):
            at = pl.multiple_of(j * BLK, BLK)
            mask = rows_mask(at - BLK, 2 * BLK, begin, end)
            spectra[j] = masked_spectrum(causal[...], window[pl.ds(at, 2 * BLK), :], mask)
            return 0

        lax.fori_loop(head, tail + 1, transform, 0)

        def produce(j, _):
            reach = jnp.minimum(j - head, TAPS - 1) + 1
            for lane in range(0, lanes, 128):
                part = slice(lane, lane + 128)

                def lag(b, carry):
                    return multiply_add(
                        carry,
                        kernel[b, :BLK, part],
                        kernel[b, BLK:, part],
                        spectra[j - b, :BLK, part],
                        spectra[j - b, BLK:, part],
                        False,
                    )

                zero = jnp.zeros((BLK, 128), f32)
                re, im = lax.fori_loop(0, reach, lag, (zero, zero))
                total[:BLK, part] = re.astype(bf16)
                total[BLK:, part] = im.astype(bf16)
            value = jnp.dot(back[...], total[...], preferred_element_type=f32)
            at = pl.multiple_of((j - own_block) * BLK, BLK)
            mask = rows_mask(j * BLK, BLK, begin, end)
            out[pl.ds(at, BLK), :] = jnp.where(mask, value, out[pl.ds(at, BLK), :])
            return 0

        lax.fori_loop(jnp.maximum(head, own_block), tail + 1, produce, 0)
        return 0

    lax.fori_loop(table[0], table[1] + 1, segment, 0)


def conv_backward_body(
    own_block,
    table,
    window,
    grads,
    kernel,
    causal,
    ahead,
    single,
    back,
    signal_grad,
    kernel_grad,
    spectra,
    grad_spectra,
    own_spectra,
    sums,
    total,
):
    blocks = spectra.shape[0]
    grad_blocks = grad_spectra.shape[0]
    own_blocks = own_spectra.shape[0]
    lanes = signal_grad.shape[1]
    origin = table[2]
    sums[...] = jnp.zeros_like(sums)

    def segment(n, _):
        begin = table[3 + n] - origin
        end = table[4 + n] - origin
        head = lax.div(begin, BLK)
        tail = jnp.minimum(lax.div(end - 1, BLK), blocks - 1)
        first = jnp.maximum(head, own_block)
        last = jnp.minimum(lax.div(end - 1, BLK), own_block + grad_blocks - 1)

        def transform(j, _):
            at = pl.multiple_of(j * BLK, BLK)
            mask = rows_mask(at - BLK, 2 * BLK, begin, end)
            spectra[j] = masked_spectrum(causal[...], window[pl.ds(at, 2 * BLK), :], mask)
            return 0

        lax.fori_loop(head, tail + 1, transform, 0)

        def transform_grad(j, _):
            at = pl.multiple_of((j - own_block) * BLK, BLK)
            mask = rows_mask(j * BLK, 2 * BLK, begin, end)
            grad_spectra[j - own_block] = masked_spectrum(
                ahead[...], grads[pl.ds(at, 2 * BLK), :], mask
            )
            return 0

        lax.fori_loop(first, last + 1, transform_grad, 0)

        def transform_own(j, _):
            at = pl.multiple_of((j - own_block) * BLK, BLK)
            mask = rows_mask(j * BLK, BLK, begin, end)
            own_spectra[j - own_block] = masked_spectrum(
                single[...], grads[pl.ds(at, BLK), :], mask
            )
            return 0

        lax.fori_loop(first, tail + 1, transform_own, 0)

        def produce(j, _):
            reach = jnp.minimum(last - j, TAPS - 1) + 1
            for lane in range(0, lanes, 128):
                part = slice(lane, lane + 128)

                def lag(b, carry):
                    at = j - own_block + b
                    return multiply_add(
                        carry,
                        kernel[b, :BLK, part],
                        kernel[b, BLK:, part],
                        grad_spectra[at, :BLK, part],
                        grad_spectra[at, BLK:, part],
                        True,
                    )

                zero = jnp.zeros((BLK, 128), f32)
                re, im = lax.fori_loop(0, reach, lag, (zero, zero))
                total[:BLK, part] = re.astype(bf16)
                total[BLK:, part] = im.astype(bf16)
            value = jnp.dot(back[...], total[...], preferred_element_type=f32)
            at = pl.multiple_of((j - own_block) * BLK, BLK)
            mask = rows_mask(j * BLK, BLK, begin, end)
            signal_grad[pl.ds(at, BLK), :] = jnp.where(
                mask, value, signal_grad[pl.ds(at, BLK), :]
            )
            return 0

        lax.fori_loop(first, tail + 1, produce, 0)

        def accumulate(b, _):
            for lane in range(0, lanes, 128):
                part = slice(lane, lane + 128)

                def at_block(j, carry):
                    return multiply_add(
                        carry,
                        spectra[j - b, :BLK, part],
                        spectra[j - b, BLK:, part],
                        own_spectra[j - own_block, :BLK, part],
                        own_spectra[j - own_block, BLK:, part],
                        True,
                    )

                re, im = lax.fori_loop(
                    jnp.maximum(first, head + b),
                    tail + 1,
                    at_block,
                    (sums[b, :BLK, part], sums[b, BLK:, part]),
                )
                sums[b, :BLK, part] = re
                sums[b, BLK:, part] = im
            return 0

        lax.fori_loop(0, jnp.minimum(tail - head, TAPS - 1) + 1, accumulate, 0)
        return 0

    lax.fori_loop(table[0], table[1] + 1, segment, 0)
    for b in range(TAPS):
        kernel_grad[b * BLK : (b + 1) * BLK, :] = jnp.dot(
            back[...], sums[b].astype(bf16), preferred_element_type=f32
        )


def fixed(shape):
    return pl.BlockSpec(shape, lambda c, table: (0,) * len(shape))


def by_lane(shape):
    return pl.BlockSpec(shape, lambda c, table: (0,) * (len(shape) - 1) + (c,))


def conv_forward(table, window, kernel, rows, tables):
    causal, _, _, back = tables
    wide = window.shape[0]
    blocks = wide // BLK - 1
    own_block = (wide - BLK - rows) // BLK
    return pl.pallas_call(
        functools.partial(conv_forward_body, own_block),
        out_shape=jax.ShapeDtypeStruct((rows, D), f32),
        grid_spec=pltpu.PrefetchScalarGridSpec(
            num_scalar_prefetch=1,
            grid=(D // LANES,),
            in_specs=[
                by_lane((wide, LANES)),
                by_lane((TAPS, 2 * BLK, LANES)),
                fixed((2 * BLK, 2 * BLK)),
                fixed((BLK, 2 * BLK)),
            ],
            out_specs=by_lane((rows, LANES)),
            scratch_shapes=[
                pltpu.VMEM((blocks, 2 * BLK, LANES), f32),
                pltpu.VMEM((2 * BLK, LANES), bf16),
            ],
        ),
        compiler_params=pltpu.CompilerParams(vmem_limit_bytes=40 << 20),
        cost_estimate=pl.CostEstimate(
            flops=4_000_000_000, bytes_accessed=20_000_000, transcendentals=0
        ),
        name="conv_forward",
    )(table, window, kernel, causal, back)


def conv_backward(table, window, grads, kernel, rows, tables):
    causal, ahead, single, back = tables
    wide = window.shape[0]
    blocks = wide // BLK - 1
    grad_blocks = grads.shape[0] // BLK - 1
    own_block = (wide - BLK - rows) // BLK
    return pl.pallas_call(
        functools.partial(conv_backward_body, own_block),
        out_shape=(
            jax.ShapeDtypeStruct((rows, D), f32),
            jax.ShapeDtypeStruct((LMAX, D), f32),
        ),
        grid_spec=pltpu.PrefetchScalarGridSpec(
            num_scalar_prefetch=1,
            grid=(D // LANES,),
            in_specs=[
                by_lane((wide, LANES)),
                by_lane((grads.shape[0], LANES)),
                by_lane((TAPS, 2 * BLK, LANES)),
                fixed((2 * BLK, 2 * BLK)),
                fixed((2 * BLK, 2 * BLK)),
                fixed((2 * BLK, BLK)),
                fixed((BLK, 2 * BLK)),
            ],
            out_specs=(by_lane((rows, LANES)), by_lane((LMAX, LANES))),
            scratch_shapes=[
                pltpu.VMEM((blocks, 2 * BLK, LANES), f32),
                pltpu.VMEM((grad_blocks, 2 * BLK, LANES), f32),
                pltpu.VMEM((rows // BLK, 2 * BLK, LANES), f32),
                pltpu.VMEM((TAPS, 2 * BLK, LANES), f32),
                pltpu.VMEM((2 * BLK, LANES), bf16),
            ],
        ),
        compiler_params=pltpu.CompilerParams(vmem_limit_bytes=50 << 20),
        cost_estimate=pl.CostEstimate(
            flops=8_000_000_000, bytes_accessed=30_000_000, transcendentals=0
        ),
        name="conv_backward",
    )(table, window, grads, kernel, causal, ahead, single, back)


def shards(
    tokens,
    out_grad,
    seq_lengths,
    deal_order,
    input_weight,
    output_weight,
    up_projection_weight,
    down_projection_weight,
    input_bias,
    short_taps,
    filter_first,
    filter_inner,
    filter_biases,
    filter_rates,
    filter_out,
    conv_bias,
    norm_gains,
    norm_biases,
    output_biases,
    up_projection_bias,
):
    tensor_count = lax.axis_size("tensor")
    group_count = lax.axis_size("dp")
    devices = tensor_count * group_count
    rank = lax.axis_index("dp") * tensor_count + lax.axis_index("tensor")
    rows = tokens.shape[0]
    width = input_weight.shape[3]
    hidden = up_projection_weight.shape[2]
    depth = input_weight.shape[2]
    columns = 4 * width + 2 * hidden
    count = seq_lengths.shape[0]
    everyone = ("dp", "tensor")
    owners = ("tensor", "dp")
    hops = -(-(LMAX - 1) // rows)

    def from_before(values, hop=1):
        return lax.ppermute(values, everyone, [(i, i + hop) for i in range(devices - hop)])

    def from_after(values, hop=1):
        return lax.ppermute(values, everyone, [(i + hop, i) for i in range(devices - hop)])

    held = [
        jnp.concatenate(
            [
                jnp.transpose(input_weight[layer].astype(bf16), (1, 0, 2)).reshape(
                    depth, 3 * width
                ),
                jnp.transpose(output_weight[layer].astype(bf16)),
                up_projection_weight[layer].astype(bf16),
                jnp.transpose(down_projection_weight[layer].astype(bf16)),
            ],
            axis=1,
        )
        for layer in range(LAYERS)
    ]
    gathered = [
        lax.all_gather(part, owners, axis=0, tiled=True).reshape(tensor_count, D, columns)
        for part in held
    ]

    def whole(layer, start, parts, size):
        piece = gathered[layer][:, :, start : start + parts * size]
        piece = piece.reshape(tensor_count, D, parts, size)
        return jnp.transpose(piece, (1, 2, 0, 3)).reshape(D, parts * tensor_count * size)

    numbers = jnp.arange(count, dtype=jnp.int32)
    match = deal_order[:, None] == numbers[None, :]
    lengths = jnp.sum(jnp.where(match, seq_lengths[:, None], 0), axis=0)
    ends = jnp.sum(jnp.where(numbers[:, None] <= numbers[None, :], lengths[:, None], 0), axis=0)
    starts = ends - lengths
    base = rank * rows
    first_segment = jnp.sum((starts <= base).astype(jnp.int32)) - 1
    last_segment = jnp.sum((starts < base + rows).astype(jnp.int32)) - 1
    table = jnp.concatenate(
        [
            jnp.stack([first_segment, last_segment, base - hops * rows]),
            starts,
            ends[count - 1 :],
        ]
    ).astype(jnp.int32)
    places = base + jnp.arange(rows + 2, dtype=jnp.int32)
    begun = jnp.max(jnp.where(starts[None, :] <= places[:, None], starts[None, :], 0), axis=1)
    age = places - begun
    after_one = (age >= 1).astype(f32)[:, None]
    after_two = (age >= 2).astype(f32)[:, None]

    causal, ahead, single, back = wave_tables()
    tables = tuple(jnp.asarray(t, f32).astype(bf16) for t in (causal, ahead, single, back))
    positions = positions_table(LMAX)
    modulation = decay_table(LMAX)
    blank = jnp.zeros((BLK, D), bf16)

    filters = []
    for layer in range(LAYERS):
        inner, filter_back = jax.vjp(
            lambda a, b, c, d: filter_hidden(positions, a, b, c, d),
            filter_first[layer],
            filter_inner[layer],
            filter_biases[layer],
            filter_rates[layer],
        )
        kernel = jnp.dot(inner, filter_out[layer], precision=highest) * modulation
        kernel_spectra = jnp.einsum(
            "kr,brc->bkc",
            tables[2],
            kernel.reshape(TAPS, BLK, D).astype(bf16),
            preferred_element_type=f32,
        )
        filters.append((inner, filter_back, kernel_spectra))

    state = tokens.astype(f32)
    kept = []
    outputs = []
    for layer in range(LAYERS):
        in_all = whole(layer, 0, 3, width)
        out_all = whole(layer, 3 * width, 1, width)
        up_all = whole(layer, 4 * width, 1, hidden)
        down_all = whole(layer, 4 * width + hidden, 1, hidden)
        gains, biases = norm_gains[layer], norm_biases[layer]
        before_state = from_before(state[rows - 8 :].astype(f32))
        joined = jnp.concatenate([before_state, state], axis=0)
        scaled, rate = layer_norm_parts(joined)
        normed = (scaled * gains[0] + biases[0]).astype(bf16)
        projected = jnp.dot(normed, in_all, preferred_element_type=f32) + input_bias[
            layer
        ].reshape(3 * D)
        taps = short_taps[layer].reshape(3, 3 * D)
        mixed = (
            taps[0] * projected[8:]
            + taps[1] * projected[7:-1] * after_one[:rows]
            + taps[2] * projected[6:-2] * after_two[:rows]
        )
        gate_out = mixed[:, :D]
        gate_in = mixed[:, D : 2 * D]
        values = mixed[:, 2 * D :]
        signal = gate_in * values
        signal_low = signal.astype(bf16)
        window = jnp.concatenate(
            [blank] + [from_before(signal_low, hop) for hop in range(hops, 0, -1)] + [signal_low]
        )
        carried = (
            conv_forward(table, window, filters[layer][2], rows, tables)
            + conv_bias[layer] * signal
        )
        mixer = (gate_out * carried).astype(bf16)
        middle = (
            state
            + jnp.einsum("rc,dc->rd", mixer, out_all, preferred_element_type=f32)
            + output_biases[layer, 0]
        )
        second_scaled, second_rate = layer_norm_parts(middle)
        second = (second_scaled * gains[1] + biases[1]).astype(bf16)
        before = (
            jnp.dot(second, up_all, preferred_element_type=f32) + up_projection_bias[layer]
        )
        cumulative = 0.5 * (1.0 + lax.erf(before * math.sqrt(0.5)))
        slope = (
            cumulative + before * jnp.exp(-0.5 * before * before) * (1.0 / math.sqrt(2 * math.pi))
        ).astype(bf16)
        activated = (before * cumulative).astype(bf16)
        new_state = (
            middle
            + jnp.einsum("rf,df->rd", activated, down_all, preferred_element_type=f32)
            + output_biases[layer, 1]
        )
        outputs.append(new_state.astype(bf16))
        kept.append(
            (
                in_all, out_all, up_all, down_all, scaled[8:], rate[8:], normed[8:], projected,
                gate_out, gate_in, values, signal, window, carried, mixer, second_scaled,
                second_rate, second, slope, activated,
            )
        )
        state = new_state

    def sum_rows(values):
        return jnp.sum(values, axis=0)

    grad = out_grad.astype(f32)
    owned = [None] * LAYERS
    small = [None] * LAYERS
    for layer in reversed(range(LAYERS)):
        (
            in_all, out_all, up_all, down_all, scaled, rate, normed, projected,
            gate_out, gate_in, values, signal, window, carried, mixer, second_scaled,
            second_rate, second, slope, activated,
        ) = kept[layer]
        gains = norm_gains[layer]
        inner, filter_back, kernel_spectra = filters[layer]
        down_bias_grad = sum_rows(grad)
        grad_low = grad.astype(bf16)
        down_grad = jnp.einsum("rd,rf->df", grad_low, activated, preferred_element_type=f32)
        before_grad = (
            jnp.dot(grad_low, down_all, preferred_element_type=f32) * slope.astype(f32)
        )
        up_bias_grad = sum_rows(before_grad)
        before_low = before_grad.astype(bf16)
        up_grad = jnp.einsum("rd,rf->df", second, before_low, preferred_element_type=f32)
        second_grad = jnp.einsum("rf,df->rd", before_low, up_all, preferred_element_type=f32)
        second_gain_grad = sum_rows(second_grad * second_scaled)
        second_bias_grad = sum_rows(second_grad)
        middle_grad = grad + layer_norm_back(second_grad, second_scaled, second_rate, gains[1])
        mixer_bias_grad = sum_rows(middle_grad)
        middle_low = middle_grad.astype(bf16)
        out_grad_part = jnp.einsum("rd,rc->dc", middle_low, mixer, preferred_element_type=f32)
        mixer_grad = jnp.dot(middle_low, out_all, preferred_element_type=f32)
        carried_grad = mixer_grad * gate_out
        carried_low = carried_grad.astype(bf16)
        grads_window = jnp.concatenate(
            [carried_low] + [from_after(carried_low, hop) for hop in range(1, hops + 1)] + [blank]
        )
        conv_bias_grad = sum_rows(carried_grad * signal)
        signal_grad, kernel_grad = conv_backward(
            table, window, grads_window, kernel_spectra, rows, tables
        )
        signal_grad = signal_grad + conv_bias[layer] * carried_grad
        mixed_grad = jnp.concatenate(
            [mixer_grad * carried, signal_grad * values, signal_grad * gate_in], axis=1
        )
        after = from_after(mixed_grad[:8])
        spread = jnp.concatenate([mixed_grad, after], axis=0)
        taps = short_taps[layer].reshape(3, 3 * D)
        projected_grad = (
            taps[0] * mixed_grad
            + taps[1] * spread[1 : rows + 1] * after_one[1 : rows + 1]
            + taps[2] * spread[2 : rows + 2] * after_two[2 : rows + 2]
        )
        taps_grad = jnp.stack(
            [
                sum_rows(mixed_grad * projected[8:]),
                sum_rows(mixed_grad * projected[7:-1] * after_one[:rows]),
                sum_rows(mixed_grad * projected[6:-2] * after_two[:rows]),
            ]
        )
        in_bias_grad = sum_rows(projected_grad)
        projected_low = projected_grad.astype(bf16)
        in_grad_part = jnp.einsum("rd,rc->dc", normed, projected_low, preferred_element_type=f32)
        first_grad = jnp.einsum("rc,dc->rd", projected_low, in_all, preferred_element_type=f32)
        first_gain_grad = sum_rows(first_grad * scaled)
        first_bias_grad = sum_rows(first_grad)
        grad = middle_grad + layer_norm_back(first_grad, scaled, rate, gains[0])

        def by_owner(whole_grad, parts):
            size = whole_grad.shape[1] // (parts * tensor_count)
            piece = whole_grad.astype(bf16).reshape(D, parts, tensor_count, size)
            return jnp.transpose(piece, (2, 0, 1, 3)).reshape(tensor_count, D, parts * size)

        stacked = jnp.concatenate(
            [
                by_owner(in_grad_part, 3),
                by_owner(out_grad_part, 1),
                by_owner(up_grad, 1),
                by_owner(down_grad, 1),
            ],
            axis=2,
        ).reshape(tensor_count * D, columns)
        owned[layer] = lax.psum_scatter(
            stacked, owners, scatter_dimension=0, tiled=True
        ).astype(f32)

        shaped = kernel_grad * modulation
        filter_out_grad = jnp.dot(jnp.transpose(inner), shaped, precision=highest)
        inner_grad = jnp.dot(shaped, jnp.transpose(filter_out[layer]), precision=highest)
        filter_grads = filter_back(inner_grad)
        small[layer] = (
            in_bias_grad.reshape(3, D),
            taps_grad.reshape(3, 3, D),
            *filter_grads,
            filter_out_grad,
            conv_bias_grad,
            jnp.stack([first_gain_grad, second_gain_grad]),
            jnp.stack([first_bias_grad, second_bias_grad]),
            jnp.stack([mixer_bias_grad, down_bias_grad]),
            up_bias_grad,
        )

    small_stacked = [
        jnp.stack([small[layer][index] for layer in range(LAYERS)])
        for index in range(len(small[0]))
    ]
    sizes = [part.size for part in small_stacked]
    flat = jnp.concatenate([part.reshape(-1) for part in small_stacked])
    unit = 1024
    padded = -(-flat.shape[0] // unit) * unit
    flat = jnp.pad(flat, (0, padded - flat.shape[0])).reshape(padded // 128, 128)
    step = 1
    while step < devices:
        low = flat.astype(bf16)
        other = lax.ppermute(low, everyone, [(i, i ^ step) for i in range(devices)])
        flat = low.astype(f32) + other.astype(f32)
        step *= 2
    flat = flat.reshape(-1)
    summed = []
    offset = 0
    for part, size in zip(small_stacked, sizes):
        summed.append(flat[offset : offset + size].reshape(part.shape))
        offset += size

    in_owned = jnp.stack(
        [
            jnp.transpose(owned[layer][:, : 3 * width].reshape(depth, 3, width), (1, 0, 2))
            for layer in range(LAYERS)
        ]
    )
    out_owned = jnp.stack(
        [jnp.transpose(owned[layer][:, 3 * width : 4 * width]) for layer in range(LAYERS)]
    )
    up_owned = jnp.stack(
        [owned[layer][:, 4 * width : 4 * width + hidden] for layer in range(LAYERS)]
    )
    down_owned = jnp.stack(
        [jnp.transpose(owned[layer][:, 4 * width + hidden :]) for layer in range(LAYERS)]
    )
    return (
        outputs[0],
        outputs[1],
        grad.astype(bf16),
        in_owned,
        out_owned,
        up_owned,
        down_owned,
        *summed,
    )


def solution(mesh):
    rows = P(("dp", "tensor"), None)
    weights = (
        P(None, None, "dp", "tensor"),
        P(None, "tensor", "dp"),
        P(None, "dp", "tensor"),
        P(None, "tensor", "dp"),
    )
    return jax.shard_map(
        shards,
        mesh=mesh,
        in_specs=(rows, rows, P(), P(), *weights) + (P(),) * 12,
        out_specs=(rows, rows, rows, *weights) + (P(),) * 12,
        check_vma=False,
    )
```

time: 4020 us -> 1110 us (0.28)
  waiting for transfers between devices: 1910 us -> 185 us
  matrix products: 1250 us -> 267 us
  blocking collectives: 213 us -> 0 us
  other arithmetic: 332 us -> 173 us
  Pallas kernels: 0 us -> 113 us
    dot_general x70 -> x48, matrix products: 1250 us -> 267 us  [the longest x2 37.3 us: shards(): jnp.dot(grad_low, down_all, preferred_element_type=f32) * slope.astype(f32)]
    all_gather x19 -> x2, waiting for transfers between devices: 913 us -> 70.1 us  [shards(): lax.all_gather(part, owners, axis=0, tiled=True)]
    reduce_scatter x12 -> x2, waiting for transfers between devices: 455 us -> 0.02 us  [shards(): lax.psum_scatter(stacked, owners, scatter_dimension=0, tiled=True)]
    psum x2 -> x0, waiting for transfers between devices: 252 us -> none  [shards(): lax.psum((stacked[0], stacked[1], stacked[2], stacked[3], stacked[4], sta...]
    unnamed x35 -> x4, waiting for transfers between devices: 226 us -> 0.07 us
    reduce_sum x33 -> x15, other arithmetic: 222 us -> 49.4 us  [the longest x6 44.4 us: sum_rows(): return jnp.sum(values, axis=0)]
    all_to_all x5 -> x0, blocking collectives: 164 us -> none  [the longest x1 57.6 us: shards(): lax.all_to_all(layer_outputs[1], 'tensor', split_axis=1, concat_axis=0, t...]
    gather x5 -> x0, local copies, waits for them, and re-layouts: 135 us -> none  [the longest x2 54.8 us: shards(): jnp.take(pieces[0], picked, axis=0)]
  transfers between devices with their start and end apart: 39 -> 17, of which waited for: 27 -> 9; matrix products, arithmetic and copies ran while one was open for 19% -> 47% of each run, Pallas kernels for 0% -> 5%
where the time goes in v1:
time: 1110 us; the launch traced here: 1100 us
  local copies, waits for them, and re-layouts  281 us (25%)
  matrix products  267 us (24%)
  waiting for transfers between devices  185 us (17%)
  other arithmetic  173 us (16%)
  Pallas kernels  113 us (10%)
  starting transfers between devices  60.9 us (5%)
  between operations  18.1 us (2%)
    pallas_call x2, Pallas kernels, conv_backward(): pl.pallas_call(functools.partial(conv_backward_body, own_block), out_shap...  81.8 us
    reshape x7, local copies, waits for them, and re-layouts, by_owner(): piece = whole_grad.astype(bf16).reshape(D, parts, tensor_count, size)  71.6 us
    all_gather x2, waiting for transfers between devices, shards(): lax.all_gather(part, owners, axis=0, tiled=True)  70.1 us
    transpose x12, local copies, waits for them, and re-layouts, whole(): jnp.transpose(piece, (1, 2, 0, 3)).reshape(D, parts * tensor_count * size)  55.1 us
    unnamed x423, local copies, waits for them, and re-layouts  49.5 us
    ppermute x4, waiting for transfers between devices, from_after(): lax.ppermute(values, everyone, [(i + hop, i) for i in range(devices - hop)])  49.3 us
    ppermute x5, waiting for transfers between devices, shards(): other = lax.ppermute(low, everyone, [(i, i ^ step) for i in range(devices)])  48.6 us
    reduce_sum x6, other arithmetic, sum_rows(): return jnp.sum(values, axis=0)  44.4 us
  transfers between devices with their start and end apart: 17, of which 9 were waited for; matrix products, arithmetic and copies ran while one was open for 47% of the time, Pallas kernels for 5%

profile of v1, /device:TPU:0, one launch (start us, length us, event | category | flops | bytes accessed | tf_op | source)
XLA Modules:
  0.0 1097.7 jit_solution(7813711467528173276)
XLA Ops:
  32.5 5.4 multiply_convert_fusion.5
  47.5 70.1 %all-gather.3.cloned.1.call-done = bf16[1536,4608]{1,0:T(8,128)(2,1)} async-done(((bf16[48,4608]{1,0:T(8,128)(2,1)}), bf16[1536,4608]{1,0:T(8,128)(2,1)}) %all-gather.3.cloned.1.call-update) | async-done | bytes 14155792 | tf_op jit(solution)/shard_map/all_gather | solution.py:412
  154.1 7.9 slice_bitcast_fusion.2
  162.1 6.6 copy.163
  168.7 6.6 copy.162
  175.3 16.0 %collective-permute-done.1 = bf16[1024,768]{1,0:T(8,128)(2,1)} collective-permute-done((bf16[1024,768]{1,0:T(8,128)(2,1)}, bf16[1024,768]{1,0:T(8,128)(2,1)}, u32[]{:S(2)}, u32[]{:S(2)}) %collective-permute-start.1) | collective-permute-done | bytes 1572896 | tf_op jit(solution)/shard_map/ppermute | solution.py:392
  196.5 15.7 %conv_forward.2 = f32[1024,768]{1,0:T(8,128)S(1)} custom-call(s32[52]{0:T(128)S(1)} %concatenate.83.table, bf16[2176,768]{1,0:T(8,128)(2,1)S(1)} %fusion.22.window, f32[8,256,768]{2,1,0:T(8,128)S(1)} %copy-done.2, bf16[256,256]{1,0:T(8,128)(2,1)S(1)} %copy-done.6, bf16[128,256]{1,0:T(8,128)(2,1)S(1)} %copy-done.8), custom_call_target="tpu_custom_call" | custom-call | flops 4000000000 | bytes 20000000 | tf_op jit(solution)/shard_map/conv_forward/pallas_call | solution.py:288
  219.7 8.4 multiply_convert_fusion.1
  228.2 6.2 fusion.189
  235.0 10.7 collective-permute-start.2
  258.9 5.8 copy.165
  299.7 8.1 slice_bitcast_fusion
  307.7 6.6 copy.172
  314.4 6.7 copy.171
  328.0 15.7 %conv_forward.3 = f32[1024,768]{1,0:T(8,128)S(1)} custom-call(s32[52]{0:T(128)S(1)} %concatenate.83.table, bf16[2176,768]{1,0:T(8,128)(2,1)S(1)} %fusion.23.window, f32[8,256,768]{2,1,0:T(8,128)S(1)} %copy-done.3, bf16[256,256]{1,0:T(8,128)(2,1)S(1)} %copy-done.6, bf16[128,256]{1,0:T(8,128)(2,1)S(1)} %copy-done.8), custom_call_target="tpu_custom_call" | custom-call | flops 4000000000 | bytes 20000000 | tf_op jit(solution)/shard_map/conv_forward/pallas_call | solution.py:288
  350.2 8.2 fusion.170
  358.4 18.0 %fusion.20 = (bf16[3072]{0:T(1024)(128)(2,1)}, bf16[1024,3072]{1,0:T(8,128)(2,1)}, bf16[1024,3072]{1,0:T(8,128)(2,1)}, f32[3072,1024]{0,1:T(8,128)}) fusion(f32[1024,3072]{1,0:T(8,128)} %fusion.170, f32[3072]{0:T(1024)S(1)} %bitcast.392, bf16[768,3072]{0,1:T(8,128)(2,1)S(1)} %bitcast.357, bf16[1024,768]{1,0:T(8,128)(2,1)S(1)} %copy-done.30), kind=kOutput, calls=%fused_computation.48 | convolution fusion | flops 4879021056 | bytes 44058624 | tf_op jit(solution)/shard_map/dot_general | solution.py:549
  376.4 11.5 %multiply_reduce_fusion.8 = (bf16[768]{0:T(1024)(128)(2,1)}, f32[1024]{0:T(1024)S(1)}, f32[1024]{0:T(1024)S(1)}, bf16[768]{0:T(1024)(128)(2,1)}, f32[1024,768]{1,0:T(8,128)}) fusion(f32[1024,768]{1,0:T(8,128)S(1)} %get-tuple-element.254, f32[1024]{0:T(1024)S(1)} %add_rsqrt_fusion.2, f32[1024]{0:T(1024)S(1)} %broadcast_multiply_fusion.10, ...), kind=kOutput, calls=%fused_computation.72 | convolution fusion | flops 4848349184 | bytes 29906944 | tf_op jit(solution)/shard_map/rf,df->rd/dot_general | solution.py:554
  391.6 7.2 multiply_reduce_fusion.12
  400.3 6.9 convolution_convert_fusion
  407.2 13.9 %convolution_convert_fusion.1 = bf16[768,3072]{1,0:T(8,128)(2,1)} fusion(bf16[1024,3072]{1,0:T(8,128)(2,1)} %get-tuple-element.165, f32[3072,1024]{0,1:T(8,128)} %get-tuple-element.255, f32[1024,768]{1,0:T(8,128)S(1)} %get-tuple-element.254, f32[768]{0:T(1024)S(1)} %copy-done.167, f32[768]{0:T(1024)S(1)} %copy-done.136, f32[1024]{0:T(1024)S(1)} %add_rsqrt_fusion.2, ...), kind=kOutput, calls=%fused_computation.51 | convolution fusion | flops 4847566848 | bytes 26753024 | tf_op jit(solution)/shard_map/rd,rf->df/dot_general | solution.py:553
  421.1 20.5 %collective-permute-done.4 = bf16[1024,768]{1,0:T(8,128)(2,1)S(1)} collective-permute-done((bf16[1024,768]{1,0:T(8,128)(2,1)S(1)}, bf16[1024,768]{1,0:T(8,128)(2,1)S(1)}, u32[]{:S(2)}, u32[]{:S(2)}) %collective-permute-start.4) | collective-permute-done | bytes 1572896 | tf_op jit(solution)/shard_map/ppermute | solution.py:395
  443.5 40.9 %conv_backward.2 = (f32[1024,768]{1,0:T(8,128)S(1)}, f32[1024,768]{1,0:T(8,128)}) custom-call(s32[52]{0:T(128)S(1)} %concatenate.83.table, bf16[2176,768]{1,0:T(8,128)(2,1)} %copy-done.5, bf16[2176,768]{1,0:T(8,128)(2,1)} %pad_maximum_fusion.9.grads, f32[8,256,768]{2,1,0:T(8,128)} %convolution_bitcast_fusion.kernel, bf16[256,256]{1,0:T(8,128)(2,1)S(1)} %copy-done.6, ...), custom_call_target="tpu_custom_call" | custom-call | flops 8000000000 | bytes 30000000 | tf_op jit(solution)/shard_map/conv_backward/pallas_call | solution.py:320
  484.4 5.3 slice_multiply_fusion.4
  489.7 7.1 pad_maximum_fusion.4
  507.0 6.6 copy.181
  513.6 11.6 %reshape.605 = bf16[768,1,2,1536]{3,2,0,1:T(2,128)(2,1)} reshape(bf16[768,3072]{1,0:T(8,128)(2,1)} %convolution_convert_fusion.1) | data formatting | bytes 9437184 | tf_op jit(solution)/shard_map/reshape | solution.py:600
  525.3 5.4 copy.180
  530.7 7.6 pad_maximum_fusion.2
  538.4 16.4 %multiply_reduce_fusion.2 = (bf16[2304]{0:T(1024)(128)(2,1)}, bf16[2304]{0:T(1024)(128)(2,1)}, bf16[2304]{0:T(1024)(128)(2,1)}, bf16[2304]{0:T(1024)(128)(2,1)}, bf16[1024,2304]{1,0:T(8,128)(2,1)}) fusion(f32[1032,2304]{1,0:T(8,128)S(1)} %bitcast.328, f32[1024,768]{1,0:T(8,128)S(1)} %copy-done.15, f32[1024,768]{1,0:T(8,128)S(1)} %get-tuple-element.191, ...), kind=kLoop, calls=%fused_computation.40 | loop fusion | flops 44817408 | bytes 61404160 | tf_op jit(solution)/shard_map/reduce_sum | solution.py:532
  554.8 7.8 convolution_convert_fusion.4
  562.6 6.4 multiply_reduce_fusion.9
  569.7 8.1 reshape.603
  577.8 12.4 %copy.178 = bf16[768,3,2,384]{0,2,3,1:T(2,128)(2,1)} copy(bf16[768,3,2,384]{3,2,1,0:T(2,128)(2,1)} %reshape.603) | data formatting | bytes 7077888 | tf_op jit(solution)/shard_map/reshape | solution.py:600
  594.6 5.9 copy.182
  600.5 12.5 %pad_maximum_fusion.1 = bf16[1536,4608]{1,0:T(8,128)(2,1)} fusion(bf16[1536,1536]{1,0:T(8,128)(2,1)} %bitcast.329, bf16[1536,1536]{1,0:T(8,128)(2,1)} %bitcast.330, bf16[1536,384]{1,0:T(8,128)(2,1)S(1)} %bitcast.352, bf16[1536,1152]{1,0:T(8,128)(2,1)} %copy.182), kind=kLoop, calls=%fused_computation.5 | loop fusion | flops 56623104 | bytes 28311552 | tf_op jit(solution)/shard_map/concatenate | solution.py:603
  619.1 19.4 %fusion.18 = (bf16[3072]{0:T(1024)(128)(2,1)}, bf16[1024,3072]{1,0:T(8,128)(2,1)}, f32[1024,3072]{1,0:T(8,128)}) fusion(f32[1024,3072]{1,0:T(8,128)} %get-tuple-element.250, f32[3072]{0:T(1024)S(1)} %bitcast.391, bf16[768,3072]{0,1:T(8,128)(2,1)} %bitcast.364, f32[1024,768]{1,0:T(8,128)S(1)} %get-tuple-element.169), kind=kOutput, calls=%fused_computation.46 | convolution fusion | flops 4873516032 | bytes 39340032 | tf_op jit(solution)/shard_map/dot_general | solution.py:549
  638.5 11.3 %multiply_reduce_fusion.10 = (bf16[768]{0:T(1024)(128)(2,1)}, f32[1024]{0:T(1024)S(1)}, f32[1024]{0:T(1024)S(1)}, bf16[768]{0:T(1024)(128)(2,1)}, f32[1024,768]{1,0:T(8,128)S(1)}) fusion(f32[1024,768]{1,0:T(8,128)S(1)} %copy-done.29, f32[1024]{0:T(1024)S(1)} %copy-done.135, f32[1024]{0:T(1024)S(1)} %copy-done.114, f32[768]{0:T(1024)S(1)} %copy-done.132, ...), kind=kOutput, calls=%fused_computation.74 | convolution fusion | flops 4848349184 | bytes 29906944 | tf_op jit(solution)/shard_map/rf,df->rd/dot_general | solution.py:554
  654.6 6.7 multiply_reduce_fusion.13
  662.9 7.1 convolution_convert_fusion.2
  669.9 14.1 %convolution_convert_fusion.3 = bf16[768,3072]{1,0:T(8,128)(2,1)} fusion(f32[1024,3072]{1,0:T(8,128)} %get-tuple-element.258, bf16[1024,3072]{1,0:T(8,128)(2,1)} %get-tuple-element.163, f32[1024,768]{1,0:T(8,128)S(1)} %copy-done.29, f32[768]{0:T(1024)S(1)} %copy-done.166, f32[768]{0:T(1024)S(1)} %copy-done.132, f32[1024]{0:T(1024)S(1)} %copy-done.135, ...), kind=kOutput, calls=%fused_computation.53 | convolution fusion | flops 4847566848 | bytes 26753024 | tf_op jit(solution)/shard_map/rd,rf->df/dot_general | solution.py:553
  684.0 28.8 %collective-permute-done.6 = bf16[1024,768]{1,0:T(8,128)(2,1)S(1)} collective-permute-done((bf16[1024,768]{1,0:T(8,128)(2,1)S(1)}, bf16[1024,768]{1,0:T(8,128)(2,1)S(1)}, u32[]{:S(2)}, u32[]{:S(2)}) %collective-permute-start.6) | collective-permute-done | bytes 1572896 | tf_op jit(solution)/shard_map/ppermute | solution.py:395
  714.8 41.0 %conv_backward.3 = (f32[1024,768]{1,0:T(8,128)S(1)}, f32[1024,768]{1,0:T(8,128)}) custom-call(s32[52]{0:T(128)S(1)} %concatenate.83.table, bf16[2176,768]{1,0:T(8,128)(2,1)} %copy-done.4, bf16[2176,768]{1,0:T(8,128)(2,1)} %pad_maximum_fusion.8.grads, f32[8,256,768]{2,1,0:T(8,128)} %convolution_bitcast_fusion.1.kernel, bf16[256,256]{1,0:T(8,128)(2,1)S(1)} %copy-done.6, ...), custom_call_target="tpu_custom_call" | custom-call | flops 8000000000 | bytes 30000000 | tf_op jit(solution)/shard_map/conv_backward/pallas_call | solution.py:320
  755.7 5.4 slice_multiply_fusion.8
  761.2 7.0 pad_maximum_fusion.5
  775.2 11.8 %reshape.601 = bf16[768,1,2,1536]{3,2,0,1:T(2,128)(2,1)} reshape(bf16[768,3072]{1,0:T(8,128)(2,1)} %convolution_convert_fusion.2) | data formatting | bytes 9437184 | tf_op jit(solution)/shard_map/reshape | solution.py:600
  787.1 5.2 copy.176
  794.7 11.6 %reshape.600 = bf16[768,1,2,1536]{3,2,0,1:T(2,128)(2,1)} reshape(bf16[768,3072]{1,0:T(8,128)(2,1)} %convolution_convert_fusion.3) | data formatting | bytes 9437184 | tf_op jit(solution)/shard_map/reshape | solution.py:600
  806.3 5.5 copy.175
  811.9 7.4 pad_maximum_fusion.3
  819.3 16.5 %multiply_reduce_fusion.5 = (bf16[2304]{0:T(1024)(128)(2,1)}, bf16[2304]{0:T(1024)(128)(2,1)}, bf16[2304]{0:T(1024)(128)(2,1)}, bf16[2304]{0:T(1024)(128)(2,1)}, bf16[1024,2304]{1,0:T(8,128)(2,1)}) fusion(f32[1032,2304]{1,0:T(8,128)S(1)} %bitcast.326, f32[1024,768]{1,0:T(8,128)S(1)} %copy-done.14, f32[1024,768]{1,0:T(8,128)S(1)} %get-tuple-element.189, ...), kind=kLoop, calls=%fused_computation.43 | loop fusion | flops 44817408 | bytes 61404160 | tf_op jit(solution)/shard_map/reduce_sum | solution.py:532
  835.8 7.7 convolution_convert_fusion.5
  843.5 6.5 reshape.598
  850.0 9.4 copy.173
  868.3 11.8 %pad_maximum_fusion = bf16[1536,4608]{1,0:T(8,128)(2,1)} fusion(bf16[1536,1536]{1,0:T(8,128)(2,1)} %bitcast.331, bf16[1536,1536]{1,0:T(8,128)(2,1)} %bitcast.332, bf16[1536,384]{1,0:T(8,128)(2,1)} %bitcast.353, bf16[1536,1152]{1,0:T(8,128)(2,1)S(1)} %copy.177), kind=kLoop, calls=%fused_computation.4 | loop fusion | flops 56623104 | bytes 28311552 | tf_op jit(solution)/shard_map/concatenate | solution.py:603
  884.6 5.6 multiply_reduce_fusion.26
  919.2 5.6 fusion.70
  925.8 7.4 multiply_reduce_fusion.29
  952.5 9.8 multiply_reduce_fusion.11
  991.1 19.4 %collective-permute-start.9 = (bf16[1216,128]{1,0:T(8,128)(2,1)S(1)}, bf16[1216,128]{1,0:T(8,128)(2,1)S(1)}, u32[]{:S(2)}, u32[]{:S(2)}) collective-permute-start(bf16[1216,128]{1,0:T(8,128)(2,1)S(1)} %add_convert_fusion.9), channel_id=1, source_target_pairs={{0,2},{1,3},{2,0},{3,1},{4,6},{5,7},{6,4},{7,5},{8,10},{9,11},{10,... | collective-permute-start | bytes 933896 | tf_op jit(solution)/shard_map/ppermute | solution.py:644
  1011.8 7.4 collective-permute-start.10
  1019.3 10.0 add_convert_fusion.3
  1029.6 20.9 %collective-permute-done.11 = bf16[1216,128]{1,0:T(8,128)(2,1)S(1)} collective-permute-done((bf16[1216,128]{1,0:T(8,128)(2,1)S(1)}, bf16[1216,128]{1,0:T(8,128)(2,1)S(1)}, u32[]{:S(2)}, u32[]{:S(2)}) %collective-permute-start.11) | collective-permute-done | bytes 311328 | tf_op jit(solution)/shard_map/ppermute | solution.py:644
  1052.8 22.3 %collective-permute-done.12 = bf16[1216,128]{1,0:T(8,128)(2,1)S(1)} collective-permute-done((bf16[1216,128]{1,0:T(8,128)(2,1)S(1)}, bf16[1216,128]{1,0:T(8,128)(2,1)S(1)}, u32[]{:S(2)}, u32[]{:S(2)}) %collective-permute-start.12) | collective-permute-done | bytes 311328 | tf_op jit(solution)/shard_map/ppermute | solution.py:644
  (694 shorter events, 300.1 us)
Async XLA Ops:
  7.2 110.5 %all-gather.3.cloned.1.call-start = ((), (), s32[]{:S(2)}) async-start(), calls=%async_computation.2 | async-start | bytes 14598144 | tf_op jit(solution)/shard_map/all_gather | solution.py:412
  10.7 21.8 %copy-start.71 = (f32[2,64,768]{2,1,0:T(8,128)S(1)}, f32[2,64,768]{2,1,0:T(8,128)}, u32[]{:S(2)}) copy-start(f32[2,64,768]{2,1,0:T(8,128)} %param.40) | copy-start | bytes 1179652
  11.5 243.3 %all-gather.5.cloned.1.call-start = ((), (), s32[]{:S(2)}) async-start(), calls=%async_computation.3 | async-start | bytes 14598144 | tf_op jit(solution)/shard_map/all_gather | solution.py:412
  12.4 1070.8 %reduce-scatter.5.cloned.1.call-start = ((), (), s32[]{:S(2)}) async-start(), calls=%async_computation.5 | async-start | bytes 14598144 | tf_op jit(solution)/shard_map/reduce_scatter | solution.py:612
  13.2 30.7 %collective-permute-start = (f32[8,768]{1,0:T(8,128)S(1)}, f32[8,768]{1,0:T(8,128)S(1)}, u32[]{:S(2)}, u32[]{:S(2)}) collective-permute-start(f32[8,768]{1,0:T(8,128)S(1)} %slice.574), channel_id=1, source_target_pairs={{0,1},{1,2},{2,3},{3,4},{4,5},{5,6},{6,7},{7,8},{8,9},{9,10},{10,1... | collective-permute-start | bytes 73736 | tf_op jit(solution)/shard_map/ppermute | solution.py:392
  18.1 19.7 %copy-start.88 = (f32[768]{0:T(1024)}, f32[768]{0:T(1024)S(1)}, u32[]{:S(2)}) copy-start(f32[768]{0:T(1024)S(1)} %add_abs_fusion) | copy-start | bytes 9220
  18.3 19.6 %copy-start.86 = (f32[1024]{0:T(1024)}, f32[1024]{0:T(1024)S(1)}, u32[]{:S(2)}) copy-start(f32[1024]{0:T(1024)S(1)} %get-tuple-element.233) | copy-start | bytes 12292
  18.3 19.6 %copy-start.91 = (f32[1024]{0:T(1024)}, f32[1024]{0:T(1024)S(1)}, u32[]{:S(2)}) copy-start(f32[1024]{0:T(1024)S(1)} %get-tuple-element.234) | copy-start | bytes 12292
  20.4 24.3 %copy-start.109 = (f32[768]{0:T(1024)}, f32[768]{0:T(1024)S(1)}, u32[]{:S(2)}) copy-start(f32[768]{0:T(1024)S(1)} %get-tuple-element.268) | copy-start | bytes 9220
  22.5 15.4 %copy-start.127 = (f32[64]{0:T(128)}, f32[64]{0:T(128)S(1)}, u32[]{:S(2)}) copy-start(f32[64]{0:T(128)S(1)} %get-tuple-element.237) | copy-start | bytes 772
  22.5 15.4 %copy-start.129 = (f32[64]{0:T(128)}, f32[64]{0:T(128)S(1)}, u32[]{:S(2)}) copy-start(f32[64]{0:T(128)S(1)} %get-tuple-element.240) | copy-start | bytes 772
  22.5 15.4 %copy-start.139 = (f32[64]{0:T(128)}, f32[64]{0:T(128)S(1)}, u32[]{:S(2)}) copy-start(f32[64]{0:T(128)S(1)} %get-tuple-element.238) | copy-start | bytes 772
  22.5 15.4 %copy-start.144 = (f32[64]{0:T(128)}, f32[64]{0:T(128)S(1)}, u32[]{:S(2)}) copy-start(f32[64]{0:T(128)S(1)} %get-tuple-element.236) | copy-start | bytes 772
  22.5 15.4 %copy-start.146 = (f32[64]{0:T(128)}, f32[64]{0:T(128)S(1)}, u32[]{:S(2)}) copy-start(f32[64]{0:T(128)S(1)} %get-tuple-element.239) | copy-start | bytes 772
  24.0 15.8 %copy-start.59 = (bf16[1024,768]{1,0:T(8,128)(2,1)S(1)}, bf16[1024,768]{1,0:T(8,128)(2,1)}, u32[]{:S(2)}) copy-start(bf16[1024,768]{1,0:T(8,128)(2,1)} %param.26) | copy-start | bytes 4718596
  41.9 90.3 %copy-start.76 = (f32[2304]{0:T(1024)}, f32[2304]{0:T(1024)S(1)}, u32[]{:S(2)}) copy-start(f32[2304]{0:T(1024)S(1)} %mul.764) | copy-start | bytes 27652
  141.1 71.1 %copy-start.18 = (f32[1024,768]{1,0:T(8,128)}, f32[1024,768]{1,0:T(8,128)S(1)}, u32[]{:S(2)}) copy-start(f32[1024,768]{1,0:T(8,128)S(1)} %get-tuple-element.185) | copy-start | bytes 9437188
  141.1 50.2 %collective-permute-start.1 = (bf16[1024,768]{1,0:T(8,128)(2,1)}, bf16[1024,768]{1,0:T(8,128)(2,1)}, u32[]{:S(2)}, u32[]{:S(2)}) collective-permute-start(bf16[1024,768]{1,0:T(8,128)(2,1)} %get-tuple-element.184), channel_id=1, source_target_pairs={{0,1},{1,2},{2,3},{3,4},{4,5},{5,6},{6,7},{7,8},{8,9},{9,10},{10,1... | collective-permute-start | bytes 4718600 | tf_op jit(solution)/shard_map/ppermute | solution.py:392
  191.4 250.2 %copy-start.31 = (bf16[128,768]{1,0:T(8,128)(2,1)}, bf16[128,768]{1,0:T(8,128)(2,1)S(1)}, u32[]{:S(2)}) copy-start(bf16[128,768]{1,0:T(8,128)(2,1)S(1)} %broadcast_in_dim.47) | copy-start | bytes 589828
  196.5 15.7 %copy-start.4 = (bf16[2176,768]{1,0:T(8,128)(2,1)}, bf16[2176,768]{1,0:T(8,128)(2,1)S(1)}, u32[]{:S(2)}) copy-start(bf16[2176,768]{1,0:T(8,128)(2,1)S(1)} %fusion.22.window) | copy-start | bytes 10027012
  196.5 15.8 %copy-start.102 = (f32[768]{0:T(1024)S(1)}, f32[768]{0:T(1024)}, u32[]{:S(2)}) copy-start(f32[768]{0:T(1024)} %get-tuple-element.159) | copy-start | bytes 9220
  228.1 17.6 %copy-start.52 = (f32[1024,64]{0,1:T(8,128)S(1)}, f32[1024,64]{0,1:T(8,128)}, u32[]{:S(2)}) copy-start(f32[1024,64]{0,1:T(8,128)} %convolution_add_fusion.2) | copy-start | bytes 786436
  228.1 17.6 %copy-start.72 = (f32[2,64,768]{2,1,0:T(8,128)S(1)}, f32[2,64,768]{2,1,0:T(8,128)}, u32[]{:S(2)}) copy-start(f32[2,64,768]{2,1,0:T(8,128)} %param.40) | copy-start | bytes 1179652
  228.1 17.6 %copy-start.89 = (f32[768]{0:T(1024)S(1)}, f32[768]{0:T(1024)}, u32[]{:S(2)}) copy-start(f32[768]{0:T(1024)} %copy-done.88) | copy-start | bytes 9220
  228.2 17.6 %copy-start.92 = (f32[1024]{0:T(1024)S(1)}, f32[1024]{0:T(1024)}, u32[]{:S(2)}) copy-start(f32[1024]{0:T(1024)} %copy-done.91) | copy-start | bytes 12292
  228.2 17.6 %copy-start.141 = (f32[64]{0:T(128)S(1)}, f32[64]{0:T(128)}, u32[]{:S(2)}) copy-start(f32[64]{0:T(128)} %get-tuple-element.235) | copy-start | bytes 772
  234.4 16.5 %copy-start.108 = (f32[3,768]{1,0:T(4,128)S(1)}, f32[3,768]{1,0:T(4,128)}, u32[]{:S(2)}) copy-start(f32[3,768]{1,0:T(4,128)} %get-tuple-element.144) | copy-start | bytes 27652
  235.0 31.9 %collective-permute-start.2 = (f32[8,768]{1,0:T(8,128)}, f32[8,768]{1,0:T(8,128)}, u32[]{:S(2)}, u32[]{:S(2)}) collective-permute-start(f32[8,768]{1,0:T(8,128)} %slice.591), channel_id=1, source_target_pairs={{0,1},{1,2},{2,3},{3,4},{4,5},{5,6},{6,7},{7,8},{8,9},{9,10},{10,1... | collective-permute-start | bytes 73736 | tf_op jit(solution)/shard_map/ppermute | solution.py:392
  287.4 35.8 %collective-permute-start.3 = (bf16[1024,768]{1,0:T(8,128)(2,1)}, bf16[1024,768]{1,0:T(8,128)(2,1)}, u32[]{:S(2)}, u32[]{:S(2)}) collective-permute-start(bf16[1024,768]{1,0:T(8,128)(2,1)} %get-tuple-element.180), channel_id=1, source_target_pairs={{0,1},{1,2},{2,3},{3,4},{4,5},{5,6},{6,7},{7,8},{8,9},{9,10},{10,1... | collective-permute-start | bytes 4718600 | tf_op jit(solution)/shard_map/ppermute | solution.py:392
  328.0 15.7 %copy-start.5 = (bf16[2176,768]{1,0:T(8,128)(2,1)}, bf16[2176,768]{1,0:T(8,128)(2,1)S(1)}, u32[]{:S(2)}) copy-start(bf16[2176,768]{1,0:T(8,128)(2,1)S(1)} %fusion.23.window) | copy-start | bytes 10027012
  328.0 15.7 %copy-start.22 = (f32[1024,768]{1,0:T(8,128)S(1)}, f32[1024,768]{1,0:T(8,128)}, u32[]{:S(2)}) copy-start(f32[1024,768]{1,0:T(8,128)} %get-tuple-element.181) | copy-start | bytes 9437188
  328.0 15.8 %copy-start.104 = (f32[768]{0:T(1024)S(1)}, f32[768]{0:T(1024)}, u32[]{:S(2)}) copy-start(f32[768]{0:T(1024)} %get-tuple-element.158) | copy-start | bytes 9220
  348.4 58.8 %copy-start.27 = (f32[1024,768]{1,0:T(8,128)}, f32[1024,768]{1,0:T(8,128)S(1)}, u32[]{:S(2)}) copy-start(f32[1024,768]{1,0:T(8,128)S(1)} %get-tuple-element.254) | copy-start | bytes 9437188
  399.0 42.6 %collective-permute-start.4 = (bf16[1024,768]{1,0:T(8,128)(2,1)S(1)}, bf16[1024,768]{1,0:T(8,128)(2,1)S(1)}, u32[]{:S(2)}, u32[]{:S(2)}) collective-permute-start(bf16[1024,768]{1,0:T(8,128)(2,1)S(1)} %convert_element_type.281), channel_id=1, source_target_pairs={{1,0},{2,1},{3,2},{4,3},{5,4},{6,5},{7,6},{8,7},{9,8},{10,9},{11,1... | collective-permute-start | bytes 4718600 | tf_op jit(solution)/shard_map/ppermute | solution.py:395
  421.1 22.4 %copy-start.7 = (bf16[256,256]{1,0:T(8,128)(2,1)S(1)}, bf16[256,256]{1,0:T(8,128)(2,1)}, u32[]{:S(2)}) copy-start(bf16[256,256]{1,0:T(8,128)(2,1)} %constant.142.ahead) | copy-start | bytes 393220
  421.1 22.4 %copy-start.9 = (bf16[256,128]{1,0:T(8,128)(2,1)S(1)}, bf16[256,128]{1,0:T(8,128)(2,1)}, u32[]{:S(2)}) copy-start(bf16[256,128]{1,0:T(8,128)(2,1)} %constant.139.single) | copy-start | bytes 196612
  498.3 32.4 %collective-permute-start.5 = (f32[8,2304]{1,0:T(8,128)}, f32[8,2304]{1,0:T(8,128)}, u32[]{:S(2)}, u32[]{:S(2)}) collective-permute-start(f32[8,2304]{1,0:T(8,128)} %slice.607), channel_id=1, source_target_pairs={{1,0},{2,1},{3,2},{4,3},{5,4},{6,5},{7,6},{8,7},{9,8},{10,9},{11,1... | collective-permute-start | bytes 221192 | tf_op jit(solution)/shard_map/ppermute | solution.py:395
  538.4 16.4 %copy-start.64 = (bf16[1032,768]{1,0:T(8,128)(2,1)S(1)}, bf16[1032,768]{1,0:T(8,128)(2,1)}, u32[]{:S(2)}) copy-start(bf16[1032,768]{1,0:T(8,128)(2,1)} %copy-done.63) | copy-start | bytes 4755460
  613.0 472.4 %reduce-scatter.3.cloned.1.call-start = ((), (), s32[]{:S(2)}) async-start(), calls=%async_computation.4 | async-start | bytes 14598144 | tf_op jit(solution)/shard_map/reduce_scatter | solution.py:612
  614.9 23.6 %slice-start.10 = ((s8[4718592]{0:T(1024)(128)(4,1)}), s8[4194304]{0:T(1024)(128)(4,1)S(1)}, s32[]{:S(2)}) async-start(s8[4718592]{0:T(1024)(128)(4,1)} %bitcast.361), calls=%async_computation.16 | async-start | bytes 8388608
  619.1 19.4 %copy-start.29 = (f32[1024,768]{1,0:T(8,128)S(1)}, f32[1024,768]{1,0:T(8,128)}, u32[]{:S(2)}) copy-start(f32[1024,768]{1,0:T(8,128)} %copy-done.28) | copy-start | bytes 9437188
  619.1 19.4 %slice-start.11 = ((s8[4718592]{0:T(1024)(128)(4,1)}), s8[524288]{0:T(1024)(128)(4,1)S(1)}, s32[]{:S(2)}) async-start(s8[4718592]{0:T(1024)(128)(4,1)} %bitcast.361), calls=%async_computation.17 | async-start | bytes 1048576
  619.1 19.4 %copy-start.114 = (f32[1024]{0:T(1024)S(1)}, f32[1024]{0:T(1024)}, u32[]{:S(2)}) copy-start(f32[1024]{0:T(1024)} %copy-done.113) | copy-start | bytes 12292
  619.1 19.4 %copy-start.132 = (f32[768]{0:T(1024)S(1)}, f32[768]{0:T(1024)}, u32[]{:S(2)}) copy-start(f32[768]{0:T(1024)} %get-tuple-element.269) | copy-start | bytes 9220
  619.1 19.4 %copy-start.135 = (f32[1024]{0:T(1024)S(1)}, f32[1024]{0:T(1024)}, u32[]{:S(2)}) copy-start(f32[1024]{0:T(1024)} %copy-done.134) | copy-start | bytes 12292
  661.5 51.3 %collective-permute-start.6 = (bf16[1024,768]{1,0:T(8,128)(2,1)S(1)}, bf16[1024,768]{1,0:T(8,128)(2,1)S(1)}, u32[]{:S(2)}, u32[]{:S(2)}) collective-permute-start(bf16[1024,768]{1,0:T(8,128)(2,1)S(1)} %convert_element_type.289), channel_id=1, source_target_pairs={{1,0},{2,1},{3,2},{4,3},{5,4},{6,5},{7,6},{8,7},{9,8},{10,9},{11,1... | collective-permute-start | bytes 4718600 | tf_op jit(solution)/shard_map/ppermute | solution.py:395
  669.9 42.9 %copy-start.32 = (bf16[128,768]{1,0:T(8,128)(2,1)S(1)}, bf16[128,768]{1,0:T(8,128)(2,1)}, u32[]{:S(2)}) copy-start(bf16[128,768]{1,0:T(8,128)(2,1)} %copy-done.31) | copy-start | bytes 589828
  769.1 42.8 %collective-permute-start.7 = (f32[8,2304]{1,0:T(8,128)S(1)}, f32[8,2304]{1,0:T(8,128)S(1)}, u32[]{:S(2)}, u32[]{:S(2)}) collective-permute-start(f32[8,2304]{1,0:T(8,128)S(1)} %slice.614), channel_id=1, source_target_pairs={{1,0},{2,1},{3,2},{4,3},{5,4},{6,5},{7,6},{8,7},{9,8},{10,9},{11,1... | collective-permute-start | bytes 221192 | tf_op jit(solution)/shard_map/ppermute | solution.py:395
  819.3 16.5 %copy-start.62 = (bf16[1032,768]{1,0:T(8,128)(2,1)S(1)}, bf16[1032,768]{1,0:T(8,128)(2,1)}, u32[]{:S(2)}) copy-start(bf16[1032,768]{1,0:T(8,128)(2,1)} %get-tuple-element.187) | copy-start | bytes 4755460
  892.3 15.3 %copy-start.121 = (bf16[2304]{0:T(1024)(128)(2,1)S(1)}, bf16[2304]{0:T(1024)(128)(2,1)}, u32[]{:S(2)}) copy-start(bf16[2304]{0:T(1024)(128)(2,1)} %get-tuple-element.109) | copy-start | bytes 13828
  892.3 15.9 %copy-start.120 = (bf16[2304]{0:T(1024)(128)(2,1)S(1)}, bf16[2304]{0:T(1024)(128)(2,1)}, u32[]{:S(2)}) copy-start(bf16[2304]{0:T(1024)(128)(2,1)} %get-tuple-element.200) | copy-start | bytes 13828
  903.6 21.2 %copy-start.73 = (bf16[1,64,768]{2,1,0:T(8,128)(2,1)S(1)}, bf16[1,64,768]{2,1,0:T(8,128)(2,1)}, u32[]{:S(2)}) copy-start(bf16[1,64,768]{2,1,0:T(8,128)(2,1)} %fusion.73) | copy-start | bytes 294916
  925.8 26.7 %copy-start.24 = (f32[1032,768]{1,0:T(8,128)S(1)}, f32[1032,768]{1,0:T(8,128)}, u32[]{:S(2)}) copy-start(f32[1032,768]{1,0:T(8,128)} %get-tuple-element.188) | copy-start | bytes 9510916
  952.5 15.9 %copy-start.50 = (bf16[155008]{0:T(1024)(128)(2,1)S(1)}, bf16[155008]{0:T(1024)(128)(2,1)}, u32[]{:S(2)}) copy-start(bf16[155008]{0:T(1024)(128)(2,1)} %custom-call) | copy-start | bytes 930052
  952.5 24.5 %copy-start.138 = (bf16[1536]{0:T(1024)(128)(2,1)S(1)}, bf16[1536]{0:T(1024)(128)(2,1)}, u32[]{:S(2)}) copy-start(bf16[1536]{0:T(1024)(128)(2,1)} %reshape.627) | copy-start | bytes 9220
  967.0 52.2 %copy-start.168 = (f32[768]{0:T(1024)S(1)}, f32[768]{0:T(1024)}, u32[]{:S(2)}) copy-start(f32[768]{0:T(1024)} %get-tuple-element.146) | copy-start | bytes 9220
  981.0 10.0 collective-permute-start.8
  991.1 20.6 %collective-permute-start.9 = (bf16[1216,128]{1,0:T(8,128)(2,1)S(1)}, bf16[1216,128]{1,0:T(8,128)(2,1)S(1)}, u32[]{:S(2)}, u32[]{:S(2)}) collective-permute-start(bf16[1216,128]{1,0:T(8,128)(2,1)S(1)} %add_convert_fusion.9), channel_id=1, source_target_pairs={{0,2},{1,3},{2,0},{3,1},{4,6},{5,7},{6,4},{7,5},{8,10},{9,11},{10,... | collective-permute-start | bytes 933896 | tf_op jit(solution)/shard_map/ppermute | solution.py:644
  1011.8 17.5 %collective-permute-start.10 = (bf16[1216,128]{1,0:T(8,128)(2,1)S(1)}, bf16[1216,128]{1,0:T(8,128)(2,1)S(1)}, u32[]{:S(2)}, u32[]{:S(2)}) collective-permute-start(bf16[1216,128]{1,0:T(8,128)(2,1)S(1)} %add_convert_fusion.8), channel_id=1, source_target_pairs={{0,4},{1,5},{2,6},{3,7},{4,0},{5,1},{6,2},{7,3},{8,12},{9,13},{10,... | collective-permute-start | bytes 933896 | tf_op jit(solution)/shard_map/ppermute | solution.py:644
  1019.2 31.5 %copy-start.17 = (f32[1024,768]{1,0:T(8,128)S(1)}, f32[1024,768]{1,0:T(8,128)}, u32[]{:S(2)}) copy-start(f32[1024,768]{1,0:T(8,128)} %copy-done.16) | copy-start | bytes 9437188
  1019.2 31.5 %copy-start.49 = (f32[1024,768]{1,0:T(8,128)S(1)}, f32[1024,768]{1,0:T(8,128)}, u32[]{:S(2)}) copy-start(f32[1024,768]{1,0:T(8,128)} %get-tuple-element.260) | copy-start | bytes 9437188
  1019.3 31.5 %copy-start.110 = (f32[768]{0:T(1024)S(1)}, f32[768]{0:T(1024)}, u32[]{:S(2)}) copy-start(f32[768]{0:T(1024)} %copy-done.109) | copy-start | bytes 9220
  1029.4 21.2 %collective-permute-start.11 = (bf16[1216,128]{1,0:T(8,128)(2,1)S(1)}, bf16[1216,128]{1,0:T(8,128)(2,1)S(1)}, u32[]{:S(2)}, u32[]{:S(2)}) collective-permute-start(bf16[1216,128]{1,0:T(8,128)(2,1)S(1)} %add_convert_fusion.7), channel_id=1, source_target_pairs={{0,8},{1,9},{2,10},{3,11},{4,12},{5,13},{6,14},{7,15},{8,0},{9,1},... | collective-permute-start | bytes 933896 | tf_op jit(solution)/shard_map/ppermute | solution.py:644
  1050.6 24.4 %collective-permute-start.12 = (bf16[1216,128]{1,0:T(8,128)(2,1)S(1)}, bf16[1216,128]{1,0:T(8,128)(2,1)S(1)}, u32[]{:S(2)}, u32[]{:S(2)}) collective-permute-start(bf16[1216,128]{1,0:T(8,128)(2,1)S(1)} %add_convert_fusion.6), channel_id=1, source_target_pairs={{0,16},{1,17},{2,18},{3,19},{4,20},{5,21},{6,22},{7,23},{8,24},{9,... | collective-permute-start | bytes 933896 | tf_op jit(solution)/shard_map/ppermute | solution.py:644
  (154 other events, 1057.2 us)
Sparse Core Ops, SparseCore 0:
  11.7 105.9 all-gather.2
  121.1 121.0 all-gather.4
  613.2 184.1 reduce-scatter.4
  880.3 198.0 reduce-scatter.2

commit v2 on v1

v2 whole, which is shorter than its diff:
```python
import functools
import math

import jax
import jax.numpy as jnp
import numpy as np
from jax import lax
from jax.experimental import pallas as pl
from jax.experimental.pallas import tpu as pltpu
from jax.sharding import PartitionSpec as P

D = 768
FF = 3072
EMB = 33
LAYERS = 2
LMAX = 1024
BLK = 128
TAPS = LMAX // BLK
LANES = 384
HIDDEN = 768
HALO = 16
STRIP = 64

highest = lax.Precision.HIGHEST
f32 = jnp.float32
bf16 = jnp.bfloat16
epsilon = 1e-05
shift_value = 0.05


def wave_tables():
    waves = (np.arange(BLK) + 0.5)[:, None] * (2.0 * math.pi / (2 * BLK))

    def spectrum(places):
        angle = waves * places[None, :]
        return np.concatenate([np.cos(angle), -np.sin(angle)], axis=0)

    causal = spectrum(np.arange(2 * BLK) - BLK)
    ahead = spectrum(np.arange(2 * BLK))
    single = spectrum(np.arange(BLK))
    back = spectrum(np.arange(BLK)).T / BLK
    return causal, ahead, single, back


def positions_table(length):
    bands = (EMB - 1) // 2
    ramp = jnp.linspace(0.0, 1.0, length, dtype=f32)[:, None]
    places = jnp.arange(length, dtype=f32)[:, None] * (2.0 * math.pi / length)
    levels = jnp.linspace(0.0001, bands - 1, bands, dtype=f32)[None, :]
    return jnp.concatenate([ramp, jnp.cos(levels * places), -jnp.sin(levels * places)], axis=1)


def decay_table(length):
    ramp = jnp.linspace(0.0, 1.0, length, dtype=f32)[:, None]
    fastest = math.log(0.01) / 0.3
    slowest = math.log(0.01) / 1.5
    speeds = slowest + (fastest - slowest) * jnp.arange(D, dtype=jnp.int32).astype(f32) / (D - 1)
    return jnp.exp(-ramp * jnp.abs(speeds)[None, :]) + shift_value


def filter_hidden(positions, first_w, inner_w, bias_w, rate_w):
    inner = jnp.sin(rate_w[0] * (jnp.dot(positions, first_w, precision=highest) + bias_w[0]))
    inner = jnp.sin(rate_w[1] * (jnp.dot(inner, inner_w[0], precision=highest) + bias_w[1]))
    return jnp.sin(rate_w[2] * (jnp.dot(inner, inner_w[1], precision=highest) + bias_w[2]))


def rows_mask(first, count, begin, end):
    rows = first + lax.broadcasted_iota(jnp.int32, (count, 1), 0)
    return (rows >= begin) & (rows < end)


def masked_spectrum(table, block, mask):
    kept = jnp.where(mask, block.astype(f32), 0.0).astype(bf16)
    return jnp.dot(table, kept, preferred_element_type=f32)


def multiply_add(carry, left_re, left_im, right_re, right_im, conj):
    re, im = carry
    if conj:
        return (
            re + (left_re * right_re + left_im * right_im),
            im + (left_re * right_im - left_im * right_re),
        )
    return (
        re + (left_re * right_re - left_im * right_im),
        im + (left_re * right_im + left_im * right_re),
    )


def conv_forward_body(
    own_block, table, window, kernel, gate_out, bias, causal, back, carried, mixer, out, spectra, total
):
    blocks = spectra.shape[0]
    width = out.shape[1]
    origin = table[2]

    def segment(n, _):
        begin = table[3 + n] - origin
        end = table[4 + n] - origin
        head = lax.div(begin, BLK)
        tail = jnp.minimum(lax.div(end - 1, BLK), blocks - 1)

        def transform(j, _):
            at = pl.multiple_of(j * BLK, BLK)
            mask = rows_mask(at - BLK, 2 * BLK, begin, end)
            spectra[j] = masked_spectrum(causal[...], window[pl.ds(at, 2 * BLK), :], mask)
            return 0

        lax.fori_loop(head, tail + 1, transform, 0)

        def produce(j, _):
            reach = jnp.minimum(j - head, TAPS - 1) + 1
            for lane in range(0, width, 128):
                part = slice(lane, lane + 128)

                def lag(b, carry):
                    return multiply_add(
                        carry,
                        kernel[b, :BLK, part],
                        kernel[b, BLK:, part],
                        spectra[j - b, :BLK, part],
                        spectra[j - b, BLK:, part],
                        False,
                    )

                zero = jnp.zeros((BLK, 128), f32)
                re, im = lax.fori_loop(0, reach, lag, (zero, zero))
                total[:BLK, part] = re.astype(bf16)
                total[BLK:, part] = im.astype(bf16)
            value = jnp.dot(back[...], total[...], preferred_element_type=f32)
            at = pl.multiple_of((j - own_block) * BLK, BLK)
            mask = rows_mask(j * BLK, BLK, begin, end)
            out[pl.ds(at, BLK), :] = jnp.where(mask, value, out[pl.ds(at, BLK), :])
            return 0

        lax.fori_loop(jnp.maximum(head, own_block), tail + 1, produce, 0)
        return 0

    lax.fori_loop(table[0], table[1] + 1, segment, 0)
    own = window.shape[0] - out.shape[0]

    def strip(at):
        for part in lanes(width):
            value = out[pl.ds(at, STRIP), part] + bias[0, :, part] * window[
                pl.ds(own + at, STRIP), part
            ].astype(f32)
            carried[pl.ds(at, STRIP), part] = value.astype(bf16)
            mixer[pl.ds(at, STRIP), part] = (
                value * gate_out[pl.ds(at, STRIP), part].astype(f32)
            ).astype(bf16)

    each_strip(out.shape[0], STRIP, strip)


def signal_backward_body(
    own_block, table, grads, kernel, values, gate_in, bias, ahead, back,
    gate_in_grad, values_grad, signal_grad, spectra, total,
):
    blocks = spectra.shape[0]
    own_blocks = signal_grad.shape[0] // BLK
    width = signal_grad.shape[1]
    origin = table[2] + own_block * BLK

    def segment(n, _):
        begin = table[3 + n] - origin
        end = table[4 + n] - origin
        first = lax.div(jnp.maximum(begin, 0), BLK)
        tail = jnp.minimum(lax.div(end - 1, BLK), own_blocks - 1)
        last = jnp.minimum(lax.div(end - 1, BLK), blocks - 1)

        def transform(j, _):
            at = pl.multiple_of(j * BLK, BLK)
            mask = rows_mask(at, 2 * BLK, begin, end)
            spectra[j] = masked_spectrum(ahead[...], grads[pl.ds(at, 2 * BLK), :], mask)
            return 0

        lax.fori_loop(first, last + 1, transform, 0)

        def produce(j, _):
            reach = jnp.minimum(last - j, TAPS - 1) + 1
            for part in lanes(width):

                def lag(b, carry):
                    return multiply_add(
                        carry,
                        kernel[b, :BLK, part],
                        kernel[b, BLK:, part],
                        spectra[j + b, :BLK, part],
                        spectra[j + b, BLK:, part],
                        True,
                    )

                zero = jnp.zeros((BLK, 128), f32)
                re, im = lax.fori_loop(0, reach, lag, (zero, zero))
                total[:BLK, part] = re.astype(bf16)
                total[BLK:, part] = im.astype(bf16)
            value = jnp.dot(back[...], total[...], preferred_element_type=f32)
            at = pl.multiple_of(j * BLK, BLK)
            mask = rows_mask(at, BLK, begin, end)
            signal_grad[pl.ds(at, BLK), :] = jnp.where(
                mask, value, signal_grad[pl.ds(at, BLK), :]
            )
            return 0

        lax.fori_loop(first, tail + 1, produce, 0)
        return 0

    lax.fori_loop(table[0], table[1] + 1, segment, 0)

    def strip(at):
        for part in lanes(width):
            where = (pl.ds(at, STRIP), part)
            value = signal_grad[where] + bias[0, :, part] * grads[where].astype(f32)
            gate_in_grad[where] = (value * values[where].astype(f32)).astype(bf16)
            values_grad[where] = (value * gate_in[where].astype(f32)).astype(bf16)

    each_strip(signal_grad.shape[0], STRIP, strip)


def kernel_backward_body(
    own_block, table, window, grads, causal, single, back, kernel_grad, spectra, own_spectra, sums
):
    blocks = spectra.shape[0]
    width = kernel_grad.shape[1]
    origin = table[2]
    sums[...] = jnp.zeros_like(sums)

    def segment(n, _):
        begin = table[3 + n] - origin
        end = table[4 + n] - origin
        head = lax.div(begin, BLK)
        tail = jnp.minimum(lax.div(end - 1, BLK), blocks - 1)
        first = jnp.maximum(head, own_block)

        def transform(j, _):
            at = pl.multiple_of(j * BLK, BLK)
            mask = rows_mask(at - BLK, 2 * BLK, begin, end)
            spectra[j] = masked_spectrum(causal[...], window[pl.ds(at, 2 * BLK), :], mask)
            return 0

        lax.fori_loop(head, tail + 1, transform, 0)

        def transform_own(j, _):
            at = pl.multiple_of((j - own_block) * BLK, BLK)
            mask = rows_mask(j * BLK, BLK, begin, end)
            own_spectra[j - own_block] = masked_spectrum(
                single[...], grads[pl.ds(at, BLK), :], mask
            )
            return 0

        lax.fori_loop(first, tail + 1, transform_own, 0)

        def accumulate(b, _):
            for part in lanes(width):

                def at_block(j, carry):
                    return multiply_add(
                        carry,
                        spectra[j - b, :BLK, part],
                        spectra[j - b, BLK:, part],
                        own_spectra[j - own_block, :BLK, part],
                        own_spectra[j - own_block, BLK:, part],
                        True,
                    )

                re, im = lax.fori_loop(
                    jnp.maximum(first, head + b),
                    tail + 1,
                    at_block,
                    (sums[b, :BLK, part], sums[b, BLK:, part]),
                )
                sums[b, :BLK, part] = re
                sums[b, BLK:, part] = im
            return 0

        lax.fori_loop(0, jnp.minimum(tail - head, TAPS - 1) + 1, accumulate, 0)
        return 0

    lax.fori_loop(table[0], table[1] + 1, segment, 0)
    for b in range(TAPS):
        kernel_grad[b * BLK : (b + 1) * BLK, :] = jnp.dot(
            back[...], sums[b].astype(bf16), preferred_element_type=f32
        )


def norm_rows(values):
    centered = values - jnp.mean(values, -1, keepdims=True)
    rate = lax.rsqrt(jnp.mean(centered * centered, -1, keepdims=True) + epsilon)
    return centered * rate, rate


def norm_rows_back(grad, scaled, rate, gain):
    g = grad * gain
    return rate * (
        g - jnp.mean(g, -1, keepdims=True) - scaled * jnp.mean(g * scaled, -1, keepdims=True)
    )


def fold(values):
    return jnp.sum(values.reshape(values.shape[0] // 8, 8, values.shape[1]), axis=0)


def lanes(count):
    return [slice(q, q + 128) for q in range(0, count, 128)]


def dot(left, right):
    return jnp.dot(left, right, preferred_element_type=f32)


def dot_rows(left, right):
    return lax.dot_general(left, right, (((1,), (1,)), ((), ())), preferred_element_type=f32)


def each_strip(rows, step, body, copies=1):
    while rows % (step * copies):
        copies //= 2

    def run(c, _):
        for k in range(copies):
            body(pl.multiple_of((c * copies + k) * step, step))
        return 0

    lax.fori_loop(0, rows // (step * copies), run, 0)


def sum_strips(rows, step, body, zeros, copies=1):
    while rows % (step * copies):
        copies //= 2

    def run(c, totals):
        for k in range(copies):
            parts = body(pl.multiple_of((c * copies + k) * step, step))
            totals = tuple(total + part for total, part in zip(totals, parts))
        return totals

    return lax.fori_loop(0, rows // (step * copies), run, zeros)


def turn_into(target, chunk, at, order):
    turned = chunk.astype(bf16).T
    for first, size, place in order:
        target[pl.ds(place, size), at : at + chunk.shape[0]] = turned[first : first + size, :]


def in_forward_body(
    state, halo, norm, weight, bias, taps, age, normed, projected, gate_out, gate_in, values,
    signal, low, wide,
):
    rows = state.shape[0]

    @pl.when(pl.program_id(0) == 0)
    def _():
        gain, shift = norm[0:1, :], norm[1:2, :]
        low[:HALO, :] = (norm_rows(halo[...].astype(f32))[0] * gain + shift).astype(bf16)

        def strip(at):
            part = norm_rows(state[pl.ds(at, 32), :].astype(f32))[0] * gain + shift
            low[pl.ds(at + HALO, 32), :] = part.astype(bf16)
            normed[pl.ds(at, 32), :] = part.astype(bf16)

        each_strip(rows, 32, strip, 4)

    chunk = max(c for c in range(16, 273, 16) if (rows + HALO) % c == 0)

    def product(at):
        wide[pl.ds(at, chunk), :] = (
            dot(low[pl.ds(at, chunk), :], weight[0, :, : 3 * LANES]) + bias[0]
        )

    each_strip(rows + HALO, chunk, product)
    for part in range(3):
        projected[part, :HALO, :] = wide[:HALO, part * LANES : (part + 1) * LANES].astype(bf16)

    def strip(at):
        old = age[pl.ds(at, STRIP), :]
        for lane in lanes(LANES):
            mixed = []
            for part in range(3):
                cols = slice(part * LANES + lane.start, part * LANES + lane.stop)
                block = wide[pl.ds(at + HALO - 8, STRIP + 8), cols]
                now, once, twice = block[8:], block[7:-1], block[6:-2]
                projected[part, pl.ds(at + HALO, STRIP), lane] = now.astype(bf16)
                mixed.append(
                    taps[0, 0:1, cols] * now
                    + jnp.where(old >= 1, taps[0, 1:2, cols] * once, 0.0)
                    + jnp.where(old >= 2, taps[0, 2:3, cols] * twice, 0.0)
                )
            gate_out[pl.ds(at, STRIP), lane] = mixed[0].astype(bf16)
            gate_in[pl.ds(at, STRIP), lane] = mixed[1].astype(bf16)
            values[pl.ds(at, STRIP), lane] = mixed[2].astype(bf16)
            signal[pl.ds(at, STRIP), lane] = (mixed[1] * mixed[2]).astype(bf16)

    each_strip(rows, STRIP, strip)


def ff_forward_body(
    out_blocks, mixer, state, norm, shifts, weight, bias, *refs
):
    outs = refs[:out_blocks]
    middle, second, activated, slope, result, result_low, hidden = refs[out_blocks:]
    rows = state.shape[0]
    chunk = min(256, rows)

    @pl.when(pl.program_id(0) == 0)
    def _():
        def product(at):
            total = state[pl.ds(at, chunk), :].astype(f32) + shifts[0:1, :]
            for n, out in enumerate(outs):
                total += dot_rows(
                    mixer[pl.ds(at, chunk), n * LANES : (n + 1) * LANES], out[0]
                )
            middle[pl.ds(at, chunk), :] = total

        each_strip(rows, chunk, product)

        def strip(at):
            part = middle[pl.ds(at, 32), :]
            result[pl.ds(at, 32), :] = part + shifts[1:2, :]
            second[pl.ds(at, 32), :] = (
                norm_rows(part)[0] * norm[0:1, :] + norm[1:2, :]
            ).astype(bf16)

        each_strip(rows, 32, strip, 4)

    def product(at):
        hidden[...] = dot(second[pl.ds(at, chunk), :], weight[0, :, :HIDDEN]) + bias[0]

        def strip(inner):
            for lane in lanes(HIDDEN):
                before = hidden[pl.ds(inner, STRIP), lane]
                cumulative = 0.5 + 0.5 * lax.erf(before * math.sqrt(0.5))
                bell = jnp.exp(-0.5 * before * before) * (1.0 / math.sqrt(2 * math.pi))
                activated[pl.ds(at + inner, STRIP), lane] = (before * cumulative).astype(bf16)
                slope[pl.ds(at + inner, STRIP), lane] = (cumulative + before * bell).astype(bf16)

        each_strip(chunk, STRIP, strip)
        result[pl.ds(at, chunk), :] += dot_rows(
            activated[pl.ds(at, chunk), :], weight[0, :, HIDDEN:]
        )

    each_strip(rows, chunk, product)

    @pl.when(pl.program_id(0) == pl.num_programs(0) - 1)
    def _():
        def strip(at):
            result_low[pl.ds(at, STRIP), :] = result[pl.ds(at, STRIP), :].astype(bf16)

        each_strip(rows, STRIP, strip, 2)


def row_order(split, mine, size):
    if not split:
        return [(0, D, 0)]
    runs = []
    for run in range(D // size):
        slot = (run % 2) ^ mine
        place = pl.multiple_of(slot * (D // 2) + run // 2 * size, 16)
        runs.append((run * size, size, place))
    return runs


def ff_backward_body(
    split, place, grad, second, middle, norm, activated, slope, weight,
    middle_grad, middle_low, weight_grad, bias_grad, sums,
    grad_low, grad_turned, second_turned, hidden, hidden_low,
):
    rows = grad.shape[0]
    chunk = min(256, rows)
    order = row_order(split, place[0], 0 if not split else split)

    @pl.when(pl.program_id(0) == 0)
    def _():
        for at in range(0, rows, chunk):
            turn_into(grad_turned, grad[at : at + chunk, :], at, order)
            turn_into(second_turned, second[at : at + chunk, :], at, order)

        def strip(at):
            grad_low[pl.ds(at, 32), :] = grad[pl.ds(at, 32), :].astype(bf16)
            middle_grad[pl.ds(at, 32), :] = jnp.zeros((32, D), f32)

        each_strip(rows, 32, strip, 4)
        sums[...] = jnp.zeros_like(sums)
    bias_grad[...] = jnp.zeros_like(bias_grad)

    def product(at):
        hidden[...] = dot(grad_low[pl.ds(at, chunk), :], weight[0, :, HIDDEN:])

        def strip(inner):
            totals = []
            for lane in lanes(HIDDEN):
                part = hidden[pl.ds(inner, STRIP), lane] * slope[
                    pl.ds(at + inner, STRIP), lane
                ].astype(f32)
                hidden_low[pl.ds(at + inner, STRIP), lane] = part.astype(bf16)
                totals.append(fold(part))
            return totals

        zero = jnp.zeros((8, 128), f32)
        totals = sum_strips(chunk, STRIP, strip, (zero,) * (HIDDEN // 128))
        for lane, total in zip(lanes(HIDDEN), totals):
            bias_grad[0, :, lane] += jnp.sum(total, axis=0, keepdims=True)
        middle_grad[pl.ds(at, chunk), :] += dot_rows(
            hidden_low[pl.ds(at, chunk), :], weight[0, :, :HIDDEN]
        )

    each_strip(rows, chunk, product)

    def product_weight(at):
        weight_grad[0, pl.ds(at, 256), :HIDDEN] = dot(
            second_turned[pl.ds(at, 256), :], hidden_low[...]
        ).astype(bf16)
        weight_grad[0, pl.ds(at, 256), HIDDEN:] = dot(
            grad_turned[pl.ds(at, 256), :], activated[...]
        ).astype(bf16)

    each_strip(D, 256, product_weight)

    @pl.when(pl.program_id(0) == pl.num_programs(0) - 1)
    def _():
        def strip(at):
            above = grad[pl.ds(at, 16), :].astype(f32)
            inner = middle_grad[pl.ds(at, 16), :]
            scaled, rate = norm_rows(middle[pl.ds(at, 16), :])
            total = above + norm_rows_back(inner, scaled, rate, norm[0:1, :])
            middle_grad[pl.ds(at, 16), :] = total
            middle_low[pl.ds(at, 16), :] = total.astype(bf16)
            for k, part in enumerate((above, inner * scaled, inner, total)):
                sums[k] += fold(part)

        each_strip(rows, 16, strip, 4)


def gates_backward_body(
    middle_low, weight, gate_out, carried, signal, carried_grad, gate_grad, bias_grad, product_ref
):
    rows = middle_low.shape[0]
    chunk = min(256, rows)
    bias_grad[...] = jnp.zeros_like(bias_grad)

    def product(at):
        product_ref[...] = dot(middle_low[pl.ds(at, chunk), :], weight[0])

        def strip(inner):
            totals = []
            for lane in lanes(LANES):
                part = product_ref[pl.ds(inner, STRIP), lane]
                where = (pl.ds(at + inner, STRIP), lane)
                grown = part * gate_out[where].astype(f32)
                carried_grad[where] = grown.astype(bf16)
                gate_grad[where] = (part * carried[where].astype(f32)).astype(bf16)
                totals.append(fold(grown * signal[where].astype(f32)))
            return totals

        zero = jnp.zeros((8, 128), f32)
        totals = sum_strips(chunk, STRIP, strip, (zero,) * (LANES // 128))
        for lane, total in zip(lanes(LANES), totals):
            bias_grad[0, :, lane] += jnp.sum(total, axis=0, keepdims=True)

    each_strip(rows, chunk, product)


def in_backward_body(
    split, place, first_grad, second_grad, third_grad, halo, age, projected, taps, normed,
    middle_low, mixer, weight, state, middle_grad, norm,
    grad, grad_out, weight_grad, bias_grad, taps_grad, sums,
    normed_turned, middle_turned, spread, low,
):
    rows = normed.shape[0]
    chunk = min(256, rows)
    order = row_order(split, place[0], 0 if not split else split)

    @pl.when(pl.program_id(0) == 0)
    def _():
        for at in range(0, rows, chunk):
            turn_into(normed_turned, normed[at : at + chunk, :], at, order)
            turn_into(middle_turned, middle_low[at : at + chunk, :], at, order)
        sums[...] = jnp.zeros_like(sums)

        def strip(at):
            grad[pl.ds(at, 32), :] = jnp.zeros((32, D), f32)

        each_strip(rows, 32, strip, 4)

    for part, ref in enumerate((first_grad, second_grad, third_grad)):
        cols = slice(part * LANES, (part + 1) * LANES)

        def strip(at):
            spread[pl.ds(at, STRIP), cols] = ref[pl.ds(at, STRIP), :]

        each_strip(rows, STRIP, strip)
        spread[rows:, cols] = halo[part]

    for part in range(3):

        def strip(at):
            old = age[pl.ds(at, STRIP + HALO), :]
            mine, after_one, after_two = old[:STRIP], old[1 : STRIP + 1], old[2 : STRIP + 2]
            totals = []
            for lane in lanes(LANES):
                cols = slice(part * LANES + lane.start, part * LANES + lane.stop)
                block = spread[pl.ds(at, STRIP + HALO), cols].astype(f32)
                source = projected[part, pl.ds(at, STRIP + HALO), lane].astype(f32)
                now = block[:STRIP]
                total = (
                    taps[0, 0:1, cols] * now
                    + jnp.where(after_one >= 1, taps[0, 1:2, cols] * block[1 : STRIP + 1], 0.0)
                    + jnp.where(after_two >= 2, taps[0, 2:3, cols] * block[2 : STRIP + 2], 0.0)
                )
                low[pl.ds(at, STRIP), cols] = total.astype(bf16)
                totals += [
                    fold(now * source[HALO:]),
                    fold(jnp.where(mine >= 1, now * source[HALO - 1 : -1], 0.0)),
                    fold(jnp.where(mine >= 2, now * source[HALO - 2 : -2], 0.0)),
                    fold(total),
                ]
            return totals

        zero = jnp.zeros((8, 128), f32)
        totals = sum_strips(rows, STRIP, strip, (zero,) * (4 * LANES // 128))
        for q, lane in enumerate(lanes(LANES)):
            cols = slice(part * LANES + lane.start, part * LANES + lane.stop)
            for tap in range(3):
                taps_grad[0, tap : tap + 1, cols] = jnp.sum(
                    totals[4 * q + tap], axis=0, keepdims=True
                )
            bias_grad[0, :, cols] = jnp.sum(totals[4 * q + 3], axis=0, keepdims=True)

    def product(at):
        grad[pl.ds(at, chunk), :] += dot_rows(
            low[pl.ds(at, chunk), :], weight[0, :, : 3 * LANES]
        )

    each_strip(rows, chunk, product)

    def product_weight(at):
        weight_grad[0, pl.ds(at, 256), : 3 * LANES] = dot(
            normed_turned[pl.ds(at, 256), :], low[...]
        ).astype(bf16)
        weight_grad[0, pl.ds(at, 256), 3 * LANES :] = dot(
            middle_turned[pl.ds(at, 256), :], mixer[...]
        ).astype(bf16)

    each_strip(D, 256, product_weight)

    @pl.when(pl.program_id(0) == pl.num_programs(0) - 1)
    def _():
        def strip(at):
            inner = grad[pl.ds(at, 16), :]
            scaled, rate = norm_rows(state[pl.ds(at, 16), :].astype(f32))
            total = middle_grad[pl.ds(at, 16), :] + norm_rows_back(
                inner, scaled, rate, norm[0:1, :]
            )
            grad[pl.ds(at, 16), :] = total
            grad_out[pl.ds(at, 16), :] = total.astype(bf16)
            for k, part in enumerate((inner * scaled, inner)):
                sums[k] += fold(part)

        each_strip(rows, 16, strip, 4)


def whole(shape):
    return pl.BlockSpec(
        shape, lambda i, *_: (0,) * len(shape), pipeline_mode=pl.Buffered(1)
    )


def by_lane(shape):
    return pl.BlockSpec(shape, lambda i, *_: (0,) * (len(shape) - 1) + (i,))


def by_first(shape):
    return pl.BlockSpec(shape, lambda i, *_: (i,) + (0,) * (len(shape) - 1))


def weight_block(wide, per, first=0, stride=1):
    return pl.BlockSpec(
        (1, D, wide), lambda i, *_: (i // per, 0, first + stride * (i % per))
    )


def run(body, name, grid, scalars, ins, outs, scratch, flops, moved, limit=48):
    arrays, in_specs = zip(*ins)
    shapes, out_specs = zip(*outs)
    return pl.pallas_call(
        body,
        out_shape=shapes,
        grid_spec=pltpu.PrefetchScalarGridSpec(
            num_scalar_prefetch=len(scalars),
            grid=(grid,),
            in_specs=in_specs,
            out_specs=out_specs,
            scratch_shapes=scratch,
        ),
        compiler_params=pltpu.CompilerParams(vmem_limit_bytes=limit << 20),
        cost_estimate=pl.CostEstimate(flops=flops, bytes_accessed=moved, transcendentals=0),
        name=name,
    )(*scalars, *arrays)


def shape_of(dims, kind):
    return jax.ShapeDtypeStruct(dims, kind)


def in_forward(state, halo, norm, weights, first, per, bias, taps, age):
    rows = state.shape[0]
    blocks = D // LANES
    low = (shape_of((rows, D), bf16), by_lane((rows, LANES)))
    return run(
        in_forward_body, "in_forward", blocks, (),
        [
            (state, whole((rows, D))), (halo, whole((HALO, D))), (norm, whole((2, D))),
            (weights, weight_block(4 * LANES, per, first)),
            (bias, by_first((1, 1, 3 * LANES))), (taps, by_first((1, 3, 3 * LANES))),
            (age, whole(age.shape)),
        ],
        [
            (shape_of((rows, D), bf16), whole((rows, D))),
            (shape_of((3, rows + HALO, D), bf16), by_lane((3, rows + HALO, LANES))),
            low, low, low, low,
        ],
        [pltpu.VMEM((rows + HALO, D), bf16), pltpu.VMEM((rows + HALO, 3 * LANES), f32)],
        2 * rows * D * 3 * D, 20_000_000, 30,
    )


def ff_forward(mixer, state, norm, shifts, weights, per, hidden_per, bias, mix, first):
    rows = state.shape[0]
    hidden_blocks = FF // HIDDEN
    row = (rows, D)
    tall = (shape_of((rows, FF), bf16), by_lane((rows, HIDDEN)))
    out_specs = [
        pl.BlockSpec(
            (1, D, LANES), lambda i, *_, n=n: (n // per, 0, 4 * (first + n % per) + 3)
        )
        for n in range(D // LANES)
    ]
    return run(
        functools.partial(ff_forward_body, D // LANES), "ff_forward", hidden_blocks, (),
        [
            (mixer, whole(row)), (state, whole(row)), (norm, whole((2, D))),
            (shifts, whole((2, D))),
            (weights, weight_block(2 * HIDDEN, hidden_per)),
            (bias, by_first((1, 1, HIDDEN))),
        ]
        + [(mix, spec) for spec in out_specs],
        [
            (shape_of(row, f32), whole(row)), (shape_of(row, bf16), whole(row)), tall, tall,
            (shape_of(row, f32), whole(row)), (shape_of(row, bf16), whole(row)),
        ],
        [pltpu.VMEM((min(256, rows), HIDDEN), f32)],
        2 * rows * D * (2 * FF + D), 40_000_000, 32,
    )


def ff_backward(split, place, grad, second, middle, norm, activated, slope, weights, hidden_per):
    rows = grad.shape[0]
    row = (rows, D)
    halves = weights.shape[0]
    hidden_blocks = FF // HIDDEN
    grads = shape_of((halves, D, 2 * FF // halves), bf16)
    return run(
        functools.partial(ff_backward_body, split), "ff_backward", hidden_blocks, (place,),
        [
            (grad, whole(row)), (second, whole(row)), (middle, whole(row)), (norm, whole((2, D))),
            (activated, by_lane((rows, HIDDEN))), (slope, by_lane((rows, HIDDEN))),
            (weights, weight_block(2 * HIDDEN, hidden_per)),
        ],
        [
            (shape_of(row, f32), whole(row)), (shape_of(row, bf16), whole(row)),
            (grads, weight_block(2 * HIDDEN, hidden_per)),
            (shape_of((hidden_blocks, 1, HIDDEN), f32), by_first((1, 1, HIDDEN))),
            (shape_of((4, 8, D), f32), whole((4, 8, D))),
        ],
        [
            pltpu.VMEM(row, bf16), pltpu.VMEM((D, rows), bf16), pltpu.VMEM((D, rows), bf16),
            pltpu.VMEM((min(256, rows), HIDDEN), f32), pltpu.VMEM((rows, HIDDEN), bf16),
        ],
        8 * rows * D * FF, 50_000_000, 40,
    )


def gates_backward(middle_low, weights, first, per, gate_out, carried, signal):
    rows = middle_low.shape[0]
    block = (rows, LANES)
    low = (shape_of((rows, D), bf16), by_lane(block))
    return run(
        gates_backward_body, "gates_backward", D // LANES, (),
        [
            (middle_low, whole((rows, D))), (weights, weight_block(LANES, per, 4 * first + 3, 4)),
            (gate_out, by_lane(block)), (carried, by_lane(block)), (signal, by_lane(block)),
        ],
        [
            low, low,
            (shape_of((D // LANES, 1, LANES), f32), by_first((1, 1, LANES))),
        ],
        [pltpu.VMEM((min(256, rows), LANES), f32)],
        2 * rows * D * D, 10_000_000, 20,
    )


def in_backward(
    split, place, mixed_grads, halo, age, projected, taps, normed, middle_low, mixer, weights,
    first, per, state, middle_grad, norm,
):
    rows = normed.shape[0]
    row, block = (rows, D), (rows, LANES)
    blocks = D // LANES
    grads = shape_of((weights.shape[0], D, 4 * per * LANES), bf16)
    return run(
        functools.partial(in_backward_body, split), "in_backward", blocks, (place,),
        [(part, by_lane(block)) for part in mixed_grads]
        + [
            (halo, by_lane((3, HALO, LANES))), (age, whole(age.shape)),
            (projected, by_lane((3, rows + HALO, LANES))), (taps, by_first((1, 3, 3 * LANES))),
            (normed, whole(row)), (middle_low, whole(row)), (mixer, by_lane(block)),
            (weights, weight_block(4 * LANES, per, first)), (state, whole(row)),
            (middle_grad, whole(row)), (norm, whole((2, D))),
        ],
        [
            (shape_of(row, f32), whole(row)), (shape_of(row, bf16), whole(row)),
            (grads, weight_block(4 * LANES, per)),
            (shape_of((blocks, 1, 3 * LANES), f32), by_first((1, 1, 3 * LANES))),
            (shape_of((blocks, 3, 3 * LANES), f32), by_first((1, 3, 3 * LANES))),
            (shape_of((2, 8, D), f32), whole((2, 8, D))),
        ],
        [
            pltpu.VMEM((D, rows), bf16), pltpu.VMEM((D, rows), bf16),
            pltpu.VMEM((rows + HALO, 3 * LANES), bf16), pltpu.VMEM((rows, 3 * LANES), bf16),
        ],
        2 * rows * D * 7 * D, 40_000_000, 46,
    )


def conv_forward(table, window, kernel, gate_out, bias, rows, tables):
    causal, _, _, back = tables
    wide = window.shape[0]
    blocks = wide // BLK - 1
    own_block = (wide - BLK - rows) // BLK
    low = (shape_of((rows, D), bf16), by_lane((rows, LANES)))
    return run(
        functools.partial(conv_forward_body, own_block), "conv_forward", D // LANES, (table,),
        [
            (window, by_lane((wide, LANES))), (kernel, by_lane((TAPS, 2 * BLK, LANES))),
            (gate_out, by_lane((rows, LANES))), (bias, by_first((1, 1, LANES))),
            (causal, whole((2 * BLK, 2 * BLK))), (back, whole((BLK, 2 * BLK))),
        ],
        [low, low],
        [
            pltpu.VMEM((rows, LANES), f32),
            pltpu.VMEM((blocks, 2 * BLK, LANES), f32),
            pltpu.VMEM((2 * BLK, LANES), bf16),
        ],
        20_000_000_000, 20_000_000, 28,
    )


def signal_backward(table, grads, kernel, values, gate_in, bias, rows, hops, tables):
    _, ahead, _, back = tables
    wide = grads.shape[0]
    low = (shape_of((rows, D), bf16), by_lane((rows, LANES)))
    return run(
        functools.partial(signal_backward_body, hops * rows // BLK), "signal_backward",
        D // LANES, (table,),
        [
            (grads, by_lane((wide, LANES))),
            (kernel, by_lane((TAPS, 2 * BLK, LANES))), (values, by_lane((rows, LANES))),
            (gate_in, by_lane((rows, LANES))), (bias, by_first((1, 1, LANES))),
            (ahead, whole((2 * BLK, 2 * BLK))), (back, whole((BLK, 2 * BLK))),
        ],
        [low, low],
        [
            pltpu.VMEM((rows, LANES), f32),
            pltpu.VMEM((wide // BLK - 1, 2 * BLK, LANES), f32),
            pltpu.VMEM((2 * BLK, LANES), bf16),
        ],
        20_000_000_000, 20_000_000, 32,
    )


def kernel_backward(table, window, grads, rows, tables):
    causal, _, single, back = tables
    wide = window.shape[0]
    blocks = wide // BLK - 1
    own_block = (wide - BLK - rows) // BLK
    return run(
        functools.partial(kernel_backward_body, own_block), "kernel_backward",
        D // LANES, (table,),
        [
            (window, by_lane((wide, LANES))), (grads, by_lane((rows, LANES))),
            (causal, whole((2 * BLK, 2 * BLK))), (single, whole((2 * BLK, BLK))),
            (back, whole((BLK, 2 * BLK))),
        ],
        [(shape_of((LMAX, D), f32), by_lane((LMAX, LANES)))],
        [
            pltpu.VMEM((blocks, 2 * BLK, LANES), f32),
            pltpu.VMEM((rows // BLK, 2 * BLK, LANES), f32),
            pltpu.VMEM((TAPS, 2 * BLK, LANES), f32),
        ],
        20_000_000_000, 20_000_000, 32,
    )[0]


def shards(
    tokens,
    out_grad,
    seq_lengths,
    deal_order,
    input_weight,
    output_weight,
    up_projection_weight,
    down_projection_weight,
    input_bias,
    short_taps,
    filter_first,
    filter_inner,
    filter_biases,
    filter_rates,
    filter_out,
    conv_bias,
    norm_gains,
    norm_biases,
    output_biases,
    up_projection_bias,
):
    tensor_count = lax.axis_size("tensor")
    chips = lax.axis_size("chip")
    cores = lax.axis_size("core")
    devices = tensor_count * chips * cores
    core = lax.axis_index("core")
    rank = (lax.axis_index("chip") * cores + core) * tensor_count + lax.axis_index("tensor")
    rows = tokens.shape[0]
    width = input_weight.shape[3]
    hidden = up_projection_weight.shape[2]
    depth = input_weight.shape[2]
    count = seq_lengths.shape[0]
    everyone = ("chip", "core", "tensor")
    owners = ("tensor", "chip", "core")
    hops = -(-(LMAX - 1) // rows)
    direct = width % LANES == 0 and hidden % HIDDEN == 0
    per = width // LANES if direct else D // LANES
    hidden_per = hidden // HIDDEN if direct else FF // HIDDEN
    halves = tensor_count if direct else 1
    paired = (
        direct and depth % 16 == 0 and cores == 2 and tensor_count == 2
        and chips > 1 and chips & (chips - 1) == 0
    )
    split = depth if paired else 0
    chip, side = lax.axis_index("chip"), lax.axis_index("tensor")
    plane, row, planes = chip // 2, chip % 2, chips // 2

    def swap(values, mask):
        pairs = [(i, i ^ mask) for i in range(chips * tensor_count)]
        return lax.ppermute(values, ("chip", "tensor"), pairs)

    def swap_core(values):
        return lax.ppermute(values, "core", [(0, 1), (1, 0)])

    def pick(values, index, axis=0):
        return lax.dynamic_index_in_dim(values, index, axis, False)

    def gather_pairs(values):
        n = values.shape[-1]
        parts = jnp.stack([values] + [swap(values, k << 2) for k in range(1, planes)])
        values = jnp.stack([pick(parts, k ^ plane) for k in range(planes)])
        parts = jnp.stack([values] + [swap(values, k) for k in range(1, 4)])
        mine = row * 2 + side
        values = jnp.stack(
            [
                jnp.stack([pick(parts, (2 * r + s) ^ mine) for r in range(2)], axis=1)
                for s in range(2)
            ]
        )
        other = swap_core(values)
        values = jnp.stack(
            [jnp.where(core == 0, values, other), jnp.where(core == 0, other, values)], axis=3
        )
        return values.reshape(2, D, n)

    def scatter_pairs(values):
        half = D // 2
        other = swap_core(values[:, half:])
        total = (values[:, :half].astype(f32) + other.astype(f32)).astype(bf16)
        total = total.reshape(2, planes, 2, depth, -1)

        def block(s, r):
            return pick(pick(total, s), r, 1)

        parts = [swap(block(side ^ (k % 2), row ^ (k // 2)), k) for k in range(1, 4)]
        total = block(side, row).astype(f32)
        for part in parts:
            total += part.astype(f32)
        low = total.astype(bf16)
        parts = [swap(pick(low, plane ^ k), k << 2) for k in range(1, planes)]
        total = pick(total, plane)
        for part in parts:
            total += part.astype(f32)
        return total

    def from_before(values, hop=1):
        return lax.ppermute(values, everyone, [(i, i + hop) for i in range(devices - hop)])

    def from_after(values, hop=1):
        return lax.ppermute(values, everyone, [(i + hop, i) for i in range(devices - hop)])

    def join_columns(ins, out, up, down, mix_blocks, ff_blocks):
        lead = out.shape[:-1]
        mix = jnp.stack(
            [part.reshape(*lead, mix_blocks, -1) for part in (*ins, out)], axis=-2
        ).reshape(*lead, -1)
        ff = jnp.stack(
            [part.reshape(*lead, ff_blocks, -1) for part in (up, down)], axis=-2
        ).reshape(*lead, -1)
        return mix, ff

    def part_columns(mix, ff, mix_blocks, ff_blocks):
        lead = mix.shape[:-1]
        mix = mix.reshape(*lead, mix_blocks, 4, -1)
        ff = ff.reshape(*lead, ff_blocks, 2, -1)
        parts = [mix[..., k, :].reshape(*lead, -1) for k in range(4)]
        return parts[:3], parts[3], *[ff[..., k, :].reshape(*lead, -1) for k in range(2)]

    local_mix = per if direct else 1
    local_ff = hidden_per if direct else 1
    local = []
    for layer in range(LAYERS):
        local.append(
            join_columns(
                [input_weight[layer, k].astype(bf16) for k in range(3)],
                jnp.transpose(output_weight[layer].astype(bf16)),
                up_projection_weight[layer].astype(bf16),
                jnp.transpose(down_projection_weight[layer].astype(bf16)),
                local_mix,
                local_ff,
            )
        )

    def gather(part):
        return lax.all_gather(part, owners, axis=0, tiled=True).reshape(tensor_count, D, -1)

    gathered = []
    if paired:
        shared = gather(jnp.concatenate([local[0][1], local[1][0]], axis=1))
        last = gather(local[1][1])
        gathered.append((gather_pairs(local[0][0]), 0, shared))
        gathered.append((shared, 2 * hidden // (4 * LANES), last))
    else:
        for mix, ff in local:
            mix, ff = gather(mix), gather(ff)
            if not direct:
                ins, out, up, down = part_columns(mix, ff, local_mix, local_ff)

                def full(piece):
                    return jnp.transpose(piece, (1, 0, 2)).reshape(1, D, -1)

                mix, ff = join_columns(
                    [full(k) for k in ins], full(out), full(up), full(down), per, hidden_per
                )
            gathered.append((mix, 0, ff))

    numbers = jnp.arange(count, dtype=jnp.int32)
    match = deal_order[:, None] == numbers[None, :]
    lengths = jnp.sum(jnp.where(match, seq_lengths[:, None], 0), axis=0)
    ends = jnp.sum(jnp.where(numbers[:, None] <= numbers[None, :], lengths[:, None], 0), axis=0)
    starts = ends - lengths
    base = rank * rows
    first_segment = jnp.sum((starts <= base).astype(jnp.int32)) - 1
    last_segment = jnp.sum((starts < base + rows).astype(jnp.int32)) - 1
    table = jnp.concatenate(
        [
            jnp.stack([first_segment, last_segment, base - hops * rows]),
            starts,
            ends[count - 1 :],
        ]
    ).astype(jnp.int32)
    places = base + jnp.arange(rows + HALO, dtype=jnp.int32)
    begun = jnp.max(jnp.where(starts[None, :] <= places[:, None], starts[None, :], 0), axis=1)
    age = jnp.broadcast_to((places - begun)[:, None], (rows + HALO, 128))
    place = core.astype(jnp.int32).reshape(1)

    tables = tuple(jnp.asarray(t, f32).astype(bf16) for t in wave_tables())
    positions = positions_table(LMAX)
    modulation = decay_table(LMAX)
    blank = jnp.zeros((BLK, D), bf16)

    filters = []
    for layer in range(LAYERS):
        inner, filter_back = jax.vjp(
            lambda a, b, c, d: filter_hidden(positions, a, b, c, d),
            filter_first[layer],
            filter_inner[layer],
            filter_biases[layer],
            filter_rates[layer],
        )
        kernel = jnp.dot(inner, filter_out[layer], precision=highest) * modulation
        kernel_spectra = jnp.einsum(
            "kr,brc->bkc",
            tables[2],
            kernel.reshape(TAPS, BLK, D).astype(bf16),
            preferred_element_type=f32,
        )
        filters.append((inner, filter_back, kernel_spectra))

    def by_block(values):
        lead = values.shape[:-2]
        split_up = values.reshape(*lead, 3, D // LANES, LANES)
        return jnp.moveaxis(split_up, -2, 0).reshape(D // LANES, *lead, 3 * LANES)

    def from_block(values):
        lead = values.shape[1:-1]
        split_up = values.reshape(D // LANES, *lead, 3, LANES)
        return jnp.moveaxis(split_up, 0, -2).reshape(*lead, 3, D)

    state = tokens
    kept = []
    outputs = []
    for layer in range(LAYERS):
        mix_weights, first, ff_weights = gathered[layer]
        first_norm = jnp.stack([norm_gains[layer, 0], norm_biases[layer, 0]])
        second_norm = jnp.stack([norm_gains[layer, 1], norm_biases[layer, 1]])
        taps = by_block(short_taps[layer])
        lane_bias = conv_bias[layer].reshape(D // LANES, 1, LANES)
        normed, projected, gate_out, gate_in, values, signal = in_forward(
            state,
            from_before(state[rows - HALO :]),
            first_norm,
            mix_weights,
            first,
            per,
            by_block(input_bias[layer][None]),
            taps,
            age,
        )
        window = jnp.concatenate(
            [blank] + [from_before(signal, hop) for hop in range(hops, 0, -1)] + [signal]
        )
        carried, mixer = conv_forward(
            table, window, filters[layer][2], gate_out, lane_bias, rows, tables
        )
        middle, second, activated, slope, result, result_low = ff_forward(
            mixer, state, second_norm, output_biases[layer], ff_weights, per, hidden_per,
            up_projection_bias[layer].reshape(FF // HIDDEN, 1, HIDDEN), mix_weights, first,
        )
        outputs.append(result_low)
        kept.append(
            (
                state, first_norm, second_norm, taps, lane_bias, normed, projected, gate_out,
                gate_in, values, signal, window, carried, mixer, middle, second, activated, slope,
            )
        )
        state = result

    grad = out_grad
    owned, owned_ff = {}, {}
    small = [None] * LAYERS
    for layer in reversed(range(LAYERS)):
        (
            state, first_norm, second_norm, taps, lane_bias, normed, projected, gate_out,
            gate_in, values, signal, window, carried, mixer, middle, second, activated, slope,
        ) = kept[layer]
        mix_weights, first, ff_weights = gathered[layer]
        inner, filter_back, kernel_spectra = filters[layer]
        middle_grad, middle_low, ff_grad, up_bias_grad, ff_sums = ff_backward(
            0, place, grad, second, middle, second_norm, activated, slope, ff_weights, hidden_per
        )
        carried_grad, gate_grad, conv_bias_grad = gates_backward(
            middle_low, mix_weights, first, per, gate_out, carried, signal
        )
        ahead = [from_after(carried_grad, hop) for hop in range(1, hops + 1)]
        kernel_grad = kernel_backward(table, window, carried_grad, rows, tables)
        shaped = kernel_grad * modulation
        filter_out_grad = jnp.dot(jnp.transpose(inner), shaped, precision=highest)
        inner_grad = jnp.dot(shaped, jnp.transpose(filter_out[layer]), precision=highest)
        filter_grads = filter_back(inner_grad)
        ahead, filter_grads, filter_out_grad, owned = lax.optimization_barrier(
            (ahead, filter_grads, filter_out_grad, owned)
        )
        grads_window = jnp.concatenate([carried_grad] + ahead + [blank])
        gate_in_grad, values_grad = signal_backward(
            table, grads_window, kernel_spectra, values, gate_in, lane_bias, rows, hops, tables
        )
        mixed_grads = (gate_grad, gate_in_grad, values_grad)
        after = from_after(jnp.stack([part[:HALO] for part in mixed_grads]))
        grad, grad_low, mix_grad, in_bias_grad, taps_grad, in_sums = in_backward(
            split, place, mixed_grads, after, age, projected, taps, normed, middle_low, mixer,
            mix_weights, first, per, state, middle_grad, first_norm,
        )

        if not direct:
            ins, out, up, down = part_columns(mix_grad, ff_grad, per, hidden_per)

            def by_owner(piece):
                piece = piece.reshape(D, tensor_count, -1)
                return jnp.transpose(piece, (1, 0, 2))

            mix_grad, ff_grad = join_columns(
                [by_owner(k) for k in ins], by_owner(out), by_owner(up), by_owner(down), 1, 1
            )

        def share(part):
            return lax.psum_scatter(
                part.reshape(tensor_count * D, -1), owners, scatter_dimension=0, tiled=True
            )

        owned[layer] = (scatter_pairs(mix_grad) if paired else share(mix_grad)).astype(f32)
        owned_ff[layer] = share(ff_grad).astype(f32)
        ff_sums = jnp.sum(ff_sums, axis=1)
        in_sums = jnp.sum(in_sums, axis=1)
        small[layer] = (
            from_block(in_bias_grad)[0],
            from_block(taps_grad),
            *filter_grads,
            filter_out_grad,
            conv_bias_grad.reshape(D),
            jnp.stack([in_sums[0], ff_sums[1]]),
            jnp.stack([in_sums[1], ff_sums[2]]),
            jnp.stack([ff_sums[3], ff_sums[0]]),
            up_bias_grad.reshape(FF),
        )

    small_stacked = [
        jnp.stack([small[layer][index] for layer in range(LAYERS)])
        for index in range(len(small[0]))
    ]
    sizes = [part.size for part in small_stacked]
    flat = jnp.concatenate([part.reshape(-1) for part in small_stacked])
    unit = 1024
    padded = -(-flat.shape[0] // unit) * unit
    flat = jnp.pad(flat, (0, padded - flat.shape[0])).reshape(padded // 128, 128)
    step = 1
    while step < devices:
        low = flat.astype(bf16)
        other = lax.ppermute(low, everyone, [(i, i ^ step) for i in range(devices)])
        flat = low.astype(f32) + other.astype(f32)
        step *= 2
    flat = flat.reshape(-1)
    summed = []
    offset = 0
    for part, size in zip(small_stacked, sizes):
        summed.append(flat[offset : offset + size].reshape(part.shape))
        offset += size

    in_owned, out_owned, up_owned, down_owned = [], [], [], []
    for layer in range(LAYERS):
        ins, out, up, down = part_columns(owned[layer], owned_ff[layer], local_mix, local_ff)
        in_owned.append(jnp.stack(ins))
        out_owned.append(jnp.transpose(out))
        up_owned.append(up)
        down_owned.append(jnp.transpose(down))
    return (
        outputs[0],
        outputs[1],
        grad_low,
        jnp.stack(in_owned),
        jnp.stack(out_owned),
        jnp.stack(up_owned),
        jnp.stack(down_owned),
        *summed,
    )


def solution(mesh):
    groups, tensors = mesh.shape["dp"], mesh.shape["tensor"]
    cores = 2 if groups % 2 == 0 else 1
    fine = jax.sharding.Mesh(
        mesh.devices.reshape(groups // cores, cores, tensors), ("chip", "core", "tensor")
    )
    dp = ("chip", "core")
    rows = P(("chip", "core", "tensor"), None)
    weights = (
        P(None, None, dp, "tensor"),
        P(None, "tensor", dp),
        P(None, dp, "tensor"),
        P(None, "tensor", dp),
    )
    return jax.shard_map(
        shards,
        mesh=fine,
        in_specs=(rows, rows, P(), P(), *weights) + (P(),) * 12,
        out_specs=(rows, rows, rows, *weights) + (P(),) * 12,
        check_vma=False,
    )
```

time: 1110 us -> 918 us (0.83)
  Pallas kernels: 113 us -> 402 us
  matrix products: 267 us -> 50.2 us
  local copies, waits for them, and re-layouts: 281 us -> 115 us
  other arithmetic: 173 us -> 36.8 us
  waiting for transfers between devices: 185 us -> 215 us
  starting transfers between devices: 60.9 us -> 72.2 us
    pallas_call x4 -> x16, Pallas kernels: 113 us -> 402 us  [run(): pl.pallas_call(body, out_shape=shapes, grid_spec=pltpu.PrefetchScalarGrid...]
    dot_general x24 -> x0, matrix products: 201 us -> none  [the longest x2 37.3 us: shards(): jnp.dot(grad_low, down_all, preferred_element_type=f32) * slope.astype(f32)]
    ppermute x0 -> x21, waiting for transfers between devices: none -> 106 us  [the longest x18 106 us: swap(): return lax.ppermute(values, ('chip', 'tensor'), pairs)]
    transpose x19 -> x0, local copies, waits for them, and re-layouts: 82.7 us -> none  [the longest x12 55.1 us: whole(): jnp.transpose(piece, (1, 2, 0, 3)).reshape(D, parts * tensor_count * size)]
    all_gather x2, waiting for transfers between devices: 70.1 us -> 0.01 us  [gather(): lax.all_gather(part, owners, axis=0, tiled=True)]
    reshape x11 -> x14, local copies, waits for them, and re-layouts: 71.8 us -> 5.75 us  [the longest x2 3.07 us: part_columns(): ff = ff.reshape(*lead, ff_blocks, 2, -1)]
    concatenate x12 -> x5, other arithmetic: 63.1 us -> 5.65 us  [the longest x2 3.97 us: shards(): grads_window = jnp.concatenate([carried_grad] + ahead + [blank])]
    reduce_sum x12 -> x4, other arithmetic: 48.6 us -> 0.13 us  [the longest x2 0.08 us: shards(): ff_sums = jnp.sum(ff_sums, axis=1)]
  transfers between devices with their start and end apart: 17 -> 38, of which waited for: 9 -> 21; matrix products, arithmetic and copies ran while one was open for 47% -> 14% of each run, Pallas kernels for 5% -> 35%
where the time goes in v2:
time: 918 us; the launch traced here: 910 us
  Pallas kernels  402 us (44%)
  waiting for transfers between devices  215 us (23%)
  local copies, waits for them, and re-layouts  115 us (13%)
  starting transfers between devices  72.2 us (8%)
  matrix products  50.2 us (5%)
  other arithmetic  36.8 us (4%)
  between operations  18.3 us (2%)
    pallas_call x16, Pallas kernels, run(): pl.pallas_call(body, out_shape=shapes, grid_spec=pltpu.PrefetchScalarGrid...  402 us
    ppermute x18, waiting for transfers between devices, swap(): return lax.ppermute(values, ('chip', 'tensor'), pairs)  106 us
    unnamed x364, local copies, waits for them, and re-layouts  76.9 us
    ppermute x4, waiting for transfers between devices, from_before(): lax.ppermute(values, everyone, [(i, i + hop) for i in range(devices - hop)])  55.7 us
    ppermute x18, starting transfers between devices, swap(): return lax.ppermute(values, ('chip', 'tensor'), pairs)  39.2 us
    ppermute x5, waiting for transfers between devices, shards(): other = lax.ppermute(low, everyone, [(i, i ^ step) for i in range(devices)])  30.2 us
    ppermute x4, waiting for transfers between devices, from_after(): lax.ppermute(values, everyone, [(i + hop, i) for i in range(devices - hop)])  23.3 us
    ppermute x4, starting transfers between devices, from_before(): lax.ppermute(values, everyone, [(i, i + hop) for i in range(devices - hop)])  18.5 us
  transfers between devices with their start and end apart: 38, of which 21 were waited for; matrix products, arithmetic and copies ran while one was open for 14% of the time, Pallas kernels for 35%

profile of v2, /device:TPU:0, one launch (start us, length us, event | category | flops | bytes accessed | tf_op | source)
XLA Modules:
  0.0 910.1 jit_solution(17447574701712644609)
XLA Ops:
  14.6 5.1 collective-permute-start.3
  20.3 3.5 collective-permute-start
  26.2 15.4 %collective-permute-done.2 = bf16[48,1536]{1,0:T(8,128)(2,1)S(1)} collective-permute-done((bf16[48,1536]{1,0:T(8,128)(2,1)S(1)}, bf16[48,1536]{1,0:T(8,128)(2,1)S(1)}, u32[]{:S(2)}, u32[]{:S(2)}) %collective-permute-start.2) | collective-permute-done | bytes 147488 | tf_op jit(solution)/shard_map/ppermute | solution.py:954
  42.7 2.4 collective-permute-start.6
  49.6 21.1 %collective-permute-done.6 = bf16[4,48,1536]{2,1,0:T(8,128)(2,1)S(1)} collective-permute-done((bf16[4,48,1536]{2,1,0:T(8,128)(2,1)}, bf16[4,48,1536]{2,1,0:T(8,128)(2,1)S(1)}, u32[]{:S(2)}, u32[]{:S(2)}) %collective-permute-start.6) | collective-permute-done | bytes 589856 | tf_op jit(solution)/shard_map/ppermute | solution.py:954
  70.7 3.7 collective-permute-done.5
  74.5 6.5 collective-permute-done.4
  90.5 14.7 %in_forward.2 = (bf16[1024,768]{1,0:T(8,128)(2,1)S(1)}, bf16[3,1040,768]{2,1,0:T(8,128)(2,1)S(1)}, bf16[1024,768]{1,0:T(8,128)(2,1)S(1)}, bf16[1024,768]{1,0:T(8...) custom-call(bf16[1024,768]{1,0:T(8,128)(2,1)S(1)} %copy-done.42, ...), custom_call_target="tpu_custom_call" | custom-call | flops 3623878656 | bytes 20000000 | tf_op jit(solution)/shard_map/in_forward/pallas_call | solution.py:685
  105.3 2.2 copy-done.63
  108.6 3.9 collective-permute-start.8
  112.5 4.5 multiply_convert_fusion.1
  118.1 29.5 %collective-permute-done.8 = bf16[1024,768]{1,0:T(8,128)(2,1)S(1)} collective-permute-done((bf16[1024,768]{1,0:T(8,128)(2,1)S(1)}, bf16[1024,768]{1,0:T(8,128)(2,1)S(1)}, u32[]{:S(2)}, u32[]{:S(2)}) %collective-permute-start.8) | collective-permute-done | bytes 1572896 | tf_op jit(solution)/shard_map/ppermute | solution.py:1001
  148.7 17.7 %conv_forward.2 = (bf16[1024,768]{1,0:T(8,128)(2,1)S(1)}, bf16[1024,768]{1,0:T(8,128)(2,1)S(1)}) custom-call(s32[52]{0:T(128)S(1)} %concatenate.32.table, bf16[2176,768]{1,0:T(8,128)(2,1)S(1)} %fusion.window, f32[8,256,768]{2,1,0:T(8,128)S(1)} %convolution_bitcast_fusion.1.kernel, bf16[1024,768]{1,0:T(8,128)(2,1)S(1)} %get-tuple-element.91.gate_out, ...), custom_call_target="tpu_custom_call" | custom-call | flops 20000000000 | bytes 20000000 | tf_op jit(solution)/shard_map/conv_forward/pallas_call | solution.py:685
  170.3 2.3 copy-done.3
  175.7 33.7 %ff_forward.2 = (f32[1024,768]{1,0:T(8,128)S(1)}, bf16[1024,768]{1,0:T(8,128)(2,1)S(1)}, bf16[1024,3072]{1,0:T(8,128)(2,1)S(1)}, bf16[1024,3072]{1,0:T(8,128)(2,...) custom-call(bf16[1024,768]{1,0:T(8,128)(2,1)S(1)} %copy-done.73, bf16[1024,768]{1,0:T(8,128)(2,1)S(1)} %copy-done.43, ...), custom_call_target="tpu_custom_call" | custom-call | flops 10871635968 | bytes 40000000 | tf_op jit(solution)/shard_map/ff_forward/pallas_call | solution.py:685
  209.4 2.7 copy-done.71
  215.8 5.6 collective-permute-start.9
  224.6 16.5 %in_forward.3 = (bf16[1024,768]{1,0:T(8,128)(2,1)S(1)}, bf16[3,1040,768]{2,1,0:T(8,128)(2,1)S(1)}, bf16[1024,768]{1,0:T(8,128)(2,1)S(1)}, bf16[1024,768]{1,0:T(8...) custom-call(f32[1024,768]{1,0:T(8,128)S(1)} %get-tuple-element.94.state, ...), custom_call_target="tpu_custom_call" | custom-call | flops 3623878656 | bytes 20000000 | tf_op jit(solution)/shard_map/in_forward/pallas_call | solution.py:685
  241.1 2.3 copy-done.18
  244.5 5.5 collective-permute-start.10
  253.2 4.6 multiply_convert_fusion
  258.8 25.0 %collective-permute-done.10 = bf16[1024,768]{1,0:T(8,128)(2,1)S(1)} collective-permute-done((bf16[1024,768]{1,0:T(8,128)(2,1)S(1)}, bf16[1024,768]{1,0:T(8,128)(2,1)S(1)}, u32[]{:S(2)}, u32[]{:S(2)}) %collective-permute-start.10) | collective-permute-done | bytes 1572896 | tf_op jit(solution)/shard_map/ppermute | solution.py:1001
  284.4 17.7 %conv_forward.3 = (bf16[1024,768]{1,0:T(8,128)(2,1)S(1)}, bf16[1024,768]{1,0:T(8,128)(2,1)S(1)}) custom-call(s32[52]{0:T(128)S(1)} %concatenate.32.table, bf16[2176,768]{1,0:T(8,128)(2,1)S(1)} %fusion.1.window, f32[8,256,768]{2,1,0:T(8,128)S(1)} %convolution_bitcast_fusion.kernel, bf16[1024,768]{1,0:T(8,128)(2,1)S(1)} %get-tuple-element.96.gate_out, ...), custom_call_target="tpu_custom_call" | custom-call | flops 20000000000 | bytes 20000000 | tf_op jit(solution)/shard_map/conv_forward/pallas_call | solution.py:685
  307.6 35.1 %ff_forward.3 = (f32[1024,768]{1,0:T(8,128)S(1)}, bf16[1024,768]{1,0:T(8,128)(2,1)S(1)}, bf16[1024,3072]{1,0:T(8,128)(2,1)S(1)}, bf16[1024,3072]{1,0:T(8,128)(2,...) custom-call(bf16[1024,768]{1,0:T(8,128)(2,1)S(1)} %copy-done.5, f32[1024,768]{1,0:T(8,128)S(1)} %get-tuple-element.94.state, ...), custom_call_target="tpu_custom_call" | custom-call | flops 10871635968 | bytes 40000000 | tf_op jit(solution)/shard_map/ff_forward/pallas_call | solution.py:685
  342.7 2.7 copy-done.50
  345.4 47.8 %ff_backward.2 = (f32[1024,768]{1,0:T(8,128)S(1)}, bf16[1024,768]{1,0:T(8,128)(2,1)S(1)}, bf16[2,768,3072]{2,1,0:T(8,128)(2,1)}, f32[4,1,768]{2,1,0:T(1,128)S(1)}, f32[4,8,768]{2,1,0:T(8,128)S(1)}) custom-call(s32[1]{0:T(128)} %bitcast.87.place, bf16[1024,768]{1,0:T(8,128)(2,1)S(1)} %copy-done.52, bf16[1024,768]{1,0:T(8,128)(2,1)S(1)} %get-tuple-element.99.second, ...), custom_call_target="tpu_custom_call" | custom-call | flops 19327352832 | bytes 50000000 | tf_op jit(solution)/shard_map/ff_backward/pallas_call | solution.py:685
  396.8 5.0 copy-done
  404.7 5.7 gates_backward.2
  414.1 2.1 copy-done.22
  417.1 18.4 %kernel_backward.2 = f32[1024,768]{1,0:T(8,128)S(1)} custom-call(s32[52]{0:T(128)S(1)} %concatenate.32.table, bf16[2176,768]{1,0:T(8,128)(2,1)S(1)} %copy-done.22, bf16[1024,768]{1,0:T(8,128)(2,1)} %get-tuple-element.106.grads, bf16[256,256]{1,0:T(8,128)(2,1)S(1)} %copy-done.58, bf16[256,128]{1,0:T(8,128)(2,1)S(1)} %copy-done.61, bf16[128,256]{1,0:T(8,128)(2,1)S(1)} %copy-done.60), custom_call_target="tpu_custom_call" | custom-call | flops 20000000000 | bytes 20000000 | tf_op jit(solution)/shard_map/kernel_backward/pallas_call | solution.py:685
  435.6 5.3 multiply_reduce_fusion.5
  449.0 5.3 fusion.4
  456.7 18.3 %signal_backward.2 = (bf16[1024,768]{1,0:T(8,128)(2,1)S(1)}, bf16[1024,768]{1,0:T(8,128)(2,1)S(1)}) custom-call(s32[52]{0:T(128)S(1)} %concatenate.32.table, bf16[2176,768]{1,0:T(8,128)(2,1)S(1)} %pad_maximum_fusion.4.grads, f32[8,256,768]{2,1,0:T(8,128)S(1)} %bitcast.416, bf16[1024,768]{1,0:T(8,128)(2,1)S(1)} %copy-done.56, ...), custom_call_target="tpu_custom_call" | custom-call | flops 20000000000 | bytes 20000000 | tf_op jit(solution)/shard_map/signal_backward/pallas_call | solution.py:685
  477.0 14.6 %collective-permute-done.12.halo = bf16[3,16,768]{2,1,0:T(8,128)(2,1)S(1)} collective-permute-done((bf16[3,16,768]{2,1,0:T(8,128)(2,1)S(1)}, bf16[3,16,768]{2,1,0:T(8,128)(2,1)S(1)}, u32[]{:S(2)}, u32[]{:S(2)}) %collective-permute-start.12) | collective-permute-done | bytes 73760 | tf_op jit(solution)/shard_map/ppermute | solution.py:1004
  491.6 43.6 %in_backward.2 = (f32[1024,768]{1,0:T(8,128)}, bf16[1024,768]{1,0:T(8,128)(2,1)}, bf16[2,768,1536]{2,1,0:T(8,128)(2,1)}, f32[2,1,1152]{2,1,0:T(1,128)S(1)}, f32[...) custom-call(s32[1]{0:T(128)} %bitcast.87.place, bf16[1024,768]{1,0:T(8,128)(2,1)S(1)} %copy-done.25, ...), custom_call_target="tpu_custom_call" | custom-call | flops 8455716864 | bytes 40000000 | tf_op jit(solution)/shard_map/in_backward/pallas_call | solution.py:685
  539.4 48.0 %ff_backward.3 = (f32[1024,768]{1,0:T(8,128)S(1)}, bf16[1024,768]{1,0:T(8,128)(2,1)S(1)}, bf16[2,768,3072]{2,1,0:T(8,128)(2,1)}, f32[4,1,768]{2,1,0:T(1,128)S(1)}, f32[4,8,768]{2,1,0:T(8,128)S(1)}) custom-call(s32[1]{0:T(128)} %bitcast.87.place, f32[1024,768]{1,0:T(8,128)S(1)} %copy-done.51, bf16[1024,768]{1,0:T(8,128)(2,1)S(1)} %copy-done.77, ...), custom_call_target="tpu_custom_call" | custom-call | flops 19327352832 | bytes 50000000 | tf_op jit(solution)/shard_map/ff_backward/pallas_call | solution.py:685
  587.4 5.7 gates_backward.3
  596.0 4.0 collective-permute-start.14
  603.8 18.3 %kernel_backward.3 = f32[1024,768]{1,0:T(8,128)S(1)} custom-call(s32[52]{0:T(128)S(1)} %concatenate.32.table, bf16[2176,768]{1,0:T(8,128)(2,1)S(1)} %copy-done.20, bf16[1024,768]{1,0:T(8,128)(2,1)} %get-tuple-element.123.grads, bf16[256,256]{1,0:T(8,128)(2,1)S(1)} %copy-done.59, bf16[256,128]{1,0:T(8,128)(2,1)S(1)} %copy-done.62, bf16[128,256]{1,0:T(8,128)(2,1)S(1)} %copy-done.60), custom_call_target="tpu_custom_call" | custom-call | flops 20000000000 | bytes 20000000 | tf_op jit(solution)/shard_map/kernel_backward/pallas_call | solution.py:685
  628.0 5.5 multiply_reduce_fusion.2
  640.0 3.0 add_convert_fusion.1
  643.2 3.8 collective-permute-start.17
  647.0 2.7 collective-permute-start.16
  653.0 4.3 fusion.8
  657.4 3.3 collective-permute-done.17
  660.7 14.4 %collective-permute-done.16 = bf16[4,48,1536]{2,1,0:T(8,128)(2,1)S(1)} collective-permute-done((bf16[4,48,1536]{2,1,0:T(8,128)(2,1)S(1)}, bf16[4,48,1536]{2,1,0:T(8,128)(2,1)S(1)}, u32[]{:S(2)}, u32[]{:S(2)}) %collective-permute-start.16) | collective-permute-done | bytes 589856 | tf_op jit(solution)/shard_map/ppermute | solution.py:954
  676.0 13.4 %collective-permute-start.20 = (bf16[48,1536]{1,0:T(8,128)(2,1)S(1)}, bf16[48,1536]{1,0:T(8,128)(2,1)S(1)}, u32[]{:S(2)}, u32[]{:S(2)}) collective-permute-start(bf16[48,1536]{1,0:T(8,128)(2,1)S(1)} %get-tuple-element.265), channel_id=1, source_target_pairs={{0,24},{1,25},{4,28},{5,29},{8,16},{9,17},{12,20},{13,21},{16,8},{... | collective-permute-start | bytes 442376 | tf_op jit(solution)/shard_map/ppermute | solution.py:954
  691.3 2.9 collective-permute-done.20
  694.2 21.3 %collective-permute-done.19 = bf16[48,1536]{1,0:T(8,128)(2,1)S(1)} collective-permute-done((bf16[48,1536]{1,0:T(8,128)(2,1)S(1)}, bf16[48,1536]{1,0:T(8,128)(2,1)S(1)}, u32[]{:S(2)}, u32[]{:S(2)}) %collective-permute-start.19) | collective-permute-done | bytes 147488 | tf_op jit(solution)/shard_map/ppermute | solution.py:954
  715.6 2.3 pad_maximum_fusion.3.grads
  718.6 2.9 copy-done.10
  721.5 18.3 %signal_backward.3 = (bf16[1024,768]{1,0:T(8,128)(2,1)S(1)}, bf16[1024,768]{1,0:T(8,128)(2,1)S(1)}) custom-call(s32[52]{0:T(128)S(1)} %concatenate.32.table, bf16[2176,768]{1,0:T(8,128)(2,1)S(1)} %pad_maximum_fusion.3.grads, f32[8,256,768]{2,1,0:T(8,128)S(1)} %copy-done.10, bf16[1024,768]{1,0:T(8,128)(2,1)S(1)} %copy-done.70, ...), custom_call_target="tpu_custom_call" | custom-call | flops 20000000000 | bytes 20000000 | tf_op jit(solution)/shard_map/signal_backward/pallas_call | solution.py:685
  744.2 8.7 collective-permute-done.21.halo
  757.2 42.6 %in_backward.3 = (f32[1024,768]{1,0:T(8,128)}, bf16[1024,768]{1,0:T(8,128)(2,1)}, bf16[2,768,1536]{2,1,0:T(8,128)(2,1)}, f32[2,1,1152]{2,1,0:T(1,128)S(1)}, f32[...) custom-call(s32[1]{0:T(128)} %bitcast.87.place, bf16[1024,768]{1,0:T(8,128)(2,1)S(1)} %copy-done.45, ...), custom_call_target="tpu_custom_call" | custom-call | flops 8455716864 | bytes 40000000 | tf_op jit(solution)/shard_map/in_backward/pallas_call | solution.py:685
  806.5 2.2 collective-permute-start.29
  808.7 7.2 collective-permute-done.29
  816.9 3.3 slice.435
  820.5 9.6 %collective-permute-done.31 = bf16[1216,128]{1,0:T(8,128)(2,1)S(1)} collective-permute-done((bf16[1216,128]{1,0:T(8,128)(2,1)S(1)}, bf16[1216,128]{1,0:T(8,128)(2,1)S(1)}, u32[]{:S(2)}, u32[]{:S(2)}) %collective-permute-start.31) | collective-permute-done | bytes 311328 | tf_op jit(solution)/shard_map/ppermute | solution.py:1233
  832.0 7.3 collective-permute-done.32
  840.6 3.0 add_convert_fusion
  848.4 6.1 collective-permute-done.33
  864.4 7.7 collective-permute-done.24
  872.1 2.7 fusion.112
  883.6 7.3 collective-permute-done.27
  (621 shorter events, 159.7 us)
Async XLA Ops:
  7.2 163.1 %all-gather.3.cloned.1.call-start = ((), (), s32[]{:S(2)}) async-start(), calls=%async_computation.2 | async-start | bytes 14598144 | tf_op jit(solution)/shard_map/all_gather | solution.py:1039
  12.6 293.6 %all-gather.5.cloned.1.call-start = ((), (), s32[]{:S(2)}) async-start(), calls=%async_computation.3 | async-start | bytes 9732096 | tf_op jit(solution)/shard_map/all_gather | solution.py:1039
  14.4 879.7 %reduce-scatter.5.cloned.1.call-start = ((), (), s32[]{:S(2)}) async-start(), calls=%async_computation.5 | async-start | bytes 9732096 | tf_op jit(solution)/shard_map/reduce_scatter | solution.py:1201
  14.6 11.7 %collective-permute-start.3 = (bf16[48,1536]{1,0:T(8,128)(2,1)S(1)}, bf16[48,1536]{1,0:T(8,128)(2,1)S(1)}, u32[]{:S(2)}, u32[]{:S(2)}) collective-permute-start(bf16[48,1536]{1,0:T(8,128)(2,1)S(1)} %bitcast.448), channel_id=1, source_target_pairs={{0,24},{1,25},{4,28},{5,29},{8,16},{9,17},{12,20},{13,21},{16,8},{... | collective-permute-start | bytes 442376 | tf_op jit(solution)/shard_map/ppermute | solution.py:954
  19.7 22.0 %collective-permute-start.2 = (bf16[48,1536]{1,0:T(8,128)(2,1)S(1)}, bf16[48,1536]{1,0:T(8,128)(2,1)S(1)}, u32[]{:S(2)}, u32[]{:S(2)}) collective-permute-start(bf16[48,1536]{1,0:T(8,128)(2,1)S(1)} %bitcast.449), channel_id=1, source_target_pairs={{0,16},{1,17},{4,20},{5,21},{8,24},{9,25},{12,28},{13,29},{16,0},{... | collective-permute-start | bytes 442376 | tf_op jit(solution)/shard_map/ppermute | solution.py:954
  19.7 22.0 %collective-permute-start.1 = (bf16[48,1536]{1,0:T(8,128)(2,1)S(1)}, bf16[48,1536]{1,0:T(8,128)(2,1)S(1)}, u32[]{:S(2)}, u32[]{:S(2)}) collective-permute-start(bf16[48,1536]{1,0:T(8,128)(2,1)S(1)} %bitcast.450), channel_id=1, source_target_pairs={{0,8},{1,9},{4,12},{5,13},{8,0},{9,1},{12,4},{13,5},{16,24},{17,25... | collective-permute-start | bytes 442376 | tf_op jit(solution)/shard_map/ppermute | solution.py:954
  20.3 70.0 %collective-permute-start = (bf16[16,768]{1,0:T(8,128)(2,1)S(1)}, bf16[16,768]{1,0:T(8,128)(2,1)S(1)}, u32[]{:S(2)}, u32[]{:S(2)}) collective-permute-start(bf16[16,768]{1,0:T(8,128)(2,1)S(1)} %slice.374), channel_id=1, source_target_pairs={{0,1},{1,2},{2,3},{3,4},{4,5},{5,6},{6,7},{7,8},{8,9},{9,10},{10,1... | collective-permute-start | bytes 73736 | tf_op jit(solution)/shard_map/ppermute | solution.py:1001
  42.7 28.0 %collective-permute-start.6 = (bf16[4,48,1536]{2,1,0:T(8,128)(2,1)}, bf16[4,48,1536]{2,1,0:T(8,128)(2,1)S(1)}, u32[]{:S(2)}, u32[]{:S(2)}) collective-permute-start(bf16[4,48,1536]{2,1,0:T(8,128)(2,1)} %get-tuple-element.268), channel_id=1, source_target_pairs={{0,5},{1,4},{4,1},{5,0},{8,13},{9,12},{12,9},{13,8},{16,21},{17,20... | collective-permute-start | bytes 1769480 | tf_op jit(solution)/shard_map/ppermute | solution.py:954
  45.1 29.3 %collective-permute-start.5 = (bf16[4,48,1536]{2,1,0:T(8,128)(2,1)}, bf16[4,48,1536]{2,1,0:T(8,128)(2,1)}, u32[]{:S(2)}, u32[]{:S(2)}) collective-permute-start(bf16[4,48,1536]{2,1,0:T(8,128)(2,1)} %get-tuple-element.268), channel_id=1, source_target_pairs={{0,4},{1,5},{4,0},{5,1},{8,12},{9,13},{12,8},{13,9},{16,20},{17,21... | collective-permute-start | bytes 1769480 | tf_op jit(solution)/shard_map/ppermute | solution.py:954
  45.7 35.3 %collective-permute-start.4 = (bf16[4,48,1536]{2,1,0:T(8,128)(2,1)}, bf16[4,48,1536]{2,1,0:T(8,128)(2,1)}, u32[]{:S(2)}, u32[]{:S(2)}) collective-permute-start(bf16[4,48,1536]{2,1,0:T(8,128)(2,1)} %get-tuple-element.268), channel_id=1, source_target_pairs={{0,1},{1,0},{4,5},{5,4},{8,9},{9,8},{12,13},{13,12},{16,17},{17,16... | collective-permute-start | bytes 1769480 | tf_op jit(solution)/shard_map/ppermute | solution.py:954
  48.2 42.3 %copy-start.36 = (f32[2,3,1152]{2,1,0:T(4,128)}, f32[2,3,1152]{2,1,0:T(4,128)S(1)}, u32[]{:S(2)}) copy-start(f32[2,3,1152]{2,1,0:T(4,128)S(1)} %copy.135.taps) | copy-start | bytes 82948
  49.6 40.9 %copy-start.38 = (f32[2,768]{1,0:T(2,128)}, f32[2,768]{1,0:T(2,128)S(1)}, u32[]{:S(2)}) copy-start(f32[2,768]{1,0:T(2,128)S(1)} %pad_maximum_fusion.30.norm) | copy-start | bytes 18436
  83.2 6.3 collective-permute-start.7
  84.0 166.1 %copy-start.116 = (f32[1024]{0:T(1024)}, f32[1024]{0:T(1024)S(1)}, u32[]{:S(2)}) copy-start(f32[1024]{0:T(1024)S(1)} %get-tuple-element.319) | copy-start | bytes 12292
  108.6 39.1 %copy-start.12 = (bf16[1024,768]{1,0:T(8,128)(2,1)}, bf16[1024,768]{1,0:T(8,128)(2,1)S(1)}, u32[]{:S(2)}) copy-start(bf16[1024,768]{1,0:T(8,128)(2,1)S(1)} %get-tuple-element.90.signal) | copy-start | bytes 4718596
  108.6 39.8 %copy-start.31 = (bf16[1024,768]{1,0:T(8,128)(2,1)}, bf16[1024,768]{1,0:T(8,128)(2,1)S(1)}, u32[]{:S(2)}) copy-start(bf16[1024,768]{1,0:T(8,128)(2,1)S(1)} %get-tuple-element.91.gate_out) | copy-start | bytes 4718596
  108.6 39.1 %collective-permute-start.8 = (bf16[1024,768]{1,0:T(8,128)(2,1)S(1)}, bf16[1024,768]{1,0:T(8,128)(2,1)S(1)}, u32[]{:S(2)}, u32[]{:S(2)}) collective-permute-start(bf16[1024,768]{1,0:T(8,128)(2,1)S(1)} %get-tuple-element.90.signal), channel_id=1, source_target_pairs={{0,1},{1,2},{2,3},{3,4},{4,5},{5,6},{6,7},{7,8},{8,9},{9,10},{10,1... | collective-permute-start | bytes 4718600 | tf_op jit(solution)/shard_map/ppermute | solution.py:1001
  215.2 91.0 %copy-start.1 = (f32[1024,768]{1,0:T(8,128)}, f32[1024,768]{1,0:T(8,128)S(1)}, u32[]{:S(2)}) copy-start(f32[1024,768]{1,0:T(8,128)S(1)} %get-tuple-element.94.state) | copy-start | bytes 9437188
  215.8 7.7 collective-permute-start.9
  244.5 39.3 %copy-start.7 = (bf16[1024,768]{1,0:T(8,128)(2,1)}, bf16[1024,768]{1,0:T(8,128)(2,1)S(1)}, u32[]{:S(2)}) copy-start(bf16[1024,768]{1,0:T(8,128)(2,1)S(1)} %get-tuple-element.95.signal) | copy-start | bytes 4718596
  244.5 39.9 %copy-start.27 = (bf16[1024,768]{1,0:T(8,128)(2,1)}, bf16[1024,768]{1,0:T(8,128)(2,1)S(1)}, u32[]{:S(2)}) copy-start(bf16[1024,768]{1,0:T(8,128)(2,1)S(1)} %get-tuple-element.96.gate_out) | copy-start | bytes 4718596
  244.5 39.3 %collective-permute-start.10 = (bf16[1024,768]{1,0:T(8,128)(2,1)S(1)}, bf16[1024,768]{1,0:T(8,128)(2,1)S(1)}, u32[]{:S(2)}, u32[]{:S(2)}) collective-permute-start(bf16[1024,768]{1,0:T(8,128)(2,1)S(1)} %get-tuple-element.95.signal), channel_id=1, source_target_pairs={{0,1},{1,2},{2,3},{3,4},{4,5},{5,6},{6,7},{7,8},{8,9},{9,10},{10,1... | collective-permute-start | bytes 4718600 | tf_op jit(solution)/shard_map/ppermute | solution.py:1001
  307.6 37.8 %copy-start.52 = (bf16[1024,768]{1,0:T(8,128)(2,1)S(1)}, bf16[1024,768]{1,0:T(8,128)(2,1)}, u32[]{:S(2)}) copy-start(bf16[1024,768]{1,0:T(8,128)(2,1)} %grad.1) | copy-start | bytes 4718596
  394.9 502.9 %reduce-scatter.3.cloned.1.call-start = ((), (), s32[]{:S(2)}) async-start(), calls=%async_computation.4 | async-start | bytes 9732096 | tf_op jit(solution)/shard_map/reduce_scatter | solution.py:1201
  411.6 42.8 %collective-permute-start.11 = (bf16[1024,768]{1,0:T(8,128)(2,1)}, bf16[1024,768]{1,0:T(8,128)(2,1)S(1)}, u32[]{:S(2)}, u32[]{:S(2)}) collective-permute-start(bf16[1024,768]{1,0:T(8,128)(2,1)} %get-tuple-element.106.grads), channel_id=1, source_target_pairs={{1,0},{2,1},{3,2},{4,3},{5,4},{6,5},{7,6},{8,7},{9,8},{10,9},{11,1... | collective-permute-start | bytes 4718600 | tf_op jit(solution)/shard_map/ppermute | solution.py:1004
  475.1 16.5 %collective-permute-start.12 = (bf16[3,16,768]{2,1,0:T(8,128)(2,1)S(1)}, bf16[3,16,768]{2,1,0:T(8,128)(2,1)S(1)}, u32[]{:S(2)}, u32[]{:S(2)}) collective-permute-start(bf16[3,16,768]{2,1,0:T(8,128)(2,1)S(1)} %pad_maximum_fusion.20), channel_id=1, source_target_pairs={{1,0},{2,1},{3,2},{4,3},{5,4},{6,5},{7,6},{8,7},{9,8},{10,9},{11,1... | collective-permute-start | bytes 221192 | tf_op jit(solution)/shard_map/ppermute | solution.py:1004
  491.6 43.6 %copy-start.77 = (bf16[1024,768]{1,0:T(8,128)(2,1)S(1)}, bf16[1024,768]{1,0:T(8,128)(2,1)}, u32[]{:S(2)}) copy-start(bf16[1024,768]{1,0:T(8,128)(2,1)} %copy-done.76) | copy-start | bytes 4718596
  535.2 52.2 %slice-start = ((s8[4718592]{0:T(1024)(128)(4,1)}), s8[4194304]{0:T(1024)(128)(4,1)S(1)}, s32[]{:S(2)}) async-start(s8[4718592]{0:T(1024)(128)(4,1)} %bitcast.412), calls=%async_computation.6 | async-start | bytes 8388608
  539.4 48.0 %slice-start.1 = ((s8[4718592]{0:T(1024)(128)(4,1)}), s8[524288]{0:T(1024)(128)(4,1)S(1)}, s32[]{:S(2)}) async-start(s8[4718592]{0:T(1024)(128)(4,1)} %bitcast.412), calls=%async_computation.7 | async-start | bytes 1048576
  539.4 48.0 %copy-start.13 = (bf16[1024,768]{1,0:T(8,128)(2,1)S(1)}, bf16[1024,768]{1,0:T(8,128)(2,1)}, u32[]{:S(2)}) copy-start(bf16[1024,768]{1,0:T(8,128)(2,1)} %copy-done.12) | copy-start | bytes 4718596
  539.4 48.0 %copy-start.32 = (bf16[1024,768]{1,0:T(8,128)(2,1)S(1)}, bf16[1024,768]{1,0:T(8,128)(2,1)}, u32[]{:S(2)}) copy-start(bf16[1024,768]{1,0:T(8,128)(2,1)} %copy-done.31) | copy-start | bytes 4718596
  539.4 48.0 %copy-start.34 = (bf16[1024,768]{1,0:T(8,128)(2,1)S(1)}, bf16[1024,768]{1,0:T(8,128)(2,1)}, u32[]{:S(2)}) copy-start(bf16[1024,768]{1,0:T(8,128)(2,1)} %copy-done.33) | copy-start | bytes 4718596
  593.2 122.4 %collective-permute-start.13 = (bf16[1024,768]{1,0:T(8,128)(2,1)}, bf16[1024,768]{1,0:T(8,128)(2,1)}, u32[]{:S(2)}, u32[]{:S(2)}) collective-permute-start(bf16[1024,768]{1,0:T(8,128)(2,1)} %get-tuple-element.123.grads), channel_id=1, source_target_pairs={{1,0},{2,1},{3,2},{4,3},{5,4},{6,5},{7,6},{8,7},{9,8},{10,9},{11,1... | collective-permute-start | bytes 4718600 | tf_op jit(solution)/shard_map/ppermute | solution.py:1004
  596.0 44.0 %collective-permute-start.14 = (bf16[2,384,1536]{2,1,0:T(8,128)(2,1)}, bf16[2,384,1536]{2,1,0:T(8,128)(2,1)}, u32[]{:S(2)}, u32[]{:S(2)}) collective-permute-start(bf16[2,384,1536]{2,1,0:T(8,128)(2,1)} %slice.430), channel_id=1, source_target_pairs={{0,2},{2,0},{1,3},{3,1},{4,6},{6,4},{5,7},{7,5},{8,10},{10,8},{9,1... | collective-permute-start | bytes 7077896 | tf_op jit(solution)/shard_map/ppermute | solution.py:957
  643.2 17.5 %collective-permute-start.17 = (bf16[4,48,1536]{2,1,0:T(8,128)(2,1)S(1)}, bf16[4,48,1536]{2,1,0:T(8,128)(2,1)S(1)}, u32[]{:S(2)}, u32[]{:S(2)}) collective-permute-start(bf16[4,48,1536]{2,1,0:T(8,128)(2,1)S(1)} %get-tuple-element.250), channel_id=1, source_target_pairs={{0,5},{1,4},{4,1},{5,0},{8,13},{9,12},{12,9},{13,8},{16,21},{17,20... | collective-permute-start | bytes 1769480 | tf_op jit(solution)/shard_map/ppermute | solution.py:954
  647.0 28.1 %collective-permute-start.16 = (bf16[4,48,1536]{2,1,0:T(8,128)(2,1)S(1)}, bf16[4,48,1536]{2,1,0:T(8,128)(2,1)S(1)}, u32[]{:S(2)}, u32[]{:S(2)}) collective-permute-start(bf16[4,48,1536]{2,1,0:T(8,128)(2,1)S(1)} %get-tuple-element.251), channel_id=1, source_target_pairs={{0,4},{1,5},{4,0},{5,1},{8,12},{9,13},{12,8},{13,9},{16,20},{17,21... | collective-permute-start | bytes 1769480 | tf_op jit(solution)/shard_map/ppermute | solution.py:954
  649.7 25.9 %collective-permute-start.15 = (bf16[4,48,1536]{2,1,0:T(8,128)(2,1)S(1)}, bf16[4,48,1536]{2,1,0:T(8,128)(2,1)S(1)}, u32[]{:S(2)}, u32[]{:S(2)}) collective-permute-start(bf16[4,48,1536]{2,1,0:T(8,128)(2,1)S(1)} %get-tuple-element.249), channel_id=1, source_target_pairs={{0,1},{1,0},{4,5},{5,4},{8,9},{9,8},{12,13},{13,12},{16,17},{17,16... | collective-permute-start | bytes 1769480 | tf_op jit(solution)/shard_map/ppermute | solution.py:954
  657.4 58.2 %copy-start.81 = (bf16[128,768]{1,0:T(8,128)(2,1)S(1)}, bf16[128,768]{1,0:T(8,128)(2,1)}, u32[]{:S(2)}) copy-start(bf16[128,768]{1,0:T(8,128)(2,1)} %copy-done.78) | copy-start | bytes 589828
  676.0 18.2 %collective-permute-start.20 = (bf16[48,1536]{1,0:T(8,128)(2,1)S(1)}, bf16[48,1536]{1,0:T(8,128)(2,1)S(1)}, u32[]{:S(2)}, u32[]{:S(2)}) collective-permute-start(bf16[48,1536]{1,0:T(8,128)(2,1)S(1)} %get-tuple-element.265), channel_id=1, source_target_pairs={{0,24},{1,25},{4,28},{5,29},{8,16},{9,17},{12,20},{13,21},{16,8},{... | collective-permute-start | bytes 442376 | tf_op jit(solution)/shard_map/ppermute | solution.py:954
  689.4 26.1 %collective-permute-start.19 = (bf16[48,1536]{1,0:T(8,128)(2,1)S(1)}, bf16[48,1536]{1,0:T(8,128)(2,1)S(1)}, u32[]{:S(2)}, u32[]{:S(2)}) collective-permute-start(bf16[48,1536]{1,0:T(8,128)(2,1)S(1)} %get-tuple-element.266), channel_id=1, source_target_pairs={{0,16},{1,17},{4,20},{5,21},{8,24},{9,25},{12,28},{13,29},{16,0},{... | collective-permute-start | bytes 442376 | tf_op jit(solution)/shard_map/ppermute | solution.py:954
  689.4 26.1 %collective-permute-start.18 = (bf16[48,1536]{1,0:T(8,128)(2,1)S(1)}, bf16[48,1536]{1,0:T(8,128)(2,1)S(1)}, u32[]{:S(2)}, u32[]{:S(2)}) collective-permute-start(bf16[48,1536]{1,0:T(8,128)(2,1)S(1)} %get-tuple-element.264), channel_id=1, source_target_pairs={{0,8},{1,9},{4,12},{5,13},{8,0},{9,1},{12,4},{13,5},{16,24},{17,25... | collective-permute-start | bytes 442376 | tf_op jit(solution)/shard_map/ppermute | solution.py:954
  742.2 10.7 %collective-permute-start.21 = (bf16[3,16,768]{2,1,0:T(8,128)(2,1)S(1)}, bf16[3,16,768]{2,1,0:T(8,128)(2,1)S(1)}, u32[]{:S(2)}, u32[]{:S(2)}) collective-permute-start(bf16[3,16,768]{2,1,0:T(8,128)(2,1)S(1)} %pad_maximum_fusion.21), channel_id=1, source_target_pairs={{1,0},{2,1},{3,2},{4,3},{5,4},{6,5},{7,6},{8,7},{9,8},{10,9},{11,1... | collective-permute-start | bytes 221192 | tf_op jit(solution)/shard_map/ppermute | solution.py:1004
  757.2 42.8 %copy-start.129 = (bf16[2,1,3,384]{3,2,0,1:T(4,128)(2,1)S(1)}, bf16[2,1,3,384]{3,2,0,1:T(4,128)(2,1)}, u32[]{:S(2)}) copy-start(bf16[2,1,3,384]{3,2,0,1:T(4,128)(2,1)} %reshape.522) | copy-start | bytes 13828
  757.2 42.9 %copy-start.120 = (bf16[2,3,3,384]{3,2,0,1:T(4,128)(2,1)S(1)}, bf16[2,3,3,384]{3,2,0,1:T(4,128)(2,1)}, u32[]{:S(2)}) copy-start(bf16[2,3,3,384]{3,2,0,1:T(4,128)(2,1)} %reshape.525) | copy-start | bytes 41476
  757.2 43.0 %copy-start.145 = (bf16[1,768]{1,0:T(2,128)(2,1)S(1)}, bf16[1,768]{1,0:T(2,128)(2,1)}, u32[]{:S(2)}) copy-start(bf16[1,768]{1,0:T(2,128)(2,1)} %get-tuple-element.309) | copy-start | bytes 4612
  757.2 43.1 %copy-start.154 = (bf16[1,2,768]{2,1,0:T(2,128)(2,1)S(1)}, bf16[1,2,768]{2,1,0:T(2,128)(2,1)}, u32[]{:S(2)}) copy-start(bf16[1,2,768]{2,1,0:T(2,128)(2,1)} %maximum_bitcast_fusion.6) | copy-start | bytes 9220
  757.2 43.1 %copy-start.144 = (bf16[1,768]{1,0:T(2,128)(2,1)S(1)}, bf16[1,768]{1,0:T(2,128)(2,1)}, u32[]{:S(2)}) copy-start(bf16[1,768]{1,0:T(2,128)(2,1)} %get-tuple-element.308) | copy-start | bytes 4612
  757.2 43.1 %copy-start.155 = (bf16[1,2,768]{2,1,0:T(2,128)(2,1)S(1)}, bf16[1,2,768]{2,1,0:T(2,128)(2,1)}, u32[]{:S(2)}) copy-start(bf16[1,2,768]{2,1,0:T(2,128)(2,1)} %maximum_bitcast_fusion.8) | copy-start | bytes 9220
  757.2 43.2 %copy-start.91 = (bf16[155008]{0:T(1024)(128)(2,1)S(1)}, bf16[155008]{0:T(1024)(128)(2,1)}, u32[]{:S(2)}) copy-start(bf16[155008]{0:T(1024)(128)(2,1)} %custom-call) | copy-start | bytes 930052
  757.2 47.5 %copy-start.133 = (bf16[1536]{0:T(1024)(128)(2,1)S(1)}, bf16[1536]{0:T(1024)(128)(2,1)}, u32[]{:S(2)}) copy-start(bf16[1536]{0:T(1024)(128)(2,1)} %reshape.532) | copy-start | bytes 9220
  757.2 48.3 %copy-start.128 = (bf16[3072]{0:T(1024)(128)(2,1)S(1)}, bf16[3072]{0:T(1024)(128)(2,1)}, u32[]{:S(2)}) copy-start(bf16[3072]{0:T(1024)(128)(2,1)} %reshape.535) | copy-start | bytes 18436
  757.2 48.6 %copy-start.122 = (bf16[1,24,2,128]{3,1,2,0:T(8,128)(2,1)S(1)}, bf16[1,24,2,128]{3,1,2,0:T(8,128)(2,1)}, u32[]{:S(2)}) copy-start(bf16[1,24,2,128]{3,1,2,0:T(8,128)(2,1)} %copy.188) | copy-start | bytes 36868
  806.5 9.4 %collective-permute-start.29 = (bf16[1216,128]{1,0:T(8,128)(2,1)S(1)}, bf16[1216,128]{1,0:T(8,128)(2,1)S(1)}, u32[]{:S(2)}, u32[]{:S(2)}) collective-permute-start(bf16[1216,128]{1,0:T(8,128)(2,1)S(1)} %pad_bitcast_fusion), channel_id=1, source_target_pairs={{0,1},{1,0},{2,3},{3,2},{4,5},{5,4},{6,7},{7,6},{8,9},{9,8},{10,11... | collective-permute-start | bytes 933896 | tf_op jit(solution)/shard_map/ppermute | solution.py:1233
  815.9 4.2 collective-permute-start.30
  820.1 20.5 %collective-permute-start.22 = (bf16[2,384,1536]{2,1,0:T(8,128)(2,1)}, bf16[2,384,1536]{2,1,0:T(8,128)(2,1)}, u32[]{:S(2)}, u32[]{:S(2)}) collective-permute-start(bf16[2,384,1536]{2,1,0:T(8,128)(2,1)} %slice.435), channel_id=1, source_target_pairs={{0,2},{2,0},{1,3},{3,1},{4,6},{6,4},{5,7},{7,5},{8,10},{10,8},{9,1... | collective-permute-start | bytes 7077896 | tf_op jit(solution)/shard_map/ppermute | solution.py:957
  820.3 9.8 %collective-permute-start.31 = (bf16[1216,128]{1,0:T(8,128)(2,1)S(1)}, bf16[1216,128]{1,0:T(8,128)(2,1)S(1)}, u32[]{:S(2)}, u32[]{:S(2)}) collective-permute-start(bf16[1216,128]{1,0:T(8,128)(2,1)S(1)} %add_convert_fusion.4), channel_id=1, source_target_pairs={{0,4},{1,5},{2,6},{3,7},{4,0},{5,1},{6,2},{7,3},{8,12},{9,13},{10,... | collective-permute-start | bytes 933896 | tf_op jit(solution)/shard_map/ppermute | solution.py:1233
  830.2 9.0 collective-permute-start.32
  839.3 15.1 %collective-permute-start.33 = (bf16[1216,128]{1,0:T(8,128)(2,1)S(1)}, bf16[1216,128]{1,0:T(8,128)(2,1)S(1)}, u32[]{:S(2)}, u32[]{:S(2)}) collective-permute-start(bf16[1216,128]{1,0:T(8,128)(2,1)S(1)} %add_convert_fusion.2), channel_id=1, source_target_pairs={{0,16},{1,17},{2,18},{3,19},{4,20},{5,21},{6,22},{7,23},{8,24},{9,... | collective-permute-start | bytes 933896 | tf_op jit(solution)/shard_map/ppermute | solution.py:1233
  844.9 19.5 %collective-permute-start.25 = (bf16[4,48,1536]{2,1,0:T(8,128)(2,1)}, bf16[4,48,1536]{2,1,0:T(8,128)(2,1)}, u32[]{:S(2)}, u32[]{:S(2)}) collective-permute-start(bf16[4,48,1536]{2,1,0:T(8,128)(2,1)} %get-tuple-element.247), channel_id=1, source_target_pairs={{0,5},{1,4},{4,1},{5,0},{8,13},{9,12},{12,9},{13,8},{16,21},{17,20... | collective-permute-start | bytes 1769480 | tf_op jit(solution)/shard_map/ppermute | solution.py:954
  845.6 26.5 %collective-permute-start.24 = (bf16[4,48,1536]{2,1,0:T(8,128)(2,1)}, bf16[4,48,1536]{2,1,0:T(8,128)(2,1)}, u32[]{:S(2)}, u32[]{:S(2)}) collective-permute-start(bf16[4,48,1536]{2,1,0:T(8,128)(2,1)} %get-tuple-element.248), channel_id=1, source_target_pairs={{0,4},{1,5},{4,0},{5,1},{8,12},{9,13},{12,8},{13,9},{16,20},{17,21... | collective-permute-start | bytes 1769480 | tf_op jit(solution)/shard_map/ppermute | solution.py:954
  847.0 25.1 %collective-permute-start.23 = (bf16[4,48,1536]{2,1,0:T(8,128)(2,1)}, bf16[4,48,1536]{2,1,0:T(8,128)(2,1)}, u32[]{:S(2)}, u32[]{:S(2)}) collective-permute-start(bf16[4,48,1536]{2,1,0:T(8,128)(2,1)} %get-tuple-element.246), channel_id=1, source_target_pairs={{0,1},{1,0},{4,5},{5,4},{8,9},{9,8},{12,13},{13,12},{16,17},{17,16... | collective-permute-start | bytes 1769480 | tf_op jit(solution)/shard_map/ppermute | solution.py:954
  874.9 8.7 collective-permute-start.28
  876.5 14.4 %collective-permute-start.27 = (bf16[48,1536]{1,0:T(8,128)(2,1)S(1)}, bf16[48,1536]{1,0:T(8,128)(2,1)S(1)}, u32[]{:S(2)}, u32[]{:S(2)}) collective-permute-start(bf16[48,1536]{1,0:T(8,128)(2,1)S(1)} %get-tuple-element.263), channel_id=1, source_target_pairs={{0,16},{1,17},{4,20},{5,21},{8,24},{9,25},{12,28},{13,29},{16,0},{... | collective-permute-start | bytes 442376 | tf_op jit(solution)/shard_map/ppermute | solution.py:954
  877.8 13.1 %collective-permute-start.26 = (bf16[48,1536]{1,0:T(8,128)(2,1)S(1)}, bf16[48,1536]{1,0:T(8,128)(2,1)S(1)}, u32[]{:S(2)}, u32[]{:S(2)}) collective-permute-start(bf16[48,1536]{1,0:T(8,128)(2,1)S(1)} %get-tuple-element.261), channel_id=1, source_target_pairs={{0,8},{1,9},{4,12},{5,13},{8,0},{9,1},{12,4},{13,5},{16,24},{17,25... | collective-permute-start | bytes 442376 | tf_op jit(solution)/shard_map/ppermute | solution.py:954
  (144 other events, 1647.5 us)
Sparse Core Ops, SparseCore 0:
  12.7 127.2 all-gather.2
  143.5 85.2 all-gather.4
  395.0 145.8 reduce-scatter.4
  626.2 161.6 reduce-scatter.2

commit v3 on v2

--- a/solution.py
+++ b/solution.py
@@ -17,6 +17,9 @@
 BLK = 128
 TAPS = LMAX // BLK
 LANES = 384
+CONV_LANES = 768
+STEP = 1
+GROUP = 16
 HIDDEN = 768
 HALO = 16
 STRIP = 64
@@ -74,23 +77,33 @@
     return jnp.dot(table, kept, preferred_element_type=f32)
 
 
-def multiply_add(carry, left_re, left_im, right_re, right_im, conj):
-    re, im = carry
-    if conj:
-        return (
-            re + (left_re * right_re + left_im * right_im),
-            im + (left_re * right_im - left_im * right_re),
-        )
-    return (
-        re + (left_re * right_re - left_im * right_im),
-        im + (left_re * right_im + left_im * right_re),
-    )
+def groups():
+    return [(slice(f, f + GROUP), slice(BLK + f, BLK + f + GROUP)) for f in range(0, BLK, GROUP)]
+
+
+def no_sums():
+    return tuple(jnp.zeros((GROUP, 128), f32) for _ in range(2 * BLK // GROUP))
+
+
+def multiply_add(carry, left, a, right, b, part, conj):
+    result = []
+    for k, (up, down) in enumerate(groups()):
+        left_re, left_im = left[a, up, part], left[a, down, part]
+        right_re, right_im = right[b, up, part], right[b, down, part]
+        if conj:
+            re = left_re * right_re + left_im * right_im
+            im = left_re * right_im - left_im * right_re
+        else:
+            re = left_re * right_re - left_im * right_im
+            im = left_re * right_im + left_im * right_re
+        result += [carry[2 * k] + re, carry[2 * k + 1] + im]
+    return tuple(result)
 
 
 def conv_forward_body(
     own_block, table, window, kernel, gate_out, bias, causal, back, carried, mixer, out, spectra, total
 ):
-    blocks = spectra.shape[0]
+    blocks = spectra.shape[0] - STEP + 1
     width = out.shape[1]
     origin = table[2]
 
@@ -100,33 +113,35 @@
         head = lax.div(begin, BLK)
         tail = jnp.minimum(lax.div(end - 1, BLK), blocks - 1)
 
+        for k in range(STEP - 1):
+            spectra[head + k] = jnp.zeros(spectra.shape[1:], f32)
+
         def transform(j, _):
             at = pl.multiple_of(j * BLK, BLK)
             mask = rows_mask(at - BLK, 2 * BLK, begin, end)
-            spectra[j] = masked_spectrum(causal[...], window[pl.ds(at, 2 * BLK), :], mask)
+            spectra[j + STEP - 1] = masked_spectrum(
+                causal[...], window[pl.ds(at, 2 * BLK), :], mask
+            )
             return 0
 
         lax.fori_loop(head, tail + 1, transform, 0)
 
         def produce(j, _):
-            reach = jnp.minimum(j - head, TAPS - 1) + 1
+            reach = lax.div(jnp.minimum(j - head, TAPS - 1) + STEP, STEP)
             for lane in range(0, width, 128):
                 part = slice(lane, lane + 128)
 
-                def lag(b, carry):
-                    return multiply_add(
-                        carry,
-                        kernel[b, :BLK, part],
-                        kernel[b, BLK:, part],
-                        spectra[j - b, :BLK, part],
-                        spectra[j - b, BLK:, part],
-                        False,
-                    )
-
-                zero = jnp.zeros((BLK, 128), f32)
-                re, im = lax.fori_loop(0, reach, lag, (zero, zero))
-                total[:BLK, part] = re.astype(bf16)
-                total[BLK:, part] = im.astype(bf16)
+                def lag(c, carry):
+                    for k in range(STEP):
+                        b = c * STEP + k
+                        at = j - b + STEP - 1
+                        carry = multiply_add(carry, kernel, b, spectra, at, part, False)
+                    return carry
+
+                held = lax.fori_loop(0, reach, lag, no_sums())
+                for k, pair in enumerate(groups()):
+                    total[pair[0], part] = held[2 * k].astype(bf16)
+                    total[pair[1], part] = held[2 * k + 1].astype(bf16)
             value = jnp.dot(back[...], total[...], preferred_element_type=f32)
             at = pl.multiple_of((j - own_block) * BLK, BLK)
             mask = rows_mask(j * BLK, BLK, begin, end)
@@ -156,7 +171,7 @@
     own_block, table, grads, kernel, values, gate_in, bias, ahead, back,
     gate_in_grad, values_grad, signal_grad, spectra, total,
 ):
-    blocks = spectra.shape[0]
+    blocks = spectra.shape[0] - STEP + 1
     own_blocks = signal_grad.shape[0] // BLK
     width = signal_grad.shape[1]
     origin = table[2] + own_block * BLK
@@ -175,25 +190,23 @@
             return 0
 
         lax.fori_loop(first, last + 1, transform, 0)
+        for k in range(1, STEP):
+            spectra[last + k] = jnp.zeros(spectra.shape[1:], f32)
 
         def produce(j, _):
-            reach = jnp.minimum(last - j, TAPS - 1) + 1
+            reach = lax.div(jnp.minimum(last - j, TAPS - 1) + STEP, STEP)
             for part in lanes(width):
 
-                def lag(b, carry):
-                    return multiply_add(
-                        carry,
-                        kernel[b, :BLK, part],
-                        kernel[b, BLK:, part],
-                        spectra[j + b, :BLK, part],
-                        spectra[j + b, BLK:, part],
-                        True,
-                    )
-
-                zero = jnp.zeros((BLK, 128), f32)
-                re, im = lax.fori_loop(0, reach, lag, (zero, zero))
-                total[:BLK, part] = re.astype(bf16)
-                total[BLK:, part] = im.astype(bf16)
+                def lag(c, carry):
+                    for k in range(STEP):
+                        b = c * STEP + k
+                        carry = multiply_add(carry, kernel, b, spectra, j + b, part, True)
+                    return carry
+
+                held = lax.fori_loop(0, reach, lag, no_sums())
+                for k, pair in enumerate(groups()):
+                    total[pair[0], part] = held[2 * k].astype(bf16)
+                    total[pair[1], part] = held[2 * k + 1].astype(bf16)
             value = jnp.dot(back[...], total[...], preferred_element_type=f32)
             at = pl.multiple_of(j * BLK, BLK)
             mask = rows_mask(at, BLK, begin, end)
@@ -220,7 +233,7 @@
 def kernel_backward_body(
     own_block, table, window, grads, causal, single, back, kernel_grad, spectra, own_spectra, sums
 ):
-    blocks = spectra.shape[0]
+    blocks = spectra.shape[0] - STEP + 1
     width = kernel_grad.shape[1]
     origin = table[2]
     sums[...] = jnp.zeros_like(sums)
@@ -249,28 +262,28 @@
             return 0
 
         lax.fori_loop(first, tail + 1, transform_own, 0)
+        for k in range(1, STEP):
+            spectra[tail + k] = jnp.zeros(spectra.shape[1:], f32)
+            own_spectra[tail - own_block + k] = jnp.zeros(own_spectra.shape[1:], f32)
 
         def accumulate(b, _):
+            begin_at = jnp.maximum(first, head + b)
             for part in lanes(width):
 
-                def at_block(j, carry):
-                    return multiply_add(
-                        carry,
-                        spectra[j - b, :BLK, part],
-                        spectra[j - b, BLK:, part],
-                        own_spectra[j - own_block, :BLK, part],
-                        own_spectra[j - own_block, BLK:, part],
-                        True,
-                    )
-
-                re, im = lax.fori_loop(
-                    jnp.maximum(first, head + b),
-                    tail + 1,
-                    at_block,
-                    (sums[b, :BLK, part], sums[b, BLK:, part]),
-                )
-                sums[b, :BLK, part] = re
-                sums[b, BLK:, part] = im
+                def at_blocks(c, carry):
+                    for k in range(STEP):
+                        j = begin_at + c * STEP + k
+                        carry = multiply_add(
+                            carry, spectra, j - b, own_spectra, j - own_block, part, True
+                        )
+                    return carry
+
+                held = [sums[b, rows, part] for pair in groups() for rows in pair]
+                count = lax.div(tail - begin_at + STEP, STEP)
+                held = lax.fori_loop(0, count, at_blocks, tuple(held))
+                for k, pair in enumerate(groups()):
+                    sums[b, pair[0], part] = held[2 * k]
+                    sums[b, pair[1], part] = held[2 * k + 1]
             return 0
 
         lax.fori_loop(0, jnp.minimum(tail - head, TAPS - 1) + 1, accumulate, 0)
@@ -343,10 +356,8 @@
         target[pl.ds(place, size), at : at + chunk.shape[0]] = turned[first : first + size, :]
 
 
-def in_forward_body(
-    state, halo, norm, weight, bias, taps, age, normed, projected, gate_out, gate_in, values,
-    signal, low, wide,
-):
+def in_forward_body(state, halo, norm, weight, bias, taps, age, *refs):
+    normed, projected, gate_out, gate_in, values, signal, low, wide = refs
     rows = state.shape[0]
 
     @pl.when(pl.program_id(0) == 0)
@@ -386,9 +397,8 @@
                     + jnp.where(old >= 1, taps[0, 1:2, cols] * once, 0.0)
                     + jnp.where(old >= 2, taps[0, 2:3, cols] * twice, 0.0)
                 )
-            gate_out[pl.ds(at, STRIP), lane] = mixed[0].astype(bf16)
-            gate_in[pl.ds(at, STRIP), lane] = mixed[1].astype(bf16)
-            values[pl.ds(at, STRIP), lane] = mixed[2].astype(bf16)
+            for ref, value in zip((gate_out, gate_in, values), mixed):
+                ref[pl.ds(at, STRIP), lane] = value.astype(bf16)
             signal[pl.ds(at, STRIP), lane] = (mixed[1] * mixed[2]).astype(bf16)
 
     each_strip(rows, STRIP, strip)
@@ -400,7 +410,7 @@
     outs = refs[:out_blocks]
     middle, second, activated, slope, result, result_low, hidden = refs[out_blocks:]
     rows = state.shape[0]
-    chunk = min(256, rows)
+    chunk = min(512, rows)
 
     @pl.when(pl.program_id(0) == 0)
     def _():
@@ -415,13 +425,13 @@
         each_strip(rows, chunk, product)
 
         def strip(at):
-            part = middle[pl.ds(at, 32), :]
-            result[pl.ds(at, 32), :] = part + shifts[1:2, :]
-            second[pl.ds(at, 32), :] = (
+            part = middle[pl.ds(at, 64), :]
+            result[pl.ds(at, 64), :] = part + shifts[1:2, :]
+            second[pl.ds(at, 64), :] = (
                 norm_rows(part)[0] * norm[0:1, :] + norm[1:2, :]
             ).astype(bf16)
 
-        each_strip(rows, 32, strip, 4)
+        each_strip(rows, 64, strip, 2)
 
     def product(at):
         hidden[...] = dot(second[pl.ds(at, chunk), :], weight[0, :, :HIDDEN]) + bias[0]
@@ -461,12 +471,12 @@
 
 
 def ff_backward_body(
-    split, place, grad, second, middle, norm, activated, slope, weight,
-    middle_grad, middle_low, weight_grad, bias_grad, sums,
-    grad_low, grad_turned, second_turned, hidden, hidden_low,
+    split, place, grad, second, middle, norm, activated, slope, weight, *refs
 ):
+    middle_grad, middle_low, weight_grad, bias_grad, sums = refs[-10:-5]
+    grad_low, grad_turned, second_turned, hidden, hidden_low = refs[-5:]
     rows = grad.shape[0]
-    chunk = min(256, rows)
+    chunk = min(512, rows)
     order = row_order(split, place[0], 0 if not split else split)
 
     @pl.when(pl.program_id(0) == 0)
@@ -519,23 +529,23 @@
     @pl.when(pl.program_id(0) == pl.num_programs(0) - 1)
     def _():
         def strip(at):
-            above = grad[pl.ds(at, 16), :].astype(f32)
-            inner = middle_grad[pl.ds(at, 16), :]
-            scaled, rate = norm_rows(middle[pl.ds(at, 16), :])
+            above = grad[pl.ds(at, 128), :].astype(f32)
+            inner = middle_grad[pl.ds(at, 128), :]
+            scaled, rate = norm_rows(middle[pl.ds(at, 128), :])
             total = above + norm_rows_back(inner, scaled, rate, norm[0:1, :])
-            middle_grad[pl.ds(at, 16), :] = total
-            middle_low[pl.ds(at, 16), :] = total.astype(bf16)
+            middle_grad[pl.ds(at, 128), :] = total
+            middle_low[pl.ds(at, 128), :] = total.astype(bf16)
             for k, part in enumerate((above, inner * scaled, inner, total)):
                 sums[k] += fold(part)
 
-        each_strip(rows, 16, strip, 4)
+        each_strip(rows, 128, strip)
 
 
 def gates_backward_body(
     middle_low, weight, gate_out, carried, signal, carried_grad, gate_grad, bias_grad, product_ref
 ):
     rows = middle_low.shape[0]
-    chunk = min(256, rows)
+    chunk = min(512, rows)
     bias_grad[...] = jnp.zeros_like(bias_grad)
 
     def product(at):
@@ -563,11 +573,12 @@
 def in_backward_body(
     split, place, first_grad, second_grad, third_grad, halo, age, projected, taps, normed,
     middle_low, mixer, weight, state, middle_grad, norm,
-    grad, grad_out, weight_grad, bias_grad, taps_grad, sums,
-    normed_turned, middle_turned, spread, low,
+    grad, grad_out, bias_grad, taps_grad, sums, *refs
 ):
+    normed_turned, middle_turned, spread, low = refs[-4:]
+    weight_grads = refs[:-4]
     rows = normed.shape[0]
-    chunk = min(256, rows)
+    chunk = min(512, rows)
     order = row_order(split, place[0], 0 if not split else split)
 
     @pl.when(pl.program_id(0) == 0)
@@ -633,30 +644,34 @@
 
     each_strip(rows, chunk, product)
 
-    def product_weight(at):
-        weight_grad[0, pl.ds(at, 256), : 3 * LANES] = dot(
-            normed_turned[pl.ds(at, 256), :], low[...]
-        ).astype(bf16)
-        weight_grad[0, pl.ds(at, 256), 3 * LANES :] = dot(
-            middle_turned[pl.ds(at, 256), :], mixer[...]
-        ).astype(bf16)
-
-    each_strip(D, 256, product_weight)
+    size = D // len(weight_grads)
+    for k, weight_grad in enumerate(weight_grads):
+
+        def product_weight(at):
+            source = pl.ds(k * size + at, 192)
+            weight_grad[0, pl.ds(at, 192), : 3 * LANES] = dot(
+                normed_turned[source, :], low[...]
+            ).astype(bf16)
+            weight_grad[0, pl.ds(at, 192), 3 * LANES :] = dot(
+                middle_turned[source, :], mixer[...]
+            ).astype(bf16)
+
+        each_strip(size, 192, product_weight)
 
     @pl.when(pl.program_id(0) == pl.num_programs(0) - 1)
     def _():
         def strip(at):
-            inner = grad[pl.ds(at, 16), :]
-            scaled, rate = norm_rows(state[pl.ds(at, 16), :].astype(f32))
-            total = middle_grad[pl.ds(at, 16), :] + norm_rows_back(
+            inner = grad[pl.ds(at, 128), :]
+            scaled, rate = norm_rows(state[pl.ds(at, 128), :].astype(f32))
+            total = middle_grad[pl.ds(at, 128), :] + norm_rows_back(
                 inner, scaled, rate, norm[0:1, :]
             )
-            grad[pl.ds(at, 16), :] = total
-            grad_out[pl.ds(at, 16), :] = total.astype(bf16)
+            grad[pl.ds(at, 128), :] = total
+            grad_out[pl.ds(at, 128), :] = total.astype(bf16)
             for k, part in enumerate((inner * scaled, inner)):
                 sums[k] += fold(part)
 
-        each_strip(rows, 16, strip, 4)
+        each_strip(rows, 128, strip)
 
 
 def whole(shape):
@@ -673,13 +688,13 @@
     return pl.BlockSpec(shape, lambda i, *_: (i,) + (0,) * (len(shape) - 1))
 
 
-def weight_block(wide, per, first=0, stride=1):
+def weight_block(wide, per, first=0, stride=1, depth=D):
     return pl.BlockSpec(
-        (1, D, wide), lambda i, *_: (i // per, 0, first + stride * (i % per))
-    )
-
-
-def run(body, name, grid, scalars, ins, outs, scratch, flops, moved, limit=48):
+        (1, depth, wide), lambda i, *_: (i // per, 0, first + stride * (i % per))
+    )
+
+
+def run(body, name, grid, scalars, ins, outs, scratch, flops, moved, limit=48, aliases={}):
     arrays, in_specs = zip(*ins)
     shapes, out_specs = zip(*outs)
     return pl.pallas_call(
@@ -693,6 +708,7 @@
             scratch_shapes=scratch,
         ),
         compiler_params=pltpu.CompilerParams(vmem_limit_bytes=limit << 20),
+        input_output_aliases=aliases,
         cost_estimate=pl.CostEstimate(flops=flops, bytes_accessed=moved, transcendentals=0),
         name=name,
     )(*scalars, *arrays)
@@ -748,24 +764,28 @@
             (shape_of(row, f32), whole(row)), (shape_of(row, bf16), whole(row)), tall, tall,
             (shape_of(row, f32), whole(row)), (shape_of(row, bf16), whole(row)),
         ],
-        [pltpu.VMEM((min(256, rows), HIDDEN), f32)],
+        [pltpu.VMEM((min(512, rows), HIDDEN), f32)],
         2 * rows * D * (2 * FF + D), 40_000_000, 32,
     )
 
 
-def ff_backward(split, place, grad, second, middle, norm, activated, slope, weights, hidden_per):
+def ff_backward(
+    split, place, grad, second, middle, norm, activated, slope, weights, hidden_per, shared
+):
     rows = grad.shape[0]
     row = (rows, D)
+    hidden_blocks = FF // HIDDEN
     halves = weights.shape[0]
-    hidden_blocks = FF // HIDDEN
-    grads = shape_of((halves, D, 2 * FF // halves), bf16)
+    grads = shape_of((halves, D, 2 * FF // halves) if shared is None else shared.shape, bf16)
+    base = [] if shared is None else [(shared, pl.BlockSpec(memory_space=pl.ANY))]
     return run(
         functools.partial(ff_backward_body, split), "ff_backward", hidden_blocks, (place,),
         [
             (grad, whole(row)), (second, whole(row)), (middle, whole(row)), (norm, whole((2, D))),
             (activated, by_lane((rows, HIDDEN))), (slope, by_lane((rows, HIDDEN))),
             (weights, weight_block(2 * HIDDEN, hidden_per)),
-        ],
+        ]
+        + base,
         [
             (shape_of(row, f32), whole(row)), (shape_of(row, bf16), whole(row)),
             (grads, weight_block(2 * HIDDEN, hidden_per)),
@@ -774,9 +794,9 @@
         ],
         [
             pltpu.VMEM(row, bf16), pltpu.VMEM((D, rows), bf16), pltpu.VMEM((D, rows), bf16),
-            pltpu.VMEM((min(256, rows), HIDDEN), f32), pltpu.VMEM((rows, HIDDEN), bf16),
-        ],
-        8 * rows * D * FF, 50_000_000, 40,
+            pltpu.VMEM((min(512, rows), HIDDEN), f32), pltpu.VMEM((rows, HIDDEN), bf16),
+        ],
+        8 * rows * D * FF, 50_000_000, 40, {8: 2} if base else {},
     )
 
 
@@ -794,19 +814,23 @@
             low, low,
             (shape_of((D // LANES, 1, LANES), f32), by_first((1, 1, LANES))),
         ],
-        [pltpu.VMEM((min(256, rows), LANES), f32)],
+        [pltpu.VMEM((min(512, rows), LANES), f32)],
         2 * rows * D * D, 10_000_000, 20,
     )
 
 
 def in_backward(
     split, place, mixed_grads, halo, age, projected, taps, normed, middle_low, mixer, weights,
-    first, per, state, middle_grad, norm,
+    first, per, state, middle_grad, norm, columns, grad_first,
 ):
     rows = normed.shape[0]
     row, block = (rows, D), (rows, LANES)
     blocks = D // LANES
-    grads = shape_of((weights.shape[0], D, 4 * per * LANES), bf16)
+    count = 2 if split else 1
+    grads = (
+        shape_of((weights.shape[0], D // count, columns), bf16),
+        weight_block(4 * LANES, per, grad_first, depth=D // count),
+    )
     return run(
         functools.partial(in_backward_body, split), "in_backward", blocks, (place,),
         [(part, by_lane(block)) for part in mixed_grads]
@@ -819,11 +843,11 @@
         ],
         [
             (shape_of(row, f32), whole(row)), (shape_of(row, bf16), whole(row)),
-            (grads, weight_block(4 * LANES, per)),
             (shape_of((blocks, 1, 3 * LANES), f32), by_first((1, 1, 3 * LANES))),
             (shape_of((blocks, 3, 3 * LANES), f32), by_first((1, 3, 3 * LANES))),
             (shape_of((2, 8, D), f32), whole((2, 8, D))),
-        ],
+        ]
+        + [grads] * count,
         [
             pltpu.VMEM((D, rows), bf16), pltpu.VMEM((D, rows), bf16),
             pltpu.VMEM((rows + HALO, 3 * LANES), bf16), pltpu.VMEM((rows, 3 * LANES), bf16),
@@ -837,19 +861,19 @@
     wide = window.shape[0]
     blocks = wide // BLK - 1
     own_block = (wide - BLK - rows) // BLK
-    low = (shape_of((rows, D), bf16), by_lane((rows, LANES)))
+    low = (shape_of((rows, D), bf16), by_lane((rows, CONV_LANES)))
     return run(
-        functools.partial(conv_forward_body, own_block), "conv_forward", D // LANES, (table,),
-        [
-            (window, by_lane((wide, LANES))), (kernel, by_lane((TAPS, 2 * BLK, LANES))),
-            (gate_out, by_lane((rows, LANES))), (bias, by_first((1, 1, LANES))),
+        functools.partial(conv_forward_body, own_block), "conv_forward", D // CONV_LANES, (table,),
+        [
+            (window, by_lane((wide, CONV_LANES))), (kernel, by_lane((TAPS, 2 * BLK, CONV_LANES))),
+            (gate_out, by_lane((rows, CONV_LANES))), (bias, by_first((1, 1, CONV_LANES))),
             (causal, whole((2 * BLK, 2 * BLK))), (back, whole((BLK, 2 * BLK))),
         ],
         [low, low],
         [
-            pltpu.VMEM((rows, LANES), f32),
-            pltpu.VMEM((blocks, 2 * BLK, LANES), f32),
-            pltpu.VMEM((2 * BLK, LANES), bf16),
+            pltpu.VMEM((rows, CONV_LANES), f32),
+            pltpu.VMEM((blocks + STEP - 1, 2 * BLK, CONV_LANES), f32),
+            pltpu.VMEM((2 * BLK, CONV_LANES), bf16),
         ],
         20_000_000_000, 20_000_000, 28,
     )
@@ -858,21 +882,21 @@
 def signal_backward(table, grads, kernel, values, gate_in, bias, rows, hops, tables):
     _, ahead, _, back = tables
     wide = grads.shape[0]
-    low = (shape_of((rows, D), bf16), by_lane((rows, LANES)))
+    low = (shape_of((rows, D), bf16), by_lane((rows, CONV_LANES)))
     return run(
         functools.partial(signal_backward_body, hops * rows // BLK), "signal_backward",
-        D // LANES, (table,),
-        [
-            (grads, by_lane((wide, LANES))),
-            (kernel, by_lane((TAPS, 2 * BLK, LANES))), (values, by_lane((rows, LANES))),
-            (gate_in, by_lane((rows, LANES))), (bias, by_first((1, 1, LANES))),
+        D // CONV_LANES, (table,),
+        [
+            (grads, by_lane((wide, CONV_LANES))),
+            (kernel, by_lane((TAPS, 2 * BLK, CONV_LANES))), (values, by_lane((rows, CONV_LANES))),
+            (gate_in, by_lane((rows, CONV_LANES))), (bias, by_first((1, 1, CONV_LANES))),
             (ahead, whole((2 * BLK, 2 * BLK))), (back, whole((BLK, 2 * BLK))),
         ],
         [low, low],
         [
-            pltpu.VMEM((rows, LANES), f32),
-            pltpu.VMEM((wide // BLK - 1, 2 * BLK, LANES), f32),
-            pltpu.VMEM((2 * BLK, LANES), bf16),
+            pltpu.VMEM((rows, CONV_LANES), f32),
+            pltpu.VMEM((wide // BLK + STEP - 2, 2 * BLK, CONV_LANES), f32),
+            pltpu.VMEM((2 * BLK, CONV_LANES), bf16),
         ],
         20_000_000_000, 20_000_000, 32,
     )
@@ -885,17 +909,17 @@
     own_block = (wide - BLK - rows) // BLK
     return run(
         functools.partial(kernel_backward_body, own_block), "kernel_backward",
-        D // LANES, (table,),
-        [
-            (window, by_lane((wide, LANES))), (grads, by_lane((rows, LANES))),
+        D // CONV_LANES, (table,),
+        [
+            (window, by_lane((wide, CONV_LANES))), (grads, by_lane((rows, CONV_LANES))),
             (causal, whole((2 * BLK, 2 * BLK))), (single, whole((2 * BLK, BLK))),
             (back, whole((BLK, 2 * BLK))),
         ],
-        [(shape_of((LMAX, D), f32), by_lane((LMAX, LANES)))],
-        [
-            pltpu.VMEM((blocks, 2 * BLK, LANES), f32),
-            pltpu.VMEM((rows // BLK, 2 * BLK, LANES), f32),
-            pltpu.VMEM((TAPS, 2 * BLK, LANES), f32),
+        [(shape_of((LMAX, D), f32), by_lane((LMAX, CONV_LANES)))],
+        [
+            pltpu.VMEM((blocks + STEP - 1, 2 * BLK, CONV_LANES), f32),
+            pltpu.VMEM((rows // BLK + STEP - 1, 2 * BLK, CONV_LANES), f32),
+            pltpu.VMEM((TAPS, 2 * BLK, CONV_LANES), f32),
         ],
         20_000_000_000, 20_000_000, 32,
     )[0]
@@ -959,7 +983,7 @@
     def pick(values, index, axis=0):
         return lax.dynamic_index_in_dim(values, index, axis, False)
 
-    def gather_pairs(values):
+    def gather_pairs(values, beside):
         n = values.shape[-1]
         parts = jnp.stack([values] + [swap(values, k << 2) for k in range(1, planes)])
         values = jnp.stack([pick(parts, k ^ plane) for k in range(planes)])
@@ -971,16 +995,21 @@
                 for s in range(2)
             ]
         )
+        values, beside = lax.optimization_barrier((values, beside))
         other = swap_core(values)
         values = jnp.stack(
             [jnp.where(core == 0, values, other), jnp.where(core == 0, other, values)], axis=3
         )
-        return values.reshape(2, D, n)
-
-    def scatter_pairs(values):
-        half = D // 2
-        other = swap_core(values[:, half:])
-        total = (values[:, :half].astype(f32) + other.astype(f32)).astype(bf16)
+        return values.reshape(2, D, n), beside
+
+    def total_of(parts, mine):
+        held = jnp.stack(parts)
+        total = pick(held, mine).astype(f32)
+        for k in range(1, len(parts)):
+            total += pick(held, k ^ mine).astype(f32)
+        return total
+
+    def reduce_plane(total):
         total = total.reshape(2, planes, 2, depth, -1)
 
         def block(s, r):
@@ -997,6 +1026,27 @@
             total += part.astype(f32)
         return total
 
+    def reduce_all(extra):
+        def rounded(values):
+            return lax.optimization_barrier(values.astype(bf16))
+
+        if paired:
+            low = rounded(extra)
+            low = rounded(low.astype(f32) + swap_core(low).astype(f32))
+            parts = [low] + [swap(low, k) for k in range(1, 4)]
+            extra = total_of(parts, row * 2 + side)
+            for k in range((planes - 1).bit_length()):
+                low = rounded(extra)
+                extra = low.astype(f32) + swap(low, 4 << k).astype(f32)
+            return extra
+        step = 1
+        while step < devices:
+            low = rounded(extra)
+            other = lax.ppermute(low, everyone, [(i, i ^ step) for i in range(devices)])
+            extra = low.astype(f32) + other.astype(f32)
+            step *= 2
+        return extra
+
     def from_before(values, hop=1):
         return lax.ppermute(values, everyone, [(i, i + hop) for i in range(devices - hop)])
 
@@ -1014,11 +1064,13 @@
         return mix, ff
 
     def part_columns(mix, ff, mix_blocks, ff_blocks):
-        lead = mix.shape[:-1]
-        mix = mix.reshape(*lead, mix_blocks, 4, -1)
-        ff = ff.reshape(*lead, ff_blocks, 2, -1)
-        parts = [mix[..., k, :].reshape(*lead, -1) for k in range(4)]
-        return parts[:3], parts[3], *[ff[..., k, :].reshape(*lead, -1) for k in range(2)]
+        def strided(values, blocks, kinds, k):
+            size = values.shape[-1] // (blocks * kinds)
+            starts = [(kinds * b + k) * size for b in range(blocks)]
+            return jnp.concatenate([values[..., at : at + size] for at in starts], axis=-1)
+
+        mixes = [strided(mix, mix_blocks, 4, k) for k in range(4)]
+        return mixes[:3], mixes[3], *[strided(ff, ff_blocks, 2, k) for k in range(2)]
 
     local_mix = per if direct else 1
     local_ff = hidden_per if direct else 1
@@ -1038,12 +1090,38 @@
     def gather(part):
         return lax.all_gather(part, owners, axis=0, tiled=True).reshape(tensor_count, D, -1)
 
+    tables = tuple(jnp.asarray(t, f32).astype(bf16) for t in wave_tables())
+    positions = positions_table(LMAX)
+    modulation = decay_table(LMAX)
+    blank = jnp.zeros((BLK, D), bf16)
+
+    filters = []
+    for layer in range(LAYERS):
+        inner, filter_back = jax.vjp(
+            lambda a, b, c, d: filter_hidden(positions, a, b, c, d),
+            filter_first[layer],
+            filter_inner[layer],
+            filter_biases[layer],
+            filter_rates[layer],
+        )
+        kernel = jnp.dot(inner, filter_out[layer], precision=highest) * modulation
+        kernel_spectra = jnp.einsum(
+            "kr,brc->bkc",
+            tables[2],
+            kernel.reshape(TAPS, BLK, D).astype(bf16),
+            preferred_element_type=f32,
+        )
+        filters.append((inner, filter_back, kernel_spectra))
+
     gathered = []
     if paired:
         shared = gather(jnp.concatenate([local[0][1], local[1][0]], axis=1))
         last = gather(local[1][1])
-        gathered.append((gather_pairs(local[0][0]), 0, shared))
-        gathered.append((shared, 2 * hidden // (4 * LANES), last))
+        inner, filter_back, kernel_spectra = filters[0]
+        mix, kernel_spectra = gather_pairs(local[0][0], kernel_spectra)
+        filters[0] = (inner, filter_back, kernel_spectra)
+        gathered.append((mix, 0, shared))
+        gathered.append((shared[:, :, 2 * hidden :], 0, last))
     else:
         for mix, ff in local:
             mix, ff = gather(mix), gather(ff)
@@ -1073,33 +1151,13 @@
             ends[count - 1 :],
         ]
     ).astype(jnp.int32)
-    places = base + jnp.arange(rows + HALO, dtype=jnp.int32)
-    begun = jnp.max(jnp.where(starts[None, :] <= places[:, None], starts[None, :], 0), axis=1)
-    age = jnp.broadcast_to((places - begun)[:, None], (rows + HALO, 128))
+
+    def ages(places):
+        begun = jnp.max(jnp.where(starts[None, :] <= places[:, None], starts[None, :], 0), axis=1)
+        return jnp.broadcast_to((places - begun)[:, None], (places.shape[0], 128))
+
+    age = ages(base + jnp.arange(rows + HALO, dtype=jnp.int32))
     place = core.astype(jnp.int32).reshape(1)
-
-    tables = tuple(jnp.asarray(t, f32).astype(bf16) for t in wave_tables())
-    positions = positions_table(LMAX)
-    modulation = decay_table(LMAX)
-    blank = jnp.zeros((BLK, D), bf16)
-
-    filters = []
-    for layer in range(LAYERS):
-        inner, filter_back = jax.vjp(
-            lambda a, b, c, d: filter_hidden(positions, a, b, c, d),
-            filter_first[layer],
-            filter_inner[layer],
-            filter_biases[layer],
-            filter_rates[layer],
-        )
-        kernel = jnp.dot(inner, filter_out[layer], precision=highest) * modulation
-        kernel_spectra = jnp.einsum(
-            "kr,brc->bkc",
-            tables[2],
-            kernel.reshape(TAPS, BLK, D).astype(bf16),
-            preferred_element_type=f32,
-        )
-        filters.append((inner, filter_back, kernel_spectra))
 
     def by_block(values):
         lead = values.shape[:-2]
@@ -1119,21 +1177,16 @@
         first_norm = jnp.stack([norm_gains[layer, 0], norm_biases[layer, 0]])
         second_norm = jnp.stack([norm_gains[layer, 1], norm_biases[layer, 1]])
         taps = by_block(short_taps[layer])
-        lane_bias = conv_bias[layer].reshape(D // LANES, 1, LANES)
+        lane_bias = conv_bias[layer].reshape(D // CONV_LANES, 1, CONV_LANES)
+        shared_in = (
+            first_norm, mix_weights, first, per, by_block(input_bias[layer][None]), taps
+        )
+        near = from_before(state[rows - HALO :])
         normed, projected, gate_out, gate_in, values, signal = in_forward(
-            state,
-            from_before(state[rows - HALO :]),
-            first_norm,
-            mix_weights,
-            first,
-            per,
-            by_block(input_bias[layer][None]),
-            taps,
-            age,
-        )
-        window = jnp.concatenate(
-            [blank] + [from_before(signal, hop) for hop in range(hops, 0, -1)] + [signal]
-        )
+            state, near, *shared_in, age
+        )
+        before = [from_before(signal, hop) for hop in range(hops, 0, -1)]
+        window = jnp.concatenate([blank, *before, signal])
         carried, mixer = conv_forward(
             table, window, filters[layer][2], gate_out, lane_bias, rows, tables
         )
@@ -1152,8 +1205,19 @@
 
     grad = out_grad
     owned, owned_ff = {}, {}
+    ff_columns = 2 * FF // halves
+    shared = None
     small = [None] * LAYERS
+
+    def share(part):
+        return lax.psum_scatter(
+            part.reshape(tensor_count * D, -1), owners, scatter_dimension=0, tiled=True
+        )
+
     for layer in reversed(range(LAYERS)):
+        joint = paired and layer == LAYERS - 1
+        mix_columns = 4 * D // halves + (ff_columns if joint else 0)
+        mix_first = ff_columns // (4 * LANES) if joint else 0
         (
             state, first_norm, second_norm, taps, lane_bias, normed, projected, gate_out,
             gate_in, values, signal, window, carried, mixer, middle, second, activated, slope,
@@ -1161,7 +1225,8 @@
         mix_weights, first, ff_weights = gathered[layer]
         inner, filter_back, kernel_spectra = filters[layer]
         middle_grad, middle_low, ff_grad, up_bias_grad, ff_sums = ff_backward(
-            0, place, grad, second, middle, second_norm, activated, slope, ff_weights, hidden_per
+            0, place, grad, second, middle, second_norm, activated, slope, ff_weights, hidden_per,
+            shared,
         )
         carried_grad, gate_grad, conv_bias_grad = gates_backward(
             middle_low, mix_weights, first, per, gate_out, carried, signal
@@ -1172,8 +1237,8 @@
         filter_out_grad = jnp.dot(jnp.transpose(inner), shaped, precision=highest)
         inner_grad = jnp.dot(shaped, jnp.transpose(filter_out[layer]), precision=highest)
         filter_grads = filter_back(inner_grad)
-        ahead, filter_grads, filter_out_grad, owned = lax.optimization_barrier(
-            (ahead, filter_grads, filter_out_grad, owned)
+        ahead, filter_grads, filter_out_grad = lax.optimization_barrier(
+            (ahead, filter_grads, filter_out_grad)
         )
         grads_window = jnp.concatenate([carried_grad] + ahead + [blank])
         gate_in_grad, values_grad = signal_backward(
@@ -1181,11 +1246,13 @@
         )
         mixed_grads = (gate_grad, gate_in_grad, values_grad)
         after = from_after(jnp.stack([part[:HALO] for part in mixed_grads]))
-        grad, grad_low, mix_grad, in_bias_grad, taps_grad, in_sums = in_backward(
-            split, place, mixed_grads, after, age, projected, taps, normed, middle_low, mixer,
-            mix_weights, first, per, state, middle_grad, first_norm,
-        )
-
+        grad, grad_low, in_bias_grad, taps_grad, in_sums, *mix_grad = in_backward(
+            0 if joint else split, place, mixed_grads, after, age, projected, taps, normed, middle_low, mixer,
+            mix_weights, first, per, state, middle_grad, first_norm, mix_columns, mix_first,
+        )
+
+        if len(mix_grad) == 1:
+            mix_grad = mix_grad[0]
         if not direct:
             ins, out, up, down = part_columns(mix_grad, ff_grad, per, hidden_per)
 
@@ -1197,13 +1264,17 @@
                 [by_owner(k) for k in ins], by_owner(out), by_owner(up), by_owner(down), 1, 1
             )
 
-        def share(part):
-            return lax.psum_scatter(
-                part.reshape(tensor_count * D, -1), owners, scatter_dimension=0, tiled=True
-            )
-
-        owned[layer] = (scatter_pairs(mix_grad) if paired else share(mix_grad)).astype(f32)
-        owned_ff[layer] = share(ff_grad).astype(f32)
+        if not paired:
+            owned[layer], owned_ff[layer] = share(mix_grad), share(ff_grad)
+        elif layer == LAYERS - 1:
+            owned_ff[layer] = share(ff_grad)
+            shared = mix_grad
+        else:
+            both = share(ff_grad)
+            owned_ff[layer] = both[:, :ff_columns]
+            owned[layer + 1] = both[:, ff_columns:]
+            last_grads = mix_grad
+
         ff_sums = jnp.sum(ff_sums, axis=1)
         in_sums = jnp.sum(in_sums, axis=1)
         small[layer] = (
@@ -1218,31 +1289,49 @@
             up_bias_grad.reshape(FF),
         )
 
-    small_stacked = [
-        jnp.stack([small[layer][index] for layer in range(LAYERS)])
-        for index in range(len(small[0]))
-    ]
-    sizes = [part.size for part in small_stacked]
-    flat = jnp.concatenate([part.reshape(-1) for part in small_stacked])
-    unit = 1024
-    padded = -(-flat.shape[0] // unit) * unit
-    flat = jnp.pad(flat, (0, padded - flat.shape[0])).reshape(padded // 128, 128)
-    step = 1
-    while step < devices:
-        low = flat.astype(bf16)
-        other = lax.ppermute(low, everyone, [(i, i ^ step) for i in range(devices)])
-        flat = low.astype(f32) + other.astype(f32)
-        step *= 2
-    flat = flat.reshape(-1)
-    summed = []
+    narrow = range(2, 6)
+    filter_size = filter_first.shape[2]
+
+    def as_rows(layer):
+        thin = jnp.concatenate([small[layer][k].reshape(-1, filter_size) for k in narrow])
+        thin = jnp.pad(thin, ((0, -thin.shape[0] % (D // filter_size)), (0, 0)))
+        wide = [small[layer][k].reshape(-1, D) for k in range(12) if k not in narrow]
+        return wide + [thin.reshape(-1, D)]
+
+    blocks = [as_rows(layer) for layer in range(LAYERS)]
+    flat = jnp.concatenate([block.astype(bf16) for part in blocks for block in part])
+    filled = flat.shape[0]
+    flat = jnp.pad(flat, ((0, -filled % 16), (0, 0)))
+    if paired:
+        keep, send = last_grads
+        total = (keep.astype(f32) + swap_core(send).astype(f32)).astype(bf16)
+        flat, _ = lax.optimization_barrier((flat, total))
+        owned[0] = reduce_plane(total)
+    flat = reduce_all(flat)
+    found = [[None] * 12 for _ in range(LAYERS)]
     offset = 0
-    for part, size in zip(small_stacked, sizes):
-        summed.append(flat[offset : offset + size].reshape(part.shape))
-        offset += size
+    for layer in range(LAYERS):
+        pieces = []
+        for block in blocks[layer]:
+            pieces.append(flat[offset : offset + block.shape[0]])
+            offset += block.shape[0]
+        thin = pieces[-1].reshape(-1, filter_size)
+        at = 0
+        for k in range(12):
+            like = small[layer][k]
+            if k in narrow:
+                count = like.size // filter_size
+                found[layer][k] = thin[at : at + count].reshape(like.shape)
+                at += count
+            else:
+                found[layer][k] = pieces[k if k < 2 else k - 4].reshape(like.shape)
+    summed = [jnp.stack([found[layer][k] for layer in range(LAYERS)]) for k in range(12)]
 
     in_owned, out_owned, up_owned, down_owned = [], [], [], []
     for layer in range(LAYERS):
-        ins, out, up, down = part_columns(owned[layer], owned_ff[layer], local_mix, local_ff)
+        ins, out, up, down = part_columns(
+            owned[layer].astype(f32), owned_ff[layer].astype(f32), local_mix, local_ff
+        )
         in_owned.append(jnp.stack(ins))
         out_owned.append(jnp.transpose(out))
         up_owned.append(up)

time: 918 us -> 787 us (0.86)
  Pallas kernels: 402 us -> 329 us
  local copies, waits for them, and re-layouts: 115 us -> 87.1 us
  waiting for transfers between devices: 215 us -> 198 us
  starting transfers between devices: 72.2 us -> 60 us
    pallas_call x16, Pallas kernels: 402 us -> 329 us  [run(): pl.pallas_call(body, out_shape=shapes, grid_spec=pltpu.PrefetchScalarGrid...]
    ppermute x5 -> x0, waiting for transfers between devices: 30.2 us -> none  [shards(): other = lax.ppermute(low, everyone, [(i, i ^ step) for i in range(devices)])]
    reshape x31 -> x2, local copies, waits for them, and re-layouts: 13.7 us -> 0.16 us  [shards(): thin = pieces[-1].reshape(-1, filter_size)]
    unnamed x364 -> x350, local copies, waits for them, and re-layouts: 76.9 us -> 64.3 us
    ppermute x18 -> x17, starting transfers between devices: 39.2 us -> 26.6 us  [swap(): return lax.ppermute(values, ('chip', 'tensor'), pairs)]
    ppermute x18 -> x17, waiting for transfers between devices: 106 us -> 115 us  [swap(): return lax.ppermute(values, ('chip', 'tensor'), pairs)]
  transfers between devices with their start and end apart: 38 -> 32, of which waited for: 21 -> 18; matrix products, arithmetic and copies ran while one was open for 14% -> 13% of each run, Pallas kernels for 35% -> 33%
where the time goes in v3:
time: 787 us; the launch traced here: 782 us
  Pallas kernels  329 us (42%)
  waiting for transfers between devices  198 us (25%)
  local copies, waits for them, and re-layouts  87.1 us (11%)
  starting transfers between devices  60 us (8%)
  matrix products  55.4 us (7%)
  other arithmetic  34.5 us (4%)
  between operations  18.4 us (2%)
    pallas_call x16, Pallas kernels, run(): pl.pallas_call(body, out_shape=shapes, grid_spec=pltpu.PrefetchScalarGrid...  329 us
    ppermute x17, waiting for transfers between devices, swap(): return lax.ppermute(values, ('chip', 'tensor'), pairs)  115 us
    unnamed x350, local copies, waits for them, and re-layouts  64.3 us
    ppermute x4, waiting for transfers between devices, from_before(): lax.ppermute(values, everyone, [(i, i + hop) for i in range(devices - hop)])  54.3 us
    ppermute x4, waiting for transfers between devices, from_after(): lax.ppermute(values, everyone, [(i + hop, i) for i in range(devices - hop)])  27 us
    ppermute x17, starting transfers between devices, swap(): return lax.ppermute(values, ('chip', 'tensor'), pairs)  26.6 us
    ppermute x4, starting transfers between devices, from_before(): lax.ppermute(values, everyone, [(i, i + hop) for i in range(devices - hop)])  19.4 us
  transfers between devices with their start and end apart: 32, of which 18 were waited for; matrix products, arithmetic and copies ran while one was open for 13% of the time, Pallas kernels for 33%

profile of v3, /device:TPU:0, one launch (start us, length us, event | category | flops | bytes accessed | tf_op | source)
XLA Modules:
  0.0 782.1 jit_solution(4410623193634915364)
XLA Ops:
  14.8 5.1 collective-permute-start.3
  27.1 14.8 %collective-permute-done.2 = bf16[48,1536]{1,0:T(8,128)(2,1)S(1)} collective-permute-done((bf16[48,1536]{1,0:T(8,128)(2,1)S(1)}, bf16[48,1536]{1,0:T(8,128)(2,1)S(1)}, u32[]{:S(2)}, u32[]{:S(2)}) %collective-permute-start.2) | collective-permute-done | bytes 147488 | tf_op jit(solution)/shard_map/ppermute | solution.py:978
  42.2 2.5 collective-permute-start.6
  45.7 4.5 multiply_convert_fusion.1
  50.3 3.6 convolution_bitcast_fusion.1.kernel
  53.9 15.3 %collective-permute-done.6 = bf16[4,48,1536]{2,1,0:T(8,128)(2,1)S(1)} collective-permute-done((bf16[4,48,1536]{2,1,0:T(8,128)(2,1)S(1)}, bf16[4,48,1536]{2,1,0:T(8,128)(2,1)S(1)}, u32[]{:S(2)}, u32[]{:S(2)}) %collective-permute-start.6) | collective-permute-done | bytes 589856 | tf_op jit(solution)/shard_map/ppermute | solution.py:978
  69.2 4.8 collective-permute-done.5
  74.0 6.4 collective-permute-done.4
  82.2 3.9 collective-permute-start
  88.7 2.7 select_bitcast_fusion.1
  92.8 14.7 %in_forward.2 = (bf16[1024,768]{1,0:T(8,128)(2,1)S(1)}, bf16[3,1040,768]{2,1,0:T(8,128)(2,1)S(1)}, bf16[1024,768]{1,0:T(8,128)(2,1)S(1)}, bf16[1024,768]{1,0:T(8...) custom-call(bf16[1024,768]{1,0:T(8,128)(2,1)S(1)} %copy-done.48, ...), custom_call_target="tpu_custom_call" | custom-call | flops 3623878656 | bytes 20000000 | tf_op jit(solution)/shard_map/in_forward/pallas_call | solution.py:700
  107.6 2.3 copy-done.64
  113.3 4.2 collective-permute-start.8
  120.3 29.8 %collective-permute-done.8 = bf16[1024,768]{1,0:T(8,128)(2,1)} collective-permute-done((bf16[1024,768]{1,0:T(8,128)(2,1)S(1)}, bf16[1024,768]{1,0:T(8,128)(2,1)}, u32[]{:S(2)}, u32[]{:S(2)}) %collective-permute-start.8) | collective-permute-done | bytes 1572896 | tf_op jit(solution)/shard_map/ppermute | solution.py:1051
  151.9 2.8 copy-done.5
  154.7 11.8 %conv_forward.2 = (bf16[1024,768]{1,0:T(8,128)(2,1)S(1)}, bf16[1024,768]{1,0:T(8,128)(2,1)S(1)}) custom-call(s32[52]{0:T(128)S(1)} %concatenate.52.table, bf16[2176,768]{1,0:T(8,128)(2,1)S(1)} %fusion.window, f32[8,256,768]{2,1,0:T(8,128)S(1)} %copy-done.5, bf16[1024,768]{1,0:T(8,128)(2,1)S(1)} %get-tuple-element.96.gate_out, ...), custom_call_target="tpu_custom_call" | custom-call | flops 20000000000 | bytes 20000000 | tf_op jit(solution)/shard_map/conv_forward/pallas_call | solution.py:700
  170.6 2.3 copy-done.1
  175.7 30.5 %ff_forward.2 = (f32[1024,768]{1,0:T(8,128)S(1)}, bf16[1024,768]{1,0:T(8,128)(2,1)S(1)}, bf16[1024,3072]{1,0:T(8,128)(2,1)S(1)}, bf16[1024,3072]{1,0:T(8,128)(2,...) custom-call(bf16[1024,768]{1,0:T(8,128)(2,1)S(1)} %copy-done.83, bf16[1024,768]{1,0:T(8,128)(2,1)S(1)} %copy-done.49, ...), custom_call_target="tpu_custom_call" | custom-call | flops 10871635968 | bytes 40000000 | tf_op jit(solution)/shard_map/ff_forward/pallas_call | solution.py:700
  206.2 2.6 copy-done.81
  213.3 5.2 collective-permute-start.9
  218.6 2.9 slice.540.weight.refs_0_.refs_1_
  222.5 14.6 %in_forward.3 = (bf16[1024,768]{1,0:T(8,128)(2,1)S(1)}, bf16[3,1040,768]{2,1,0:T(8,128)(2,1)S(1)}, bf16[1024,768]{1,0:T(8,128)(2,1)S(1)}, bf16[1024,768]{1,0:T(8...) custom-call(f32[1024,768]{1,0:T(8,128)S(1)} %copy-done.43, ...), custom_call_target="tpu_custom_call" | custom-call | flops 3623878656 | bytes 20000000 | tf_op jit(solution)/shard_map/in_forward/pallas_call | solution.py:700
  237.2 6.0 collective-permute-start.10
  247.1 4.6 multiply_convert_fusion
  252.7 24.5 %collective-permute-done.10 = bf16[1024,768]{1,0:T(8,128)(2,1)S(1)} collective-permute-done((bf16[1024,768]{1,0:T(8,128)(2,1)S(1)}, bf16[1024,768]{1,0:T(8,128)(2,1)S(1)}, u32[]{:S(2)}, u32[]{:S(2)}) %collective-permute-start.10) | collective-permute-done | bytes 1572896 | tf_op jit(solution)/shard_map/ppermute | solution.py:1051
  277.6 12.1 %conv_forward.3 = (bf16[1024,768]{1,0:T(8,128)(2,1)S(1)}, bf16[1024,768]{1,0:T(8,128)(2,1)S(1)}) custom-call(s32[52]{0:T(128)S(1)} %concatenate.52.table, bf16[2176,768]{1,0:T(8,128)(2,1)S(1)} %fusion.1.window, f32[8,256,768]{2,1,0:T(8,128)S(1)} %convolution_bitcast_fusion.kernel, bf16[1024,768]{1,0:T(8,128)(2,1)S(1)} %get-tuple-element.101.gate_out, ...), custom_call_target="tpu_custom_call" | custom-call | flops 20000000000 | bytes 20000000 | tf_op jit(solution)/shard_map/conv_forward/pallas_call | solution.py:700
  289.7 1.7 copy-done.9
  293.8 2.3 copy-done.3
  296.1 1.9 copy-done.44
  299.4 31.6 %ff_forward.3 = (f32[1024,768]{1,0:T(8,128)S(1)}, bf16[1024,768]{1,0:T(8,128)(2,1)S(1)}, bf16[1024,3072]{1,0:T(8,128)(2,1)}, bf16[1024,3072]{1,0:T(8,128)(2,1)},...) custom-call(bf16[1024,768]{1,0:T(8,128)(2,1)S(1)} %copy-done.74, f32[1024,768]{1,0:T(8,128)S(1)} %copy-done.44, ...), custom_call_target="tpu_custom_call" | custom-call | flops 10871635968 | bytes 40000000 | tf_op jit(solution)/shard_map/ff_forward/pallas_call | solution.py:700
  331.1 38.5 %ff_backward.2 = (f32[1024,768]{1,0:T(8,128)S(1)}, bf16[1024,768]{1,0:T(8,128)(2,1)S(1)}, bf16[2,768,3072]{2,1,0:T(8,128)(2,1)}, f32[4,1,768]{2,1,0:T(1,128)S(1)}, f32[4,8,768]{2,1,0:T(8,128)S(1)}) custom-call(s32[1]{0:T(128)} %bitcast.87.place, bf16[1024,768]{1,0:T(8,128)(2,1)S(1)} %copy-done.52, bf16[1024,768]{1,0:T(8,128)(2,1)S(1)} %get-tuple-element.104.second, ...), custom_call_target="tpu_custom_call" | custom-call | flops 19327352832 | bytes 50000000 | tf_op jit(solution)/shard_map/ff_backward/pallas_call | solution.py:700
  372.5 2.3 copy-done.4
  379.1 4.4 gates_backward.2
  385.0 12.7 %kernel_backward.2 = f32[1024,768]{1,0:T(8,128)S(1)} custom-call(s32[52]{0:T(128)S(1)} %concatenate.52.table, bf16[2176,768]{1,0:T(8,128)(2,1)S(1)} %copy-done.10, bf16[1024,768]{1,0:T(8,128)(2,1)S(1)} %get-tuple-element.111.grads, bf16[256,256]{1,0:T(8,128)(2,1)S(1)} %copy-done.56, bf16[256,128]{1,0:T(8,128)(2,1)S(1)} %copy-done.61, ...), custom_call_target="tpu_custom_call" | custom-call | flops 20000000000 | bytes 20000000 | tf_op jit(solution)/shard_map/kernel_backward/pallas_call | solution.py:700
  397.8 5.3 multiply_reduce_fusion.5
  412.0 5.1 fusion.4
  417.1 3.9 collective-permute-done.11
  421.5 13.9 %signal_backward.2 = (bf16[1024,768]{1,0:T(8,128)(2,1)S(1)}, bf16[1024,768]{1,0:T(8,128)(2,1)S(1)}) custom-call(s32[52]{0:T(128)S(1)} %concatenate.52.table, bf16[2176,768]{1,0:T(8,128)(2,1)S(1)} %pad_maximum_fusion.4.grads, f32[8,256,768]{2,1,0:T(8,128)S(1)} %bitcast.379, bf16[1024,768]{1,0:T(8,128)(2,1)S(1)} %copy-done.71, ...), custom_call_target="tpu_custom_call" | custom-call | flops 20000000000 | bytes 20000000 | tf_op jit(solution)/shard_map/signal_backward/pallas_call | solution.py:700
  436.7 9.5 %collective-permute-done.12.halo = bf16[3,16,768]{2,1,0:T(8,128)(2,1)S(1)} collective-permute-done((bf16[3,16,768]{2,1,0:T(8,128)(2,1)S(1)}, bf16[3,16,768]{2,1,0:T(8,128)(2,1)S(1)}, u32[]{:S(2)}, u32[]{:S(2)}) %collective-permute-start.12) | collective-permute-done | bytes 73760 | tf_op jit(solution)/shard_map/ppermute | solution.py:1054
  446.2 36.8 %in_backward.2 = (f32[1024,768]{1,0:T(8,128)}, bf16[1024,768]{1,0:T(8,128)(2,1)}, f32[2,1,1152]{2,1,0:T(1,128)S(1)}, f32[2,3,1152]{2,1,0:T(4,128)S(1)}, f32[2,8,...) custom-call(s32[1]{0:T(128)} %bitcast.87.place, bf16[1024,768]{1,0:T(8,128)(2,1)S(1)} %get-tuple-element.110.first_grad, ...), custom_call_target="tpu_custom_call" | custom-call | flops 8455716864 | bytes 40000000 | tf_op jit(solution)/shard_map/in_backward/pallas_call | solution.py:700
  484.8 2.1 copy-done.66
  486.8 2.1 copy-done.85
  490.4 38.6 %ff_backward.3 = (f32[1024,768]{1,0:T(8,128)S(1)}, bf16[1024,768]{1,0:T(8,128)(2,1)S(1)}, bf16[2,768,4608]{2,1,0:T(8,128)(2,1)}, f32[4,1,768]{2,1,0:T(1,128)S(1)}, f32[4,8,768]{2,1,0:T(8,128)S(1)}) custom-call(s32[1]{0:T(128)} %bitcast.87.place, f32[1024,768]{1,0:T(8,128)S(1)} %copy-done.66, ...), custom_call_target="tpu_custom_call", output_to_operand_aliasing={{2}: (8, {})} | custom-call | flops 19327352832 | bytes 50000000 | tf_op jit(solution)/shard_map/ff_backward/pallas_call | solution.py:700
  529.1 5.1 gates_backward.3
  537.3 1.9 copy-done.8
  542.5 13.9 %kernel_backward.3 = f32[1024,768]{1,0:T(8,128)S(1)} custom-call(s32[52]{0:T(128)S(1)} %copy-done.46, bf16[2176,768]{1,0:T(8,128)(2,1)S(1)} %copy-done.8, bf16[1024,768]{1,0:T(8,128)(2,1)} %get-tuple-element.129.grads, bf16[256,256]{1,0:T(8,128)(2,1)S(1)} %copy-done.57, bf16[256,128]{1,0:T(8,128)(2,1)S(1)} %copy-done.62, bf16[128,256]{1,0:T(8,128)(2,1)S(1)} %copy-done.59), custom_call_target="tpu_custom_call" | custom-call | flops 20000000000 | bytes 20000000 | tf_op jit(solution)/shard_map/kernel_backward/pallas_call | solution.py:700
  556.5 5.3 multiply_reduce_fusion.2
  568.4 5.2 fusion.8
  574.1 2.7 pad_maximum_fusion.3.grads
  577.0 13.9 %signal_backward.3 = (bf16[1024,768]{1,0:T(8,128)(2,1)S(1)}, bf16[1024,768]{1,0:T(8,128)(2,1)S(1)}) custom-call(s32[52]{0:T(128)S(1)} %copy-done.47, bf16[2176,768]{1,0:T(8,128)(2,1)S(1)} %pad_maximum_fusion.3.grads, f32[8,256,768]{2,1,0:T(8,128)S(1)} %bitcast.377, bf16[1024,768]{1,0:T(8,128)(2,1)S(1)} %copy-done.80, bf16[1024,768]{1,0:T(8,128)(2,1)S(1)} %copy-done.78, ...), custom_call_target="tpu_custom_call" | custom-call | flops 20000000000 | bytes 20000000 | tf_op jit(solution)/shard_map/signal_backward/pallas_call | solution.py:700
  592.3 13.1 %collective-permute-done.14.halo = bf16[3,16,768]{2,1,0:T(8,128)(2,1)S(1)} collective-permute-done((bf16[3,16,768]{2,1,0:T(8,128)(2,1)S(1)}, bf16[3,16,768]{2,1,0:T(8,128)(2,1)S(1)}, u32[]{:S(2)}, u32[]{:S(2)}) %collective-permute-start.14) | collective-permute-done | bytes 73760 | tf_op jit(solution)/shard_map/ppermute | solution.py:1054
  605.5 35.8 %in_backward.3 = (f32[1024,768]{1,0:T(8,128)}, bf16[1024,768]{1,0:T(8,128)(2,1)}, f32[2,1,1152]{2,1,0:T(1,128)S(1)}, f32[2,3,1152]{2,1,0:T(4,128)S(1)}, f32[2,8,...) custom-call(s32[1]{0:T(128)} %bitcast.87.place, bf16[1024,768]{1,0:T(8,128)(2,1)S(1)} %copy-done.51, ...), custom_call_target="tpu_custom_call" | custom-call | flops 8455716864 | bytes 40000000 | tf_op jit(solution)/shard_map/in_backward/pallas_call | solution.py:700
  641.3 8.2 %collective-permute-start.15 = (bf16[2,384,1536]{2,1,0:T(8,128)(2,1)}, bf16[2,384,1536]{2,1,0:T(8,128)(2,1)}, u32[]{:S(2)}, u32[]{:S(2)}) collective-permute-start(bf16[2,384,1536]{2,1,0:T(8,128)(2,1)} %get-tuple-element.140), channel_id=1, source_target_pairs={{0,2},{2,0},{1,3},{3,1},{4,6},{6,4},{5,7},{7,5},{8,10},{10,8},{9,1... | collective-permute-start | bytes 7077896 | tf_op jit(solution)/shard_map/ppermute | solution.py:981
  655.4 3.0 add_convert_fusion
  659.7 5.9 collective-permute-start.18
  667.0 5.2 concatenate.66
  674.0 3.0 collective-permute-start.25
  677.0 8.4 %collective-permute-done.18 = bf16[4,48,1536]{2,1,0:T(8,128)(2,1)S(1)} collective-permute-done((bf16[4,48,1536]{2,1,0:T(8,128)(2,1)}, bf16[4,48,1536]{2,1,0:T(8,128)(2,1)S(1)}, u32[]{:S(2)}, u32[]{:S(2)}) %collective-permute-start.18) | collective-permute-done | bytes 589856 | tf_op jit(solution)/shard_map/ppermute | solution.py:978
  685.9 24.6 %collective-permute-done.17 = bf16[4,48,1536]{2,1,0:T(8,128)(2,1)} collective-permute-done((bf16[4,48,1536]{2,1,0:T(8,128)(2,1)}, bf16[4,48,1536]{2,1,0:T(8,128)(2,1)}, u32[]{:S(2)}, u32[]{:S(2)}) %collective-permute-start.17) | collective-permute-done | bytes 589856 | tf_op jit(solution)/shard_map/ppermute | solution.py:978
  712.2 3.2 collective-permute-start.21
  719.0 3.2 collective-permute-done.21
  722.1 8.5 %collective-permute-done.20 = bf16[48,1536]{1,0:T(8,128)(2,1)S(1)} collective-permute-done((bf16[48,1536]{1,0:T(8,128)(2,1)S(1)}, bf16[48,1536]{1,0:T(8,128)(2,1)S(1)}, u32[]{:S(2)}, u32[]{:S(2)}) %collective-permute-start.20) | collective-permute-done | bytes 147488 | tf_op jit(solution)/shard_map/ppermute | solution.py:978
  730.7 3.4 collective-permute-done.26
  735.7 24.9 %collective-permute-done.27 = bf16[208,768]{1,0:T(8,128)(2,1)S(1)} collective-permute-done((bf16[208,768]{1,0:T(8,128)(2,1)S(1)}, bf16[208,768]{1,0:T(8,128)(2,1)S(1)}, u32[]{:S(2)}, u32[]{:S(2)}) %collective-permute-start.27) | collective-permute-done | bytes 319520 | tf_op jit(solution)/shard_map/ppermute | solution.py:978
  (574 shorter events, 117.8 us)
Async XLA Ops:
  7.2 163.4 %all-gather.3.cloned.1.call-start = ((), (), s32[]{:S(2)}) async-start(), calls=%async_computation.2 | async-start | bytes 14598144 | tf_op jit(solution)/shard_map/all_gather | solution.py:1091
  12.6 281.2 %all-gather.5.cloned.1.call-start = ((), (), s32[]{:S(2)}) async-start(), calls=%async_computation.3 | async-start | bytes 9732096 | tf_op jit(solution)/shard_map/all_gather | solution.py:1091
  14.4 754.3 %reduce-scatter.5.cloned.1.call-start = ((), (), s32[]{:S(2)}) async-start(), calls=%async_computation.5 | async-start | bytes 9732096 | tf_op jit(solution)/shard_map/reduce_scatter | solution.py:1213
  14.8 12.2 %collective-permute-start.3 = (bf16[48,1536]{1,0:T(8,128)(2,1)S(1)}, bf16[48,1536]{1,0:T(8,128)(2,1)S(1)}, u32[]{:S(2)}, u32[]{:S(2)}) collective-permute-start(bf16[48,1536]{1,0:T(8,128)(2,1)S(1)} %bitcast.406), channel_id=1, source_target_pairs={{0,24},{1,25},{4,28},{5,29},{8,16},{9,17},{12,20},{13,21},{16,8},{... | collective-permute-start | bytes 442376 | tf_op jit(solution)/shard_map/ppermute | solution.py:978
  19.9 22.0 %collective-permute-start.2 = (bf16[48,1536]{1,0:T(8,128)(2,1)S(1)}, bf16[48,1536]{1,0:T(8,128)(2,1)S(1)}, u32[]{:S(2)}, u32[]{:S(2)}) collective-permute-start(bf16[48,1536]{1,0:T(8,128)(2,1)S(1)} %bitcast.407), channel_id=1, source_target_pairs={{0,16},{1,17},{4,20},{5,21},{8,24},{9,25},{12,28},{13,29},{16,0},{... | collective-permute-start | bytes 442376 | tf_op jit(solution)/shard_map/ppermute | solution.py:978
  19.9 22.0 %collective-permute-start.1 = (bf16[48,1536]{1,0:T(8,128)(2,1)S(1)}, bf16[48,1536]{1,0:T(8,128)(2,1)S(1)}, u32[]{:S(2)}, u32[]{:S(2)}) collective-permute-start(bf16[48,1536]{1,0:T(8,128)(2,1)S(1)} %bitcast.408), channel_id=1, source_target_pairs={{0,8},{1,9},{4,12},{5,13},{8,0},{9,1},{12,4},{13,5},{16,24},{17,25... | collective-permute-start | bytes 442376 | tf_op jit(solution)/shard_map/ppermute | solution.py:978
  22.0 223.8 %copy-start.135 = (f32[64]{0:T(128)}, f32[64]{0:T(128)S(1)}, u32[]{:S(2)}) copy-start(f32[64]{0:T(128)S(1)} %get-tuple-element.383) | copy-start | bytes 772
  22.0 225.1 %copy-start.139 = (f32[64]{0:T(128)}, f32[64]{0:T(128)S(1)}, u32[]{:S(2)}) copy-start(f32[64]{0:T(128)S(1)} %get-tuple-element.388) | copy-start | bytes 772
  27.0 385.0 %copy-start.125 = (f32[768]{0:T(1024)}, f32[768]{0:T(1024)S(1)}, u32[]{:S(2)}) copy-start(f32[768]{0:T(1024)S(1)} %add_abs_fusion) | copy-start | bytes 9220
  42.2 27.0 %collective-permute-start.6 = (bf16[4,48,1536]{2,1,0:T(8,128)(2,1)S(1)}, bf16[4,48,1536]{2,1,0:T(8,128)(2,1)S(1)}, u32[]{:S(2)}, u32[]{:S(2)}) collective-permute-start(bf16[4,48,1536]{2,1,0:T(8,128)(2,1)S(1)} %get-tuple-element.298), channel_id=1, source_target_pairs={{0,5},{1,4},{4,1},{5,0},{8,13},{9,12},{12,9},{13,8},{16,21},{17,20... | collective-permute-start | bytes 1769480 | tf_op jit(solution)/shard_map/ppermute | solution.py:978
  44.7 29.3 %collective-permute-start.5 = (bf16[4,48,1536]{2,1,0:T(8,128)(2,1)S(1)}, bf16[4,48,1536]{2,1,0:T(8,128)(2,1)S(1)}, u32[]{:S(2)}, u32[]{:S(2)}) collective-permute-start(bf16[4,48,1536]{2,1,0:T(8,128)(2,1)S(1)} %get-tuple-element.298), channel_id=1, source_target_pairs={{0,4},{1,5},{4,0},{5,1},{8,12},{9,13},{12,8},{13,9},{16,20},{17,21... | collective-permute-start | bytes 1769480 | tf_op jit(solution)/shard_map/ppermute | solution.py:978
  45.2 35.2 %collective-permute-start.4 = (bf16[4,48,1536]{2,1,0:T(8,128)(2,1)S(1)}, bf16[4,48,1536]{2,1,0:T(8,128)(2,1)S(1)}, u32[]{:S(2)}, u32[]{:S(2)}) collective-permute-start(bf16[4,48,1536]{2,1,0:T(8,128)(2,1)S(1)} %get-tuple-element.298), channel_id=1, source_target_pairs={{0,1},{1,0},{4,5},{5,4},{8,9},{9,8},{12,13},{13,12},{16,17},{17,16... | collective-permute-start | bytes 1769480 | tf_op jit(solution)/shard_map/ppermute | solution.py:978
  81.4 7.3 collective-permute-start.7
  82.2 9.7 %collective-permute-start = (bf16[16,768]{1,0:T(8,128)(2,1)S(1)}, bf16[16,768]{1,0:T(8,128)(2,1)S(1)}, u32[]{:S(2)}, u32[]{:S(2)}) collective-permute-start(bf16[16,768]{1,0:T(8,128)(2,1)S(1)} %slice.413), channel_id=1, source_target_pairs={{0,1},{1,2},{2,3},{3,4},{4,5},{5,6},{6,7},{7,8},{8,9},{9,10},{10,1... | collective-permute-start | bytes 73736 | tf_op jit(solution)/shard_map/ppermute | solution.py:1051
  92.8 27.4 %copy-start.151 = (f32[2,768]{1,0:T(2,128)S(1)}, f32[2,768]{1,0:T(2,128)}, u32[]{:S(2)}) copy-start(f32[2,768]{1,0:T(2,128)} %param.41) | copy-start | bytes 18436
  92.8 27.4 %copy-start.145 = (f32[2,2,768]{2,1,0:T(2,128)S(1)}, f32[2,2,768]{2,1,0:T(2,128)}, u32[]{:S(2)}) copy-start(f32[2,2,768]{2,1,0:T(2,128)} %param.44) | copy-start | bytes 36868
  92.8 27.4 %copy-start.131 = (f32[2,3072]{1,0:T(2,128)S(1)}, f32[2,3072]{1,0:T(2,128)}, u32[]{:S(2)}) copy-start(f32[2,3072]{1,0:T(2,128)} %param.45) | copy-start | bytes 73732
  113.3 38.5 %copy-start.11 = (bf16[1024,768]{1,0:T(8,128)(2,1)}, bf16[1024,768]{1,0:T(8,128)(2,1)S(1)}, u32[]{:S(2)}) copy-start(bf16[1024,768]{1,0:T(8,128)(2,1)S(1)} %get-tuple-element.96.gate_out) | copy-start | bytes 4718596
  113.3 36.7 %collective-permute-start.8 = (bf16[1024,768]{1,0:T(8,128)(2,1)S(1)}, bf16[1024,768]{1,0:T(8,128)(2,1)}, u32[]{:S(2)}, u32[]{:S(2)}) collective-permute-start(bf16[1024,768]{1,0:T(8,128)(2,1)S(1)} %get-tuple-element.94.signal), channel_id=1, source_target_pairs={{0,1},{1,2},{2,3},{3,4},{4,5},{5,6},{6,7},{7,8},{8,9},{9,10},{10,1... | collective-permute-start | bytes 4718600 | tf_op jit(solution)/shard_map/ppermute | solution.py:1051
  120.2 301.2 %copy-start.45 = (s32[52]{0:T(128)}, s32[52]{0:T(128)S(1)}, u32[]{:S(2)}) copy-start(s32[52]{0:T(128)S(1)} %concatenate.52.table) | copy-start | bytes 628
  120.2 31.6 %copy-start.40 = (f32[1,1,768]{2,1,0:T(1,128)}, f32[1,1,768]{2,1,0:T(1,128)S(1)}, u32[]{:S(2)}) copy-start(f32[1,1,768]{2,1,0:T(1,128)S(1)} %get-tuple-element.350.bias) | copy-start | bytes 9220
  175.7 42.7 %copy-start.148 = (f32[1,768]{1,0:T(1,128)S(1)}, f32[1,768]{1,0:T(1,128)}, u32[]{:S(2)}) copy-start(f32[1,768]{1,0:T(1,128)} %get-tuple-element.377) | copy-start | bytes 9220
  175.7 42.8 %copy-start.128 = (f32[3,768]{1,0:T(4,128)S(1)}, f32[3,768]{1,0:T(4,128)}, u32[]{:S(2)}) copy-start(f32[3,768]{1,0:T(4,128)} %get-tuple-element.256) | copy-start | bytes 27652
  213.3 8.4 %collective-permute-start.9 = (f32[16,768]{1,0:T(8,128)S(1)}, f32[16,768]{1,0:T(8,128)S(1)}, u32[]{:S(2)}, u32[]{:S(2)}) collective-permute-start(f32[16,768]{1,0:T(8,128)S(1)} %slice.443), channel_id=1, source_target_pairs={{0,1},{1,2},{2,3},{3,4},{4,5},{5,6},{6,7},{7,8},{8,9},{9,10},{10,1... | collective-permute-start | bytes 147464 | tf_op jit(solution)/shard_map/ppermute | solution.py:1051
  221.6 25.4 %copy-start.118 = (f32[2,64,768]{2,1,0:T(8,128)S(1)}, f32[2,64,768]{2,1,0:T(8,128)}, u32[]{:S(2)}) copy-start(f32[2,64,768]{2,1,0:T(8,128)} %param.40) | copy-start | bytes 1179652
  237.1 40.5 %copy-start.18 = (bf16[1024,768]{1,0:T(8,128)(2,1)}, bf16[1024,768]{1,0:T(8,128)(2,1)S(1)}, u32[]{:S(2)}) copy-start(bf16[1024,768]{1,0:T(8,128)(2,1)S(1)} %get-tuple-element.101.gate_out) | copy-start | bytes 4718596
  237.2 40.1 %collective-permute-start.10 = (bf16[1024,768]{1,0:T(8,128)(2,1)S(1)}, bf16[1024,768]{1,0:T(8,128)(2,1)S(1)}, u32[]{:S(2)}, u32[]{:S(2)}) collective-permute-start(bf16[1024,768]{1,0:T(8,128)(2,1)S(1)} %get-tuple-element.100.signal), channel_id=1, source_target_pairs={{0,1},{1,2},{2,3},{3,4},{4,5},{5,6},{6,7},{7,8},{8,9},{9,10},{10,1... | collective-permute-start | bytes 4718600 | tf_op jit(solution)/shard_map/ppermute | solution.py:1051
  251.7 25.6 %copy-start.89 = (bf16[128,768]{1,0:T(8,128)(2,1)S(1)}, bf16[128,768]{1,0:T(8,128)(2,1)}, u32[]{:S(2)}) copy-start(bf16[128,768]{1,0:T(8,128)(2,1)} %copy-done.88) | copy-start | bytes 589828
  299.4 31.6 %copy-start.52 = (bf16[1024,768]{1,0:T(8,128)(2,1)S(1)}, bf16[1024,768]{1,0:T(8,128)(2,1)}, u32[]{:S(2)}) copy-start(bf16[1024,768]{1,0:T(8,128)(2,1)} %grad.1) | copy-start | bytes 4718596
  372.5 397.4 %reduce-scatter.3.cloned.1.call-start = ((), (), s32[]{:S(2)}) async-start(), calls=%async_computation.4 | async-start | bytes 14598144 | tf_op jit(solution)/shard_map/reduce_scatter | solution.py:1213
  383.5 37.5 %collective-permute-start.11 = (bf16[1024,768]{1,0:T(8,128)(2,1)S(1)}, bf16[1024,768]{1,0:T(8,128)(2,1)S(1)}, u32[]{:S(2)}, u32[]{:S(2)}) collective-permute-start(bf16[1024,768]{1,0:T(8,128)(2,1)S(1)} %get-tuple-element.111.grads), channel_id=1, source_target_pairs={{1,0},{2,1},{3,2},{4,3},{5,4},{6,5},{7,6},{8,7},{9,8},{10,9},{11,1... | collective-permute-start | bytes 4718600 | tf_op jit(solution)/shard_map/ppermute | solution.py:1054
  435.4 10.8 %collective-permute-start.12 = (bf16[3,16,768]{2,1,0:T(8,128)(2,1)S(1)}, bf16[3,16,768]{2,1,0:T(8,128)(2,1)S(1)}, u32[]{:S(2)}, u32[]{:S(2)}) collective-permute-start(bf16[3,16,768]{2,1,0:T(8,128)(2,1)S(1)} %pad_maximum_fusion.22), channel_id=1, source_target_pairs={{1,0},{2,1},{3,2},{4,3},{5,4},{6,5},{7,6},{8,7},{9,8},{10,9},{11,1... | collective-permute-start | bytes 221192 | tf_op jit(solution)/shard_map/ppermute | solution.py:1054
  484.8 44.3 %slice-start = ((s8[4718592]{0:T(1024)(128)(4,1)}), s8[4194304]{0:T(1024)(128)(4,1)S(1)}, s32[]{:S(2)}) async-start(s8[4718592]{0:T(1024)(128)(4,1)} %bitcast.373), calls=%async_computation.6 | async-start | bytes 8388608
  490.4 38.7 %slice-start.1 = ((s8[4718592]{0:T(1024)(128)(4,1)}), s8[524288]{0:T(1024)(128)(4,1)S(1)}, s32[]{:S(2)}) async-start(s8[4718592]{0:T(1024)(128)(4,1)} %bitcast.373), calls=%async_computation.7 | async-start | bytes 1048576
  490.4 38.7 %copy-start.12 = (bf16[1024,768]{1,0:T(8,128)(2,1)S(1)}, bf16[1024,768]{1,0:T(8,128)(2,1)}, u32[]{:S(2)}) copy-start(bf16[1024,768]{1,0:T(8,128)(2,1)} %copy-done.11) | copy-start | bytes 4718596
  490.4 38.7 %copy-start.14 = (bf16[1024,768]{1,0:T(8,128)(2,1)S(1)}, bf16[1024,768]{1,0:T(8,128)(2,1)}, u32[]{:S(2)}) copy-start(bf16[1024,768]{1,0:T(8,128)(2,1)} %copy-done.13) | copy-start | bytes 4718596
  536.0 38.1 %collective-permute-start.13 = (bf16[1024,768]{1,0:T(8,128)(2,1)}, bf16[1024,768]{1,0:T(8,128)(2,1)}, u32[]{:S(2)}, u32[]{:S(2)}) collective-permute-start(bf16[1024,768]{1,0:T(8,128)(2,1)} %get-tuple-element.129.grads), channel_id=1, source_target_pairs={{1,0},{2,1},{3,2},{4,3},{5,4},{6,5},{7,6},{8,7},{9,8},{10,9},{11,1... | collective-permute-start | bytes 4718600 | tf_op jit(solution)/shard_map/ppermute | solution.py:1054
  577.0 28.3 %copy-start.25 = (s32[1040,128]{1,0:T(8,128)S(1)}, s32[1040,128]{1,0:T(8,128)}, u32[]{:S(2)}) copy-start(s32[1040,128]{1,0:T(8,128)} %copy-done.22) | copy-start | bytes 1597444
  577.0 28.3 %copy-start.31 = (f32[2,3,1152]{2,1,0:T(4,128)S(1)}, f32[2,3,1152]{2,1,0:T(4,128)}, u32[]{:S(2)}) copy-start(f32[2,3,1152]{2,1,0:T(4,128)} %copy-done.30) | copy-start | bytes 82948
  577.0 28.3 %copy-start.37 = (f32[2,768]{1,0:T(2,128)S(1)}, f32[2,768]{1,0:T(2,128)}, u32[]{:S(2)}) copy-start(f32[2,768]{1,0:T(2,128)} %copy-done.36) | copy-start | bytes 18436
  577.0 28.3 %copy-start.76 = (bf16[1024,768]{1,0:T(8,128)(2,1)S(1)}, bf16[1024,768]{1,0:T(8,128)(2,1)}, u32[]{:S(2)}) copy-start(bf16[1024,768]{1,0:T(8,128)(2,1)} %copy-done.75) | copy-start | bytes 4718596
  591.0 14.4 %collective-permute-start.14 = (bf16[3,16,768]{2,1,0:T(8,128)(2,1)S(1)}, bf16[3,16,768]{2,1,0:T(8,128)(2,1)S(1)}, u32[]{:S(2)}, u32[]{:S(2)}) collective-permute-start(bf16[3,16,768]{2,1,0:T(8,128)(2,1)S(1)} %pad_maximum_fusion.23), channel_id=1, source_target_pairs={{1,0},{2,1},{3,2},{4,3},{5,4},{6,5},{7,6},{8,7},{9,8},{10,9},{11,1... | collective-permute-start | bytes 221192 | tf_op jit(solution)/shard_map/ppermute | solution.py:1054
  605.4 45.9 %copy-start.124 = (bf16[2,64,64]{2,1,0:T(8,128)(2,1)S(1)}, bf16[2,64,64]{2,1,0:T(8,128)(2,1)}, u32[]{:S(2)}) copy-start(bf16[2,64,64]{2,1,0:T(8,128)(2,1)} %pad_add_fusion.1) | copy-start | bytes 49156
  605.4 45.9 %copy-start.129 = (bf16[33,64]{1,0:T(8,128)(2,1)S(1)}, bf16[33,64]{1,0:T(8,128)(2,1)}, u32[]{:S(2)}) copy-start(bf16[33,64]{1,0:T(8,128)(2,1)} %fusion.37) | copy-start | bytes 12676
  605.4 45.9 %copy-start.152 = (bf16[3,64]{1,0:T(4,128)(2,1)S(1)}, bf16[3,64]{1,0:T(4,128)(2,1)}, u32[]{:S(2)}) copy-start(bf16[3,64]{1,0:T(4,128)(2,1)} %pad_add_fusion.5) | copy-start | bytes 1156
  605.4 45.9 %copy-start.153 = (bf16[3,64]{1,0:T(4,128)(2,1)S(1)}, bf16[3,64]{1,0:T(4,128)(2,1)}, u32[]{:S(2)}) copy-start(bf16[3,64]{1,0:T(4,128)(2,1)} %pad_add_fusion.4) | copy-start | bytes 1156
  605.4 46.0 %copy-start.39 = (f32[2,1,384]{2,1,0:T(1,128)S(1)}, f32[2,1,384]{2,1,0:T(1,128)}, u32[]{:S(2)}) copy-start(f32[2,1,384]{2,1,0:T(1,128)} %copy-done.38) | copy-start | bytes 9220
  605.4 47.2 %copy-start.33 = (f32[4,1,768]{2,1,0:T(1,128)S(1)}, f32[4,1,768]{2,1,0:T(1,128)}, u32[]{:S(2)}) copy-start(f32[4,1,768]{2,1,0:T(1,128)} %copy-done.32) | copy-start | bytes 36868
  605.4 47.3 %copy-start.35 = (f32[2,1,1152]{2,1,0:T(1,128)S(1)}, f32[2,1,1152]{2,1,0:T(1,128)}, u32[]{:S(2)}) copy-start(f32[2,1,1152]{2,1,0:T(1,128)} %copy-done.34) | copy-start | bytes 27652
  605.4 47.9 %copy-start.29 = (f32[2,3,1152]{2,1,0:T(4,128)S(1)}, f32[2,3,1152]{2,1,0:T(4,128)}, u32[]{:S(2)}) copy-start(f32[2,3,1152]{2,1,0:T(4,128)} %copy-done.28) | copy-start | bytes 82948
  605.5 48.0 %copy-start.27 = (f32[2,8,768]{2,1,0:T(8,128)S(1)}, f32[2,8,768]{2,1,0:T(8,128)}, u32[]{:S(2)}) copy-start(f32[2,8,768]{2,1,0:T(8,128)} %copy-done.26) | copy-start | bytes 147460
  641.3 14.2 %collective-permute-start.15 = (bf16[2,384,1536]{2,1,0:T(8,128)(2,1)}, bf16[2,384,1536]{2,1,0:T(8,128)(2,1)}, u32[]{:S(2)}, u32[]{:S(2)}) collective-permute-start(bf16[2,384,1536]{2,1,0:T(8,128)(2,1)} %get-tuple-element.140), channel_id=1, source_target_pairs={{0,2},{2,0},{1,3},{3,1},{4,6},{6,4},{5,7},{7,5},{8,10},{10,8},{9,1... | collective-permute-start | bytes 7077896 | tf_op jit(solution)/shard_map/ppermute | solution.py:981
  659.7 25.7 %collective-permute-start.18 = (bf16[4,48,1536]{2,1,0:T(8,128)(2,1)}, bf16[4,48,1536]{2,1,0:T(8,128)(2,1)S(1)}, u32[]{:S(2)}, u32[]{:S(2)}) collective-permute-start(bf16[4,48,1536]{2,1,0:T(8,128)(2,1)} %get-tuple-element.266), channel_id=1, source_target_pairs={{0,5},{1,4},{4,1},{5,0},{8,13},{9,12},{12,9},{13,8},{16,21},{17,20... | collective-permute-start | bytes 1769480 | tf_op jit(solution)/shard_map/ppermute | solution.py:978
  665.6 44.9 %collective-permute-start.17 = (bf16[4,48,1536]{2,1,0:T(8,128)(2,1)}, bf16[4,48,1536]{2,1,0:T(8,128)(2,1)}, u32[]{:S(2)}, u32[]{:S(2)}) collective-permute-start(bf16[4,48,1536]{2,1,0:T(8,128)(2,1)} %get-tuple-element.267), channel_id=1, source_target_pairs={{0,4},{1,5},{4,0},{5,1},{8,12},{9,13},{12,8},{13,9},{16,20},{17,21... | collective-permute-start | bytes 1769480 | tf_op jit(solution)/shard_map/ppermute | solution.py:978
  665.6 44.9 %collective-permute-start.16 = (bf16[4,48,1536]{2,1,0:T(8,128)(2,1)}, bf16[4,48,1536]{2,1,0:T(8,128)(2,1)}, u32[]{:S(2)}, u32[]{:S(2)}) collective-permute-start(bf16[4,48,1536]{2,1,0:T(8,128)(2,1)} %get-tuple-element.265), channel_id=1, source_target_pairs={{0,1},{1,0},{4,5},{5,4},{8,9},{9,8},{12,13},{13,12},{16,17},{17,16... | collective-permute-start | bytes 1769480 | tf_op jit(solution)/shard_map/ppermute | solution.py:978
  672.3 1.7 collective-permute-start.22
  674.0 41.4 %collective-permute-start.25 = (bf16[208,768]{1,0:T(8,128)(2,1)S(1)}, bf16[208,768]{1,0:T(8,128)(2,1)S(1)}, u32[]{:S(2)}, u32[]{:S(2)}) collective-permute-start(bf16[208,768]{1,0:T(8,128)(2,1)S(1)} %add_convert_fusion.3), channel_id=1, source_target_pairs={{0,5},{1,4},{4,1},{5,0},{8,13},{9,12},{12,9},{13,8},{16,21},{17,20... | collective-permute-start | bytes 958472 | tf_op jit(solution)/shard_map/ppermute | solution.py:978
  677.0 40.0 %collective-permute-start.24 = (bf16[208,768]{1,0:T(8,128)(2,1)S(1)}, bf16[208,768]{1,0:T(8,128)(2,1)S(1)}, u32[]{:S(2)}, u32[]{:S(2)}) collective-permute-start(bf16[208,768]{1,0:T(8,128)(2,1)S(1)} %add_convert_fusion.3), channel_id=1, source_target_pairs={{0,4},{1,5},{4,0},{5,1},{8,12},{9,13},{12,8},{13,9},{16,20},{17,21... | collective-permute-start | bytes 958472 | tf_op jit(solution)/shard_map/ppermute | solution.py:978
  685.5 31.6 %collective-permute-start.23 = (bf16[208,768]{1,0:T(8,128)(2,1)S(1)}, bf16[208,768]{1,0:T(8,128)(2,1)S(1)}, u32[]{:S(2)}, u32[]{:S(2)}) collective-permute-start(bf16[208,768]{1,0:T(8,128)(2,1)S(1)} %add_convert_fusion.3), channel_id=1, source_target_pairs={{0,1},{1,0},{4,5},{5,4},{8,9},{9,8},{12,13},{13,12},{16,17},{17,16... | collective-permute-start | bytes 958472 | tf_op jit(solution)/shard_map/ppermute | solution.py:978
  712.2 10.0 %collective-permute-start.21 = (bf16[48,1536]{1,0:T(8,128)(2,1)S(1)}, bf16[48,1536]{1,0:T(8,128)(2,1)S(1)}, u32[]{:S(2)}, u32[]{:S(2)}) collective-permute-start(bf16[48,1536]{1,0:T(8,128)(2,1)S(1)} %get-tuple-element.295), channel_id=1, source_target_pairs={{0,24},{1,25},{4,28},{5,29},{8,16},{9,17},{12,20},{13,21},{16,8},{... | collective-permute-start | bytes 442376 | tf_op jit(solution)/shard_map/ppermute | solution.py:978
  715.4 15.3 %collective-permute-start.20 = (bf16[48,1536]{1,0:T(8,128)(2,1)S(1)}, bf16[48,1536]{1,0:T(8,128)(2,1)S(1)}, u32[]{:S(2)}, u32[]{:S(2)}) collective-permute-start(bf16[48,1536]{1,0:T(8,128)(2,1)S(1)} %get-tuple-element.296), channel_id=1, source_target_pairs={{0,16},{1,17},{4,20},{5,21},{8,24},{9,25},{12,28},{13,29},{16,0},{... | collective-permute-start | bytes 442376 | tf_op jit(solution)/shard_map/ppermute | solution.py:978
  715.4 15.3 %collective-permute-start.19 = (bf16[48,1536]{1,0:T(8,128)(2,1)S(1)}, bf16[48,1536]{1,0:T(8,128)(2,1)S(1)}, u32[]{:S(2)}, u32[]{:S(2)}) collective-permute-start(bf16[48,1536]{1,0:T(8,128)(2,1)S(1)} %get-tuple-element.294), channel_id=1, source_target_pairs={{0,8},{1,9},{4,12},{5,13},{8,0},{9,1},{12,4},{13,5},{16,24},{17,25... | collective-permute-start | bytes 442376 | tf_op jit(solution)/shard_map/ppermute | solution.py:978
  717.4 16.7 %collective-permute-start.26 = (bf16[208,768]{1,0:T(8,128)(2,1)S(1)}, bf16[208,768]{1,0:T(8,128)(2,1)S(1)}, u32[]{:S(2)}, u32[]{:S(2)}) collective-permute-start(bf16[208,768]{1,0:T(8,128)(2,1)S(1)} %fusion.32), channel_id=1, source_target_pairs={{0,8},{1,9},{4,12},{5,13},{8,0},{9,1},{12,4},{13,5},{16,24},{17,25... | collective-permute-start | bytes 958472 | tf_op jit(solution)/shard_map/ppermute | solution.py:978
  734.2 26.3 %collective-permute-start.27 = (bf16[208,768]{1,0:T(8,128)(2,1)S(1)}, bf16[208,768]{1,0:T(8,128)(2,1)S(1)}, u32[]{:S(2)}, u32[]{:S(2)}) collective-permute-start(bf16[208,768]{1,0:T(8,128)(2,1)S(1)} %add_convert_fusion.1), channel_id=1, source_target_pairs={{0,16},{1,17},{4,20},{5,21},{8,24},{9,25},{12,28},{13,29},{16,0},{... | collective-permute-start | bytes 958472 | tf_op jit(solution)/shard_map/ppermute | solution.py:978
  (135 other events, 1173.5 us)
Sparse Core Ops, SparseCore 0:
  12.7 122.8 all-gather.2
  139.0 84.0 all-gather.4
  372.6 137.9 reduce-scatter.4
  537.4 221.8 reduce-scatter.2

commit v4 on v3

--- a/solution.py
+++ b/solution.py
@@ -962,9 +962,7 @@
     owners = ("tensor", "chip", "core")
     hops = -(-(LMAX - 1) // rows)
     direct = width % LANES == 0 and hidden % HIDDEN == 0
-    per = width // LANES if direct else D // LANES
-    hidden_per = hidden // HIDDEN if direct else FF // HIDDEN
-    halves = tensor_count if direct else 1
+    per, hidden_per = D // LANES, FF // HIDDEN
     paired = (
         direct and depth % 16 == 0 and cores == 2 and tensor_count == 2
         and chips > 1 and chips & (chips - 1) == 0
@@ -1009,7 +1007,32 @@
             total += pick(held, k ^ mine).astype(f32)
         return total
 
-    def reduce_plane(total):
+    def both_sides(values):
+        other = swap(values, 1)
+        first, second = jnp.where(side == 0, values, other), jnp.where(side == 0, other, values)
+        return jnp.concatenate([first, second], axis=1)
+
+    def gather_rows(values):
+        return lax.all_gather(values, ("chip", "core"), axis=0, tiled=True)[None]
+
+    def reduce_rows(values, sizes):
+        values = lax.psum_scatter(
+            values.reshape(D, -1), ("chip", "core"), scatter_dimension=0, tiled=True
+        )
+        kept, sent, at = [], [], 0
+        for size in sizes:
+            half = size // 2
+            for held, which in ((kept, side), (sent, 1 - side)):
+                held.append(lax.dynamic_slice_in_dim(values, at + which * half, half, axis=1))
+            at += size
+        other = swap(jnp.concatenate(sent, axis=1), 1).astype(f32)
+        result, at = [], 0
+        for part in kept:
+            result.append(part.astype(f32) + other[:, at : at + part.shape[1]])
+            at += part.shape[1]
+        return result
+
+    def reduce_plane(total, beside):
         total = total.reshape(2, planes, 2, depth, -1)
 
         def block(s, r):
@@ -1019,12 +1042,13 @@
         total = block(side, row).astype(f32)
         for part in parts:
             total += part.astype(f32)
+        total, beside = lax.optimization_barrier((total, beside))
         low = total.astype(bf16)
         parts = [swap(pick(low, plane ^ k), k << 2) for k in range(1, planes)]
         total = pick(total, plane)
         for part in parts:
             total += part.astype(f32)
-        return total
+        return total, beside
 
     def reduce_all(extra):
         def rounded(values):
@@ -1072,8 +1096,8 @@
         mixes = [strided(mix, mix_blocks, 4, k) for k in range(4)]
         return mixes[:3], mixes[3], *[strided(ff, ff_blocks, 2, k) for k in range(2)]
 
-    local_mix = per if direct else 1
-    local_ff = hidden_per if direct else 1
+    local_mix = width // LANES if paired else 1
+    local_ff = hidden // HIDDEN if paired else 1
     local = []
     for layer in range(LAYERS):
         local.append(
@@ -1115,26 +1139,27 @@
 
     gathered = []
     if paired:
-        shared = gather(jnp.concatenate([local[0][1], local[1][0]], axis=1))
-        last = gather(local[1][1])
+        shared = gather_rows(
+            jnp.concatenate([both_sides(local[0][1]), both_sides(local[1][0])], axis=1)
+        )
+        last = gather_rows(both_sides(local[1][1]))
         inner, filter_back, kernel_spectra = filters[0]
         mix, kernel_spectra = gather_pairs(local[0][0], kernel_spectra)
         filters[0] = (inner, filter_back, kernel_spectra)
-        gathered.append((mix, 0, shared))
-        gathered.append((shared[:, :, 2 * hidden :], 0, last))
+        gathered.append((mix, width // LANES, shared))
+        gathered.append((shared[:, :, 2 * FF :], per, last))
     else:
         for mix, ff in local:
             mix, ff = gather(mix), gather(ff)
-            if not direct:
-                ins, out, up, down = part_columns(mix, ff, local_mix, local_ff)
-
-                def full(piece):
-                    return jnp.transpose(piece, (1, 0, 2)).reshape(1, D, -1)
-
-                mix, ff = join_columns(
-                    [full(k) for k in ins], full(out), full(up), full(down), per, hidden_per
-                )
-            gathered.append((mix, 0, ff))
+            ins, out, up, down = part_columns(mix, ff, local_mix, local_ff)
+
+            def full(piece):
+                return jnp.transpose(piece, (1, 0, 2)).reshape(1, D, -1)
+
+            mix, ff = join_columns(
+                [full(k) for k in ins], full(out), full(up), full(down), per, hidden_per
+            )
+            gathered.append((mix, per, ff))
 
     numbers = jnp.arange(count, dtype=jnp.int32)
     match = deal_order[:, None] == numbers[None, :]
@@ -1173,13 +1198,13 @@
     kept = []
     outputs = []
     for layer in range(LAYERS):
-        mix_weights, first, ff_weights = gathered[layer]
+        mix_weights, mix_per, ff_weights = gathered[layer]
         first_norm = jnp.stack([norm_gains[layer, 0], norm_biases[layer, 0]])
         second_norm = jnp.stack([norm_gains[layer, 1], norm_biases[layer, 1]])
         taps = by_block(short_taps[layer])
         lane_bias = conv_bias[layer].reshape(D // CONV_LANES, 1, CONV_LANES)
         shared_in = (
-            first_norm, mix_weights, first, per, by_block(input_bias[layer][None]), taps
+            first_norm, mix_weights, 0, mix_per, by_block(input_bias[layer][None]), taps
         )
         near = from_before(state[rows - HALO :])
         normed, projected, gate_out, gate_in, values, signal = in_forward(
@@ -1191,8 +1216,8 @@
             table, window, filters[layer][2], gate_out, lane_bias, rows, tables
         )
         middle, second, activated, slope, result, result_low = ff_forward(
-            mixer, state, second_norm, output_biases[layer], ff_weights, per, hidden_per,
-            up_projection_bias[layer].reshape(FF // HIDDEN, 1, HIDDEN), mix_weights, first,
+            mixer, state, second_norm, output_biases[layer], ff_weights, mix_per, hidden_per,
+            up_projection_bias[layer].reshape(FF // HIDDEN, 1, HIDDEN), mix_weights, 0,
         )
         outputs.append(result_low)
         kept.append(
@@ -1205,7 +1230,7 @@
 
     grad = out_grad
     owned, owned_ff = {}, {}
-    ff_columns = 2 * FF // halves
+    ff_columns = 2 * FF
     shared = None
     small = [None] * LAYERS
 
@@ -1216,20 +1241,20 @@
 
     for layer in reversed(range(LAYERS)):
         joint = paired and layer == LAYERS - 1
-        mix_columns = 4 * D // halves + (ff_columns if joint else 0)
+        mix_columns = 4 * LANES * gathered[layer][1] + (ff_columns if joint else 0)
         mix_first = ff_columns // (4 * LANES) if joint else 0
         (
             state, first_norm, second_norm, taps, lane_bias, normed, projected, gate_out,
             gate_in, values, signal, window, carried, mixer, middle, second, activated, slope,
         ) = kept[layer]
-        mix_weights, first, ff_weights = gathered[layer]
+        mix_weights, mix_per, ff_weights = gathered[layer]
         inner, filter_back, kernel_spectra = filters[layer]
         middle_grad, middle_low, ff_grad, up_bias_grad, ff_sums = ff_backward(
             0, place, grad, second, middle, second_norm, activated, slope, ff_weights, hidden_per,
             shared,
         )
         carried_grad, gate_grad, conv_bias_grad = gates_backward(
-            middle_low, mix_weights, first, per, gate_out, carried, signal
+            middle_low, mix_weights, 0, mix_per, gate_out, carried, signal
         )
         ahead = [from_after(carried_grad, hop) for hop in range(1, hops + 1)]
         kernel_grad = kernel_backward(table, window, carried_grad, rows, tables)
@@ -1237,8 +1262,8 @@
         filter_out_grad = jnp.dot(jnp.transpose(inner), shaped, precision=highest)
         inner_grad = jnp.dot(shaped, jnp.transpose(filter_out[layer]), precision=highest)
         filter_grads = filter_back(inner_grad)
-        ahead, filter_grads, filter_out_grad = lax.optimization_barrier(
-            (ahead, filter_grads, filter_out_grad)
+        ahead, filter_grads, filter_out_grad, owned_ff = lax.optimization_barrier(
+            (ahead, filter_grads, filter_out_grad, owned_ff)
         )
         grads_window = jnp.concatenate([carried_grad] + ahead + [blank])
         gate_in_grad, values_grad = signal_backward(
@@ -1248,12 +1273,12 @@
         after = from_after(jnp.stack([part[:HALO] for part in mixed_grads]))
         grad, grad_low, in_bias_grad, taps_grad, in_sums, *mix_grad = in_backward(
             0 if joint else split, place, mixed_grads, after, age, projected, taps, normed, middle_low, mixer,
-            mix_weights, first, per, state, middle_grad, first_norm, mix_columns, mix_first,
+            mix_weights, 0, mix_per, state, middle_grad, first_norm, mix_columns, mix_first,
         )
 
         if len(mix_grad) == 1:
             mix_grad = mix_grad[0]
-        if not direct:
+        if not paired:
             ins, out, up, down = part_columns(mix_grad, ff_grad, per, hidden_per)
 
             def by_owner(piece):
@@ -1267,12 +1292,10 @@
         if not paired:
             owned[layer], owned_ff[layer] = share(mix_grad), share(ff_grad)
         elif layer == LAYERS - 1:
-            owned_ff[layer] = share(ff_grad)
+            owned_ff[layer] = reduce_rows(ff_grad, [ff_columns])[0]
             shared = mix_grad
         else:
-            both = share(ff_grad)
-            owned_ff[layer] = both[:, :ff_columns]
-            owned[layer + 1] = both[:, ff_columns:]
+            owned_ff[layer], owned[layer + 1] = reduce_rows(ff_grad, [ff_columns, 4 * D])
             last_grads = mix_grad
 
         ff_sums = jnp.sum(ff_sums, axis=1)
@@ -1306,7 +1329,8 @@
         keep, send = last_grads
         total = (keep.astype(f32) + swap_core(send).astype(f32)).astype(bf16)
         flat, _ = lax.optimization_barrier((flat, total))
-        owned[0] = reduce_plane(total)
+        beside = (owned_ff[0], owned[1])
+        owned[0], (owned_ff[0], owned[1]) = reduce_plane(total, beside)
     flat = reduce_all(flat)
     found = [[None] * 12 for _ in range(LAYERS)]
     offset = 0

time: 787 us -> 758 us (0.963)
  waiting for transfers between devices: 198 us -> 166 us
  starting transfers between devices: 60 us -> 69.9 us
    ppermute x17 -> x22, waiting for transfers between devices: 115 us -> 83.4 us  [swap(): return lax.ppermute(values, ('chip', 'tensor'), pairs)]
    ppermute x17 -> x22, starting transfers between devices: 26.6 us -> 44.8 us  [swap(): return lax.ppermute(values, ('chip', 'tensor'), pairs)]
    ppermute x3, starting transfers between devices: 8.31 us -> 0.29 us  [swap_core(): return lax.ppermute(values, 'core', [(0, 1), (1, 0)])]
    unnamed x350 -> x334, local copies, waits for them, and re-layouts: 64.3 us -> 69.9 us
  transfers between devices with their start and end apart: 32 -> 37, of which waited for: 18 -> 22; matrix products, arithmetic and copies ran while one was open for 13% -> 12% of each run, Pallas kernels for 33% -> 35%
where the time goes in v4:
time: 758 us; the launch traced here: 753 us
  Pallas kernels  333 us (44%)
  waiting for transfers between devices  166 us (22%)
  local copies, waits for them, and re-layouts  83.5 us (11%)
  starting transfers between devices  69.9 us (9%)
  matrix products  49.3 us (7%)
  other arithmetic  33.2 us (4%)
  between operations  18.4 us (2%)
    pallas_call x16, Pallas kernels, run(): pl.pallas_call(body, out_shape=shapes, grid_spec=pltpu.PrefetchScalarGrid...  333 us
    ppermute x22, waiting for transfers between devices, swap(): return lax.ppermute(values, ('chip', 'tensor'), pairs)  83.4 us
    unnamed x334, local copies, waits for them, and re-layouts  69.9 us
    ppermute x4, waiting for transfers between devices, from_before(): lax.ppermute(values, everyone, [(i, i + hop) for i in range(devices - hop)])  55.7 us
    ppermute x22, starting transfers between devices, swap(): return lax.ppermute(values, ('chip', 'tensor'), pairs)  44.8 us
    ppermute x4, waiting for transfers between devices, from_after(): lax.ppermute(values, everyone, [(i + hop, i) for i in range(devices - hop)])  22.6 us
    ppermute x4, starting transfers between devices, from_before(): lax.ppermute(values, everyone, [(i, i + hop) for i in range(devices - hop)])  18.9 us
  transfers between devices with their start and end apart: 37, of which 22 were waited for; matrix products, arithmetic and copies ran while one was open for 12% of the time, Pallas kernels for 35%

profile of v4, /device:TPU:0, one launch (start us, length us, event | category | flops | bytes accessed | tf_op | source)
XLA Modules:
  0.0 753.1 jit_solution(6175180808080229387)
XLA Ops:
  9.5 3.0 collective-permute-start.10
  13.8 3.0 collective-permute-done.10
  16.8 5.9 collective-permute-done.9
  23.9 3.9 collective-permute-start.3
  31.3 6.0 collective-permute-done.13
  44.3 2.9 collective-permute-done.2
  51.0 3.8 multiply_convert_fusion.1
  54.9 3.6 convolution_bitcast_fusion.1.kernel
  58.5 6.2 collective-permute-done.6
  64.7 6.6 collective-permute-done.5
  73.1 3.7 collective-permute-start
  82.3 14.7 %in_forward.2 = (bf16[1024,768]{1,0:T(8,128)(2,1)S(1)}, bf16[3,1040,768]{2,1,0:T(8,128)(2,1)S(1)}, bf16[1024,768]{1,0:T(8,128)(2,1)S(1)}, bf16[1024,768]{1,0:T(8...) custom-call(bf16[1024,768]{1,0:T(8,128)(2,1)S(1)} %copy-done.38, ...), custom_call_target="tpu_custom_call" | custom-call | flops 3623878656 | bytes 20000000 | tf_op jit(solution)/shard_map/in_forward/pallas_call | solution.py:700
  102.8 4.0 collective-permute-start.8
  109.5 30.1 %collective-permute-done.8 = bf16[1024,768]{1,0:T(8,128)(2,1)} collective-permute-done((bf16[1024,768]{1,0:T(8,128)(2,1)S(1)}, bf16[1024,768]{1,0:T(8,128)(2,1)}, u32[]{:S(2)}, u32[]{:S(2)}) %collective-permute-start.8) | collective-permute-done | bytes 1572896 | tf_op jit(solution)/shard_map/ppermute | solution.py:1075
  141.5 2.8 copy-done.6
  144.3 11.2 %conv_forward.2 = (bf16[1024,768]{1,0:T(8,128)(2,1)S(1)}, bf16[1024,768]{1,0:T(8,128)(2,1)S(1)}) custom-call(s32[52]{0:T(128)S(1)} %concatenate.58.table, bf16[2176,768]{1,0:T(8,128)(2,1)S(1)} %fusion.window, f32[8,256,768]{2,1,0:T(8,128)S(1)} %copy-done.6, bf16[1024,768]{1,0:T(8,128)(2,1)S(1)} %get-tuple-element.100.gate_out, ...), custom_call_target="tpu_custom_call" | custom-call | flops 20000000000 | bytes 20000000 | tf_op jit(solution)/shard_map/conv_forward/pallas_call | solution.py:700
  159.5 2.3 copy-done.1
  164.6 30.5 %ff_forward.2 = (f32[1024,768]{1,0:T(8,128)S(1)}, bf16[1024,768]{1,0:T(8,128)(2,1)S(1)}, bf16[1024,3072]{1,0:T(8,128)(2,1)S(1)}, bf16[1024,3072]{1,0:T(8,128)(2,...) custom-call(bf16[1024,768]{1,0:T(8,128)(2,1)S(1)} %copy-done.70, bf16[1024,768]{1,0:T(8,128)(2,1)S(1)} %copy-done.39, ...), custom_call_target="tpu_custom_call" | custom-call | flops 10871635968 | bytes 40000000 | tf_op jit(solution)/shard_map/ff_forward/pallas_call | solution.py:700
  195.1 2.6 copy-done.68
  202.2 8.1 %collective-permute-start.11 = (f32[16,768]{1,0:T(8,128)S(1)}, f32[16,768]{1,0:T(8,128)S(1)}, u32[]{:S(2)}, u32[]{:S(2)}) collective-permute-start(f32[16,768]{1,0:T(8,128)S(1)} %slice.443), channel_id=1, source_target_pairs={{0,1},{1,2},{2,3},{3,4},{4,5},{5,6},{6,7},{7,8},{8,9},{9,10},{10,1... | collective-permute-start | bytes 147464 | tf_op jit(solution)/shard_map/ppermute | solution.py:1075
  210.5 2.8 slice.540.weight.refs_0_.refs_1_
  213.9 15.0 %in_forward.3 = (bf16[1024,768]{1,0:T(8,128)(2,1)S(1)}, bf16[3,1040,768]{2,1,0:T(8,128)(2,1)S(1)}, bf16[1024,768]{1,0:T(8,128)(2,1)S(1)}, bf16[1024,768]{1,0:T(8...) custom-call(f32[1024,768]{1,0:T(8,128)S(1)} %copy-done.36, ...), custom_call_target="tpu_custom_call" | custom-call | flops 3623878656 | bytes 20000000 | tf_op jit(solution)/shard_map/in_forward/pallas_call | solution.py:700
  232.2 3.1 collective-permute-start.12
  238.5 3.9 multiply_convert_fusion
  243.5 25.6 %collective-permute-done.12 = bf16[1024,768]{1,0:T(8,128)(2,1)S(1)} collective-permute-done((bf16[1024,768]{1,0:T(8,128)(2,1)S(1)}, bf16[1024,768]{1,0:T(8,128)(2,1)S(1)}, u32[]{:S(2)}, u32[]{:S(2)}) %collective-permute-start.12) | collective-permute-done | bytes 1572896 | tf_op jit(solution)/shard_map/ppermute | solution.py:1075
  269.4 11.4 %conv_forward.3 = (bf16[1024,768]{1,0:T(8,128)(2,1)S(1)}, bf16[1024,768]{1,0:T(8,128)(2,1)S(1)}) custom-call(s32[52]{0:T(128)S(1)} %concatenate.58.table, bf16[2176,768]{1,0:T(8,128)(2,1)S(1)} %fusion.1.window, f32[8,256,768]{2,1,0:T(8,128)S(1)} %convolution_bitcast_fusion.kernel, bf16[1024,768]{1,0:T(8,128)(2,1)S(1)} %get-tuple-element.105.gate_out, ...), custom_call_target="tpu_custom_call" | custom-call | flops 20000000000 | bytes 20000000 | tf_op jit(solution)/shard_map/conv_forward/pallas_call | solution.py:700
  285.0 2.3 copy-done.4
  290.6 31.6 %ff_forward.3 = (f32[1024,768]{1,0:T(8,128)S(1)}, bf16[1024,768]{1,0:T(8,128)(2,1)S(1)}, bf16[1024,3072]{1,0:T(8,128)(2,1)}, bf16[1024,3072]{1,0:T(8,128)(2,1)},...) custom-call(bf16[1024,768]{1,0:T(8,128)(2,1)S(1)} %copy-done.61, f32[1024,768]{1,0:T(8,128)S(1)} %copy-done.37, ...), custom_call_target="tpu_custom_call" | custom-call | flops 10871635968 | bytes 40000000 | tf_op jit(solution)/shard_map/ff_forward/pallas_call | solution.py:700
  322.2 38.5 %ff_backward.2 = (f32[1024,768]{1,0:T(8,128)S(1)}, bf16[1024,768]{1,0:T(8,128)(2,1)S(1)}, bf16[1,768,6144]{2,1,0:T(8,128)(2,1)}, f32[4,1,768]{2,1,0:T(1,128)S(1)}, f32[4,8,768]{2,1,0:T(8,128)S(1)}) custom-call(s32[1]{0:T(128)} %bitcast.87.place, bf16[1024,768]{1,0:T(8,128)(2,1)S(1)} %copy-done.42, bf16[1024,768]{1,0:T(8,128)(2,1)S(1)} %get-tuple-element.108.second, ...), custom_call_target="tpu_custom_call" | custom-call | flops 19327352832 | bytes 50000000 | tf_op jit(solution)/shard_map/ff_backward/pallas_call | solution.py:700
  363.7 2.3 copy-done.5
  370.3 4.5 gates_backward.2
  376.3 12.0 %kernel_backward.2 = f32[1024,768]{1,0:T(8,128)S(1)} custom-call(s32[52]{0:T(128)S(1)} %concatenate.58.table, bf16[2176,768]{1,0:T(8,128)(2,1)S(1)} %copy-done.12, bf16[1024,768]{1,0:T(8,128)(2,1)S(1)} %get-tuple-element.115.grads, bf16[256,256]{1,0:T(8,128)(2,1)S(1)} %copy-done.45, bf16[256,128]{1,0:T(8,128)(2,1)S(1)} %copy-done.48, ...), custom_call_target="tpu_custom_call" | custom-call | flops 20000000000 | bytes 20000000 | tf_op jit(solution)/shard_map/kernel_backward/pallas_call | solution.py:700
  388.4 4.5 multiply_reduce_fusion.5
  401.1 4.2 fusion.4
  405.4 12.7 %collective-permute-done.14 = bf16[1024,768]{1,0:T(8,128)(2,1)S(1)} collective-permute-done((bf16[1024,768]{1,0:T(8,128)(2,1)S(1)}, bf16[1024,768]{1,0:T(8,128)(2,1)S(1)}, u32[]{:S(2)}, u32[]{:S(2)}) %collective-permute-start.14) | collective-permute-done | bytes 1572896 | tf_op jit(solution)/shard_map/ppermute | solution.py:1078
  418.5 17.4 %signal_backward.2 = (bf16[1024,768]{1,0:T(8,128)(2,1)S(1)}, bf16[1024,768]{1,0:T(8,128)(2,1)S(1)}) custom-call(s32[52]{0:T(128)S(1)} %concatenate.58.table, bf16[2176,768]{1,0:T(8,128)(2,1)S(1)} %pad_maximum_fusion.4.grads, f32[8,256,768]{2,1,0:T(8,128)S(1)} %bitcast.374, bf16[1024,768]{1,0:T(8,128)(2,1)S(1)} %copy-done.58, ...), custom_call_target="tpu_custom_call" | custom-call | flops 20000000000 | bytes 20000000 | tf_op jit(solution)/shard_map/signal_backward/pallas_call | solution.py:700
  437.3 4.9 collective-permute-done.15.halo
  442.3 36.9 %in_backward.2 = (f32[1024,768]{1,0:T(8,128)}, bf16[1024,768]{1,0:T(8,128)(2,1)}, f32[2,1,1152]{2,1,0:T(1,128)S(1)}, f32[2,3,1152]{2,1,0:T(4,128)S(1)}, f32[2,8,...) custom-call(s32[1]{0:T(128)} %bitcast.87.place, bf16[1024,768]{1,0:T(8,128)(2,1)S(1)} %get-tuple-element.114.first_grad, ...), custom_call_target="tpu_custom_call" | custom-call | flops 8455716864 | bytes 40000000 | tf_op jit(solution)/shard_map/in_backward/pallas_call | solution.py:700
  482.6 38.5 %ff_backward.3 = (f32[1024,768]{1,0:T(8,128)S(1)}, bf16[1024,768]{1,0:T(8,128)(2,1)S(1)}, bf16[1,768,9216]{2,1,0:T(8,128)(2,1)}, f32[4,1,768]{2,1,0:T(1,128)S(1)}, f32[4,8,768]{2,1,0:T(8,128)S(1)}) custom-call(s32[1]{0:T(128)} %bitcast.87.place, f32[1024,768]{1,0:T(8,128)S(1)} %copy-done.53, ...), custom_call_target="tpu_custom_call", output_to_operand_aliasing={{2}: (8, {})} | custom-call | flops 19327352832 | bytes 50000000 | tf_op jit(solution)/shard_map/ff_backward/pallas_call | solution.py:700
  525.4 2.3 copy-done.2
  530.6 5.1 gates_backward.3
  537.1 13.5 %kernel_backward.3 = f32[1024,768]{1,0:T(8,128)S(1)} custom-call(s32[52]{0:T(128)S(1)} %concatenate.58.table, bf16[2176,768]{1,0:T(8,128)(2,1)S(1)} %copy-done.10, bf16[1024,768]{1,0:T(8,128)(2,1)} %get-tuple-element.133.grads, bf16[256,256]{1,0:T(8,128)(2,1)S(1)} %copy-done.46, bf16[256,128]{1,0:T(8,128)(2,1)S(1)} %copy-done.49, bf16[128,256]{1,0:T(8,128)(2,1)S(1)} %copy-done.47), custom_call_target="tpu_custom_call" | custom-call | flops 20000000000 | bytes 20000000 | tf_op jit(solution)/shard_map/kernel_backward/pallas_call | solution.py:700
  550.7 4.5 multiply_reduce_fusion.2
  565.0 6.3 collective-permute-start.17
  571.4 5.3 fusion.8
  576.6 3.3 collective-permute-done.17
  582.9 2.8 copy-done.7
  585.8 15.8 %signal_backward.3 = (bf16[1024,768]{1,0:T(8,128)(2,1)S(1)}, bf16[1024,768]{1,0:T(8,128)(2,1)S(1)}) custom-call(s32[52]{0:T(128)S(1)} %concatenate.58.table, bf16[2176,768]{1,0:T(8,128)(2,1)S(1)} %pad_maximum_fusion.3.grads, f32[8,256,768]{2,1,0:T(8,128)S(1)} %copy-done.7, bf16[1024,768]{1,0:T(8,128)(2,1)S(1)} %copy-done.67, ...), custom_call_target="tpu_custom_call" | custom-call | flops 20000000000 | bytes 20000000 | tf_op jit(solution)/shard_map/signal_backward/pallas_call | solution.py:700
  602.9 4.9 collective-permute-done.18.halo
  608.0 35.9 %in_backward.3 = (f32[1024,768]{1,0:T(8,128)}, bf16[1024,768]{1,0:T(8,128)(2,1)}, f32[2,1,1152]{2,1,0:T(1,128)S(1)}, f32[2,3,1152]{2,1,0:T(4,128)S(1)}, f32[2,8,...) custom-call(s32[1]{0:T(128)} %bitcast.87.place, bf16[1024,768]{1,0:T(8,128)(2,1)S(1)} %copy-done.41, ...), custom_call_target="tpu_custom_call" | custom-call | flops 8455716864 | bytes 40000000 | tf_op jit(solution)/shard_map/in_backward/pallas_call | solution.py:700
  646.0 2.8 collective-permute-done.19
  648.8 3.0 add_convert_fusion
  654.7 6.3 collective-permute-start.30
  661.8 2.9 collective-permute-start.22
  664.7 4.7 collective-permute-done.30
  669.4 6.9 collective-permute-done.29
  676.7 8.0 %collective-permute-start.31 = (bf16[208,768]{1,0:T(8,128)(2,1)S(1)}, bf16[208,768]{1,0:T(8,128)(2,1)S(1)}, u32[]{:S(2)}, u32[]{:S(2)}) collective-permute-start(bf16[208,768]{1,0:T(8,128)(2,1)S(1)} %fusion.32), channel_id=1, source_target_pairs={{0,8},{1,9},{4,12},{5,13},{8,0},{9,1},{12,4},{13,5},{16,24},{17,25... | collective-permute-start | bytes 958472 | tf_op jit(solution)/shard_map/ppermute | solution.py:976
  686.1 6.0 collective-permute-done.31
  692.3 2.9 collective-permute-start.32
  695.2 6.0 collective-permute-done.21
  701.5 7.3 collective-permute-done.32
  719.3 9.7 %collective-permute-done.23 = bf16[48,4608]{1,0:T(8,128)(2,1)S(1)} collective-permute-done((bf16[48,4608]{1,0:T(8,128)(2,1)S(1)}, bf16[48,4608]{1,0:T(8,128)(2,1)S(1)}, u32[]{:S(2)}, u32[]{:S(2)}) %collective-permute-start.23) | collective-permute-done | bytes 442400 | tf_op jit(solution)/shard_map/ppermute | solution.py:976
  735.6 2.3 collective-permute-done.26
  737.9 6.6 collective-permute-done.25
  (575 shorter events, 132.2 us)
Async XLA Ops:
  7.2 152.3 %all-gather.3.cloned.1.call-start = ((), (), s32[]{:S(2)}) async-start(), calls=%async_computation.2 | async-start | bytes 15040512 | tf_op jit(solution)/shard_map/all_gather | solution.py:1016
  9.5 7.3 collective-permute-start.10
  13.7 9.0 %collective-permute-start.9 = (bf16[48,3072]{1,0:T(8,128)(2,1)S(1)}, bf16[48,3072]{1,0:T(8,128)(2,1)S(1)}, u32[]{:S(2)}, u32[]{:S(2)}) collective-permute-start(bf16[48,3072]{1,0:T(8,128)(2,1)S(1)} %reshape.393), channel_id=1, source_target_pairs={{0,1},{1,0},{4,5},{5,4},{8,9},{9,8},{12,13},{13,12},{16,17},{17,16... | collective-permute-start | bytes 884744 | tf_op jit(solution)/shard_map/ppermute | solution.py:976
  23.7 261.2 %all-gather.5.cloned.1.call-start = ((), (), s32[]{:S(2)}) async-start(), calls=%async_computation.3 | async-start | bytes 10027008 | tf_op jit(solution)/shard_map/all_gather | solution.py:1016
  23.9 20.4 %collective-permute-start.3 = (bf16[48,1536]{1,0:T(8,128)(2,1)S(1)}, bf16[48,1536]{1,0:T(8,128)(2,1)S(1)}, u32[]{:S(2)}, u32[]{:S(2)}) collective-permute-start(bf16[48,1536]{1,0:T(8,128)(2,1)S(1)} %bitcast.402), channel_id=1, source_target_pairs={{0,24},{1,25},{4,28},{5,29},{8,16},{9,17},{12,20},{13,21},{16,8},{... | collective-permute-start | bytes 442376 | tf_op jit(solution)/shard_map/ppermute | solution.py:976
  27.8 19.4 %collective-permute-start.2 = (bf16[48,1536]{1,0:T(8,128)(2,1)S(1)}, bf16[48,1536]{1,0:T(8,128)(2,1)S(1)}, u32[]{:S(2)}, u32[]{:S(2)}) collective-permute-start(bf16[48,1536]{1,0:T(8,128)(2,1)S(1)} %bitcast.403), channel_id=1, source_target_pairs={{0,16},{1,17},{4,20},{5,21},{8,24},{9,25},{12,28},{13,29},{16,0},{... | collective-permute-start | bytes 442376 | tf_op jit(solution)/shard_map/ppermute | solution.py:976
  27.8 19.4 %collective-permute-start.1 = (bf16[48,1536]{1,0:T(8,128)(2,1)S(1)}, bf16[48,1536]{1,0:T(8,128)(2,1)S(1)}, u32[]{:S(2)}, u32[]{:S(2)}) collective-permute-start(bf16[48,1536]{1,0:T(8,128)(2,1)S(1)} %bitcast.404), channel_id=1, source_target_pairs={{0,8},{1,9},{4,12},{5,13},{8,0},{9,1},{12,4},{13,5},{16,24},{17,25... | collective-permute-start | bytes 442376 | tf_op jit(solution)/shard_map/ppermute | solution.py:976
  29.5 7.7 %collective-permute-start.13 = (bf16[48,3072]{1,0:T(8,128)(2,1)S(1)}, bf16[48,3072]{1,0:T(8,128)(2,1)S(1)}, u32[]{:S(2)}, u32[]{:S(2)}) collective-permute-start(bf16[48,3072]{1,0:T(8,128)(2,1)S(1)} %reshape.397), channel_id=1, source_target_pairs={{0,1},{1,0},{4,5},{5,4},{8,9},{9,8},{12,13},{13,12},{16,17},{17,16... | collective-permute-start | bytes 884744 | tf_op jit(solution)/shard_map/ppermute | solution.py:976
  38.2 525.8 %reduce-scatter.3.cloned.1.call-start = ((), (), s32[]{:S(2)}) async-start(), calls=%async_computation.4 | async-start | bytes 10027008 | tf_op jit(solution)/shard_map/reduce_scatter | solution.py:1019
  44.3 356.8 %copy-start.119 = (f32[768]{0:T(1024)}, f32[768]{0:T(1024)S(1)}, u32[]{:S(2)}) copy-start(f32[768]{0:T(1024)S(1)} %add_abs_fusion) | copy-start | bytes 9220
  47.5 17.2 %collective-permute-start.6 = (bf16[4,48,1536]{2,1,0:T(8,128)(2,1)S(1)}, bf16[4,48,1536]{2,1,0:T(8,128)(2,1)S(1)}, u32[]{:S(2)}, u32[]{:S(2)}) collective-permute-start(bf16[4,48,1536]{2,1,0:T(8,128)(2,1)S(1)} %get-tuple-element.312), channel_id=1, source_target_pairs={{0,5},{1,4},{4,1},{5,0},{8,13},{9,12},{12,9},{13,8},{16,21},{17,20... | collective-permute-start | bytes 1769480 | tf_op jit(solution)/shard_map/ppermute | solution.py:976
  48.2 23.0 %collective-permute-start.5 = (bf16[4,48,1536]{2,1,0:T(8,128)(2,1)S(1)}, bf16[4,48,1536]{2,1,0:T(8,128)(2,1)S(1)}, u32[]{:S(2)}, u32[]{:S(2)}) collective-permute-start(bf16[4,48,1536]{2,1,0:T(8,128)(2,1)S(1)} %get-tuple-element.312), channel_id=1, source_target_pairs={{0,4},{1,5},{4,0},{5,1},{8,12},{9,13},{12,8},{13,9},{16,20},{17,21... | collective-permute-start | bytes 1769480 | tf_op jit(solution)/shard_map/ppermute | solution.py:976
  49.3 22.0 %collective-permute-start.4 = (bf16[4,48,1536]{2,1,0:T(8,128)(2,1)S(1)}, bf16[4,48,1536]{2,1,0:T(8,128)(2,1)S(1)}, u32[]{:S(2)}, u32[]{:S(2)}) collective-permute-start(bf16[4,48,1536]{2,1,0:T(8,128)(2,1)S(1)} %get-tuple-element.312), channel_id=1, source_target_pairs={{0,1},{1,0},{4,5},{5,4},{8,9},{9,8},{12,13},{13,12},{16,17},{17,16... | collective-permute-start | bytes 1769480 | tf_op jit(solution)/shard_map/ppermute | solution.py:976
  72.3 6.5 collective-permute-start.7
  73.1 8.2 %collective-permute-start = (bf16[16,768]{1,0:T(8,128)(2,1)S(1)}, bf16[16,768]{1,0:T(8,128)(2,1)S(1)}, u32[]{:S(2)}, u32[]{:S(2)}) collective-permute-start(bf16[16,768]{1,0:T(8,128)(2,1)S(1)} %slice.413), channel_id=1, source_target_pairs={{0,1},{1,2},{2,3},{3,4},{4,5},{5,6},{6,7},{7,8},{8,9},{9,10},{10,1... | collective-permute-start | bytes 73736 | tf_op jit(solution)/shard_map/ppermute | solution.py:1075
  82.3 27.2 %copy-start.145 = (f32[2,768]{1,0:T(2,128)S(1)}, f32[2,768]{1,0:T(2,128)}, u32[]{:S(2)}) copy-start(f32[2,768]{1,0:T(2,128)} %param.41) | copy-start | bytes 18436
  82.3 27.2 %copy-start.140 = (f32[2,2,768]{2,1,0:T(2,128)S(1)}, f32[2,2,768]{2,1,0:T(2,128)}, u32[]{:S(2)}) copy-start(f32[2,2,768]{2,1,0:T(2,128)} %param.44) | copy-start | bytes 36868
  82.3 27.2 %copy-start.126 = (f32[2,3072]{1,0:T(2,128)S(1)}, f32[2,3072]{1,0:T(2,128)}, u32[]{:S(2)}) copy-start(f32[2,3072]{1,0:T(2,128)} %param.45) | copy-start | bytes 73732
  102.8 38.6 %copy-start.13 = (bf16[1024,768]{1,0:T(8,128)(2,1)}, bf16[1024,768]{1,0:T(8,128)(2,1)S(1)}, u32[]{:S(2)}) copy-start(bf16[1024,768]{1,0:T(8,128)(2,1)S(1)} %get-tuple-element.100.gate_out) | copy-start | bytes 4718596
  102.8 36.9 %collective-permute-start.8 = (bf16[1024,768]{1,0:T(8,128)(2,1)S(1)}, bf16[1024,768]{1,0:T(8,128)(2,1)}, u32[]{:S(2)}, u32[]{:S(2)}) collective-permute-start(bf16[1024,768]{1,0:T(8,128)(2,1)S(1)} %get-tuple-element.98.signal), channel_id=1, source_target_pairs={{0,1},{1,2},{2,3},{3,4},{4,5},{5,6},{6,7},{7,8},{8,9},{9,10},{10,1... | collective-permute-start | bytes 4718600 | tf_op jit(solution)/shard_map/ppermute | solution.py:1075
  109.5 32.0 %copy-start.33 = (f32[1,1,768]{2,1,0:T(1,128)}, f32[1,1,768]{2,1,0:T(1,128)S(1)}, u32[]{:S(2)}) copy-start(f32[1,1,768]{2,1,0:T(1,128)S(1)} %get-tuple-element.362.bias) | copy-start | bytes 9220
  202.2 11.2 %collective-permute-start.11 = (f32[16,768]{1,0:T(8,128)S(1)}, f32[16,768]{1,0:T(8,128)S(1)}, u32[]{:S(2)}, u32[]{:S(2)}) collective-permute-start(f32[16,768]{1,0:T(8,128)S(1)} %slice.443), channel_id=1, source_target_pairs={{0,1},{1,2},{2,3},{3,4},{4,5},{5,6},{6,7},{7,8},{8,9},{9,10},{10,1... | collective-permute-start | bytes 147464 | tf_op jit(solution)/shard_map/ppermute | solution.py:1075
  213.4 23.8 %copy-start.130 = (f32[64]{0:T(128)S(1)}, f32[64]{0:T(128)}, u32[]{:S(2)}) copy-start(f32[64]{0:T(128)} %get-tuple-element.395) | copy-start | bytes 772
  213.4 23.8 %copy-start.153 = (f32[64]{0:T(128)S(1)}, f32[64]{0:T(128)}, u32[]{:S(2)}) copy-start(f32[64]{0:T(128)} %get-tuple-element.377) | copy-start | bytes 772
  213.4 25.1 %copy-start.110 = (f32[2,64,768]{2,1,0:T(8,128)S(1)}, f32[2,64,768]{2,1,0:T(8,128)}, u32[]{:S(2)}) copy-start(f32[2,64,768]{2,1,0:T(8,128)} %param.40) | copy-start | bytes 1179652
  213.4 25.1 %copy-start.134 = (f32[64]{0:T(128)S(1)}, f32[64]{0:T(128)}, u32[]{:S(2)}) copy-start(f32[64]{0:T(128)} %get-tuple-element.400) | copy-start | bytes 772
  232.2 37.2 %copy-start.21 = (bf16[1024,768]{1,0:T(8,128)(2,1)}, bf16[1024,768]{1,0:T(8,128)(2,1)S(1)}, u32[]{:S(2)}) copy-start(bf16[1024,768]{1,0:T(8,128)(2,1)S(1)} %get-tuple-element.105.gate_out) | copy-start | bytes 4718596
  232.2 36.8 %collective-permute-start.12 = (bf16[1024,768]{1,0:T(8,128)(2,1)S(1)}, bf16[1024,768]{1,0:T(8,128)(2,1)S(1)}, u32[]{:S(2)}, u32[]{:S(2)}) collective-permute-start(bf16[1024,768]{1,0:T(8,128)(2,1)S(1)} %get-tuple-element.104.signal), channel_id=1, source_target_pairs={{0,1},{1,2},{2,3},{3,4},{4,5},{5,6},{6,7},{7,8},{8,9},{9,10},{10,1... | collective-permute-start | bytes 4718600 | tf_op jit(solution)/shard_map/ppermute | solution.py:1075
  242.4 26.6 %copy-start.76 = (bf16[128,768]{1,0:T(8,128)(2,1)S(1)}, bf16[128,768]{1,0:T(8,128)(2,1)}, u32[]{:S(2)}) copy-start(bf16[128,768]{1,0:T(8,128)(2,1)} %copy-done.75) | copy-start | bytes 589828
  243.5 26.0 %copy-start.8 = (f32[8,256,768]{2,1,0:T(8,128)}, f32[8,256,768]{2,1,0:T(8,128)S(1)}, u32[]{:S(2)}) copy-start(f32[8,256,768]{2,1,0:T(8,128)S(1)} %convolution_bitcast_fusion.kernel) | copy-start | bytes 18874372
  290.6 31.6 %copy-start.42 = (bf16[1024,768]{1,0:T(8,128)(2,1)S(1)}, bf16[1024,768]{1,0:T(8,128)(2,1)}, u32[]{:S(2)}) copy-start(bf16[1024,768]{1,0:T(8,128)(2,1)} %grad.1) | copy-start | bytes 4718596
  363.7 352.0 %reduce-scatter.5.cloned.1.call-start = ((), (), s32[]{:S(2)}) async-start(), calls=%async_computation.5 | async-start | bytes 15040512 | tf_op jit(solution)/shard_map/reduce_scatter | solution.py:1019
  374.8 43.3 %collective-permute-start.14 = (bf16[1024,768]{1,0:T(8,128)(2,1)S(1)}, bf16[1024,768]{1,0:T(8,128)(2,1)S(1)}, u32[]{:S(2)}, u32[]{:S(2)}) collective-permute-start(bf16[1024,768]{1,0:T(8,128)(2,1)S(1)} %get-tuple-element.115.grads), channel_id=1, source_target_pairs={{1,0},{2,1},{3,2},{4,3},{5,4},{6,5},{7,6},{8,7},{9,8},{10,9},{11,1... | collective-permute-start | bytes 4718600 | tf_op jit(solution)/shard_map/ppermute | solution.py:1078
  388.4 30.1 %slice-start = ((s8[6291456]{0:T(1024)(128)(4,1)}), s8[4194304]{0:T(1024)(128)(4,1)S(1)}, s32[]{:S(2)}) async-start(s8[6291456]{0:T(1024)(128)(4,1)} %bitcast.373), calls=%async_computation.6 | async-start | bytes 8388608
  436.0 6.2 collective-permute-start.15
  442.3 36.9 %copy-start.72 = (f32[1024,768]{1,0:T(8,128)S(1)}, f32[1024,768]{1,0:T(8,128)}, u32[]{:S(2)}) copy-start(f32[1024,768]{1,0:T(8,128)} %copy-done.71) | copy-start | bytes 9437188
  535.6 27.7 %copy-start.40 = (bf16[1024,768]{1,0:T(8,128)(2,1)}, bf16[1024,768]{1,0:T(8,128)(2,1)S(1)}, u32[]{:S(2)}) copy-start(bf16[1024,768]{1,0:T(8,128)(2,1)S(1)} %get-tuple-element.132.first_grad) | copy-start | bytes 4718596
  535.6 44.4 %collective-permute-start.16 = (bf16[1024,768]{1,0:T(8,128)(2,1)}, bf16[1024,768]{1,0:T(8,128)(2,1)}, u32[]{:S(2)}, u32[]{:S(2)}) collective-permute-start(bf16[1024,768]{1,0:T(8,128)(2,1)} %get-tuple-element.133.grads), channel_id=1, source_target_pairs={{1,0},{2,1},{3,2},{4,3},{5,4},{6,5},{7,6},{8,7},{9,8},{10,9},{11,1... | collective-permute-start | bytes 4718600 | tf_op jit(solution)/shard_map/ppermute | solution.py:1078
  565.0 14.9 %collective-permute-start.17 = (bf16[48,3072]{1,0:T(8,128)(2,1)S(1)}, bf16[48,3072]{1,0:T(8,128)(2,1)S(1)}, u32[]{:S(2)}, u32[]{:S(2)}) collective-permute-start(bf16[48,3072]{1,0:T(8,128)(2,1)S(1)} %constant_dynamic-slice_fusion.2), channel_id=1, source_target_pairs={{0,1},{1,0},{4,5},{5,4},{8,9},{9,8},{12,13},{13,12},{16,17},{17,16... | collective-permute-start | bytes 884744 | tf_op jit(solution)/shard_map/ppermute | solution.py:976
  601.6 6.2 collective-permute-start.18
  607.9 36.1 %copy-start.117 = (bf16[2,64,64]{2,1,0:T(8,128)(2,1)S(1)}, bf16[2,64,64]{2,1,0:T(8,128)(2,1)}, u32[]{:S(2)}) copy-start(bf16[2,64,64]{2,1,0:T(8,128)(2,1)} %pad_add_fusion.1) | copy-start | bytes 49156
  607.9 36.1 %copy-start.123 = (bf16[33,64]{1,0:T(8,128)(2,1)S(1)}, bf16[33,64]{1,0:T(8,128)(2,1)}, u32[]{:S(2)}) copy-start(bf16[33,64]{1,0:T(8,128)(2,1)} %fusion.37) | copy-start | bytes 12676
  607.9 36.1 %copy-start.146 = (bf16[3,64]{1,0:T(4,128)(2,1)S(1)}, bf16[3,64]{1,0:T(4,128)(2,1)}, u32[]{:S(2)}) copy-start(bf16[3,64]{1,0:T(4,128)(2,1)} %pad_add_fusion.5) | copy-start | bytes 1156
  608.0 36.1 %copy-start.147 = (bf16[3,64]{1,0:T(4,128)(2,1)S(1)}, bf16[3,64]{1,0:T(4,128)(2,1)}, u32[]{:S(2)}) copy-start(bf16[3,64]{1,0:T(4,128)(2,1)} %pad_add_fusion.4) | copy-start | bytes 1156
  608.0 36.6 %copy-start.118 = (bf16[2,64,64]{2,1,0:T(8,128)(2,1)S(1)}, bf16[2,64,64]{2,1,0:T(8,128)(2,1)}, u32[]{:S(2)}) copy-start(bf16[2,64,64]{2,1,0:T(8,128)(2,1)} %pad_add_fusion) | copy-start | bytes 49156
  608.0 36.6 %copy-start.124 = (bf16[33,64]{1,0:T(8,128)(2,1)S(1)}, bf16[33,64]{1,0:T(8,128)(2,1)}, u32[]{:S(2)}) copy-start(bf16[33,64]{1,0:T(8,128)(2,1)} %fusion.35) | copy-start | bytes 12676
  608.0 36.6 %copy-start.148 = (bf16[3,64]{1,0:T(4,128)(2,1)S(1)}, bf16[3,64]{1,0:T(4,128)(2,1)}, u32[]{:S(2)}) copy-start(bf16[3,64]{1,0:T(4,128)(2,1)} %pad_add_fusion.3) | copy-start | bytes 1156
  608.0 36.6 %copy-start.149 = (bf16[3,64]{1,0:T(4,128)(2,1)S(1)}, bf16[3,64]{1,0:T(4,128)(2,1)}, u32[]{:S(2)}) copy-start(bf16[3,64]{1,0:T(4,128)(2,1)} %pad_add_fusion.2) | copy-start | bytes 1156
  608.0 37.0 %copy-start.113 = (bf16[64,768]{1,0:T(8,128)(2,1)S(1)}, bf16[64,768]{1,0:T(8,128)(2,1)}, u32[]{:S(2)}) copy-start(bf16[64,768]{1,0:T(8,128)(2,1)} %fusion.4) | copy-start | bytes 294916
  608.0 37.0 %copy-start.114 = (bf16[64,768]{1,0:T(8,128)(2,1)S(1)}, bf16[64,768]{1,0:T(8,128)(2,1)}, u32[]{:S(2)}) copy-start(bf16[64,768]{1,0:T(8,128)(2,1)} %fusion.8) | copy-start | bytes 294916
  643.9 4.9 collective-permute-start.19
  651.8 1.8 collective-permute-start.27
  654.7 14.8 %collective-permute-start.30 = (bf16[208,768]{1,0:T(8,128)(2,1)S(1)}, bf16[208,768]{1,0:T(8,128)(2,1)S(1)}, u32[]{:S(2)}, u32[]{:S(2)}) collective-permute-start(bf16[208,768]{1,0:T(8,128)(2,1)S(1)} %add_convert_fusion.3), channel_id=1, source_target_pairs={{0,5},{1,4},{4,1},{5,0},{8,13},{9,12},{12,9},{13,8},{16,21},{17,20... | collective-permute-start | bytes 958472 | tf_op jit(solution)/shard_map/ppermute | solution.py:976
  661.0 15.3 %collective-permute-start.29 = (bf16[208,768]{1,0:T(8,128)(2,1)S(1)}, bf16[208,768]{1,0:T(8,128)(2,1)S(1)}, u32[]{:S(2)}, u32[]{:S(2)}) collective-permute-start(bf16[208,768]{1,0:T(8,128)(2,1)S(1)} %add_convert_fusion.3), channel_id=1, source_target_pairs={{0,4},{1,5},{4,0},{5,1},{8,12},{9,13},{12,8},{13,9},{16,20},{17,21... | collective-permute-start | bytes 958472 | tf_op jit(solution)/shard_map/ppermute | solution.py:976
  661.0 15.3 %collective-permute-start.28 = (bf16[208,768]{1,0:T(8,128)(2,1)S(1)}, bf16[208,768]{1,0:T(8,128)(2,1)S(1)}, u32[]{:S(2)}, u32[]{:S(2)}) collective-permute-start(bf16[208,768]{1,0:T(8,128)(2,1)S(1)} %add_convert_fusion.3), channel_id=1, source_target_pairs={{0,1},{1,0},{4,5},{5,4},{8,9},{9,8},{12,13},{13,12},{16,17},{17,16... | collective-permute-start | bytes 958472 | tf_op jit(solution)/shard_map/ppermute | solution.py:976
  661.8 33.4 %collective-permute-start.22 = (bf16[4,48,1536]{2,1,0:T(8,128)(2,1)S(1)}, bf16[4,48,1536]{2,1,0:T(8,128)(2,1)S(1)}, u32[]{:S(2)}, u32[]{:S(2)}) collective-permute-start(bf16[4,48,1536]{2,1,0:T(8,128)(2,1)S(1)} %get-tuple-element.272), channel_id=1, source_target_pairs={{0,5},{1,4},{4,1},{5,0},{8,13},{9,12},{12,9},{13,8},{16,21},{17,20... | collective-permute-start | bytes 1769480 | tf_op jit(solution)/shard_map/ppermute | solution.py:976
  664.7 36.4 %collective-permute-start.21 = (bf16[4,48,1536]{2,1,0:T(8,128)(2,1)S(1)}, bf16[4,48,1536]{2,1,0:T(8,128)(2,1)S(1)}, u32[]{:S(2)}, u32[]{:S(2)}) collective-permute-start(bf16[4,48,1536]{2,1,0:T(8,128)(2,1)S(1)} %get-tuple-element.273), channel_id=1, source_target_pairs={{0,4},{1,5},{4,0},{5,1},{8,12},{9,13},{12,8},{13,9},{16,20},{17,21... | collective-permute-start | bytes 1769480 | tf_op jit(solution)/shard_map/ppermute | solution.py:976
  669.4 31.8 %collective-permute-start.20 = (bf16[4,48,1536]{2,1,0:T(8,128)(2,1)S(1)}, bf16[4,48,1536]{2,1,0:T(8,128)(2,1)S(1)}, u32[]{:S(2)}, u32[]{:S(2)}) collective-permute-start(bf16[4,48,1536]{2,1,0:T(8,128)(2,1)S(1)} %get-tuple-element.271), channel_id=1, source_target_pairs={{0,1},{1,0},{4,5},{5,4},{8,9},{9,8},{12,13},{13,12},{16,17},{17,16... | collective-permute-start | bytes 1769480 | tf_op jit(solution)/shard_map/ppermute | solution.py:976
  676.7 15.5 %collective-permute-start.31 = (bf16[208,768]{1,0:T(8,128)(2,1)S(1)}, bf16[208,768]{1,0:T(8,128)(2,1)S(1)}, u32[]{:S(2)}, u32[]{:S(2)}) collective-permute-start(bf16[208,768]{1,0:T(8,128)(2,1)S(1)} %fusion.32), channel_id=1, source_target_pairs={{0,8},{1,9},{4,12},{5,13},{8,0},{9,1},{12,4},{13,5},{16,24},{17,25... | collective-permute-start | bytes 958472 | tf_op jit(solution)/shard_map/ppermute | solution.py:976
  692.3 16.5 %collective-permute-start.32 = (bf16[208,768]{1,0:T(8,128)(2,1)S(1)}, bf16[208,768]{1,0:T(8,128)(2,1)S(1)}, u32[]{:S(2)}, u32[]{:S(2)}) collective-permute-start(bf16[208,768]{1,0:T(8,128)(2,1)S(1)} %add_convert_fusion.1), channel_id=1, source_target_pairs={{0,16},{1,17},{4,20},{5,21},{8,24},{9,25},{12,28},{13,29},{16,0},{... | collective-permute-start | bytes 958472 | tf_op jit(solution)/shard_map/ppermute | solution.py:976
  717.7 11.2 %collective-permute-start.23 = (bf16[48,4608]{1,0:T(8,128)(2,1)S(1)}, bf16[48,4608]{1,0:T(8,128)(2,1)S(1)}, u32[]{:S(2)}, u32[]{:S(2)}) collective-permute-start(bf16[48,4608]{1,0:T(8,128)(2,1)S(1)} %pad_maximum_fusion.14), channel_id=1, source_target_pairs={{0,1},{1,0},{4,5},{5,4},{8,9},{9,8},{12,13},{13,12},{16,17},{17,16... | collective-permute-start | bytes 1327112 | tf_op jit(solution)/shard_map/ppermute | solution.py:976
  729.3 8.6 %collective-permute-start.26 = (bf16[48,1536]{1,0:T(8,128)(2,1)S(1)}, bf16[48,1536]{1,0:T(8,128)(2,1)S(1)}, u32[]{:S(2)}, u32[]{:S(2)}) collective-permute-start(bf16[48,1536]{1,0:T(8,128)(2,1)S(1)} %get-tuple-element.305), channel_id=1, source_target_pairs={{0,24},{1,25},{4,28},{5,29},{8,16},{9,17},{12,20},{13,21},{16,8},{... | collective-permute-start | bytes 442376 | tf_op jit(solution)/shard_map/ppermute | solution.py:976
  730.7 13.9 %collective-permute-start.25 = (bf16[48,1536]{1,0:T(8,128)(2,1)S(1)}, bf16[48,1536]{1,0:T(8,128)(2,1)S(1)}, u32[]{:S(2)}, u32[]{:S(2)}) collective-permute-start(bf16[48,1536]{1,0:T(8,128)(2,1)S(1)} %get-tuple-element.306), channel_id=1, source_target_pairs={{0,16},{1,17},{4,20},{5,21},{8,24},{9,25},{12,28},{13,29},{16,0},{... | collective-permute-start | bytes 442376 | tf_op jit(solution)/shard_map/ppermute | solution.py:976
  732.4 12.1 %collective-permute-start.24 = (bf16[48,1536]{1,0:T(8,128)(2,1)S(1)}, bf16[48,1536]{1,0:T(8,128)(2,1)S(1)}, u32[]{:S(2)}, u32[]{:S(2)}) collective-permute-start(bf16[48,1536]{1,0:T(8,128)(2,1)S(1)} %get-tuple-element.304), channel_id=1, source_target_pairs={{0,8},{1,9},{4,12},{5,13},{8,0},{9,1},{12,4},{13,5},{16,24},{17,25... | collective-permute-start | bytes 442376 | tf_op jit(solution)/shard_map/ppermute | solution.py:976
  (132 other events, 1038.8 us)
Sparse Core Ops, SparseCore 0:
  23.8 116.8 all-gather.2
  143.6 87.7 all-gather.4
  363.8 125.2 reduce-scatter.2
  524.1 154.6 reduce-scatter.4
